TPU v7x, 128 devices: a whole 4x4x4 slice. The times are simulated.
128 devices in a mesh: seq: 32 (over x, y, core), head: 4 (over z).
Axes of the slice: x: 4, y: 4, z: 4, core: 2. Of those that a mesh axis runs over, the one named last changes fastest.
Arguments:
- queries: bfloat16 [32768, 7168], P('seq', 'head'), may hold values from -9 to 9
- token_keys: bfloat16 [32768, 7168], P('seq', 'head'), may hold values from -9 to 9
- token_values: bfloat16 [32768, 7168], P('seq', 'head'), may hold values from -6 to 6
- mem_keys: bfloat16 [16384, 7168], P('seq', 'head'), may hold values from -9 to 9
- mem_values: bfloat16 [16384, 7168], P('seq', 'head'), may hold values from -6 to 6
- retrieved: int32 [64, 56, 2], P('seq', 'head'), may hold values from 0 to 127, as said below
- gate_bias: float32 [56], P('head'), may hold values from -2 to 2
Outputs:
- attended: bfloat16 [32768, 7168], P('seq', 'head')
Inputs may be any that keep to these rules, and one draw needn't show every extreme that they name: `retrieved`: block i belongs to shard i // 4. The 2 ids of one list differ. One shard, the same for all devices, is named exactly 7 times among the ids of one device (its query blocks and its heads); every other shard is named at most 3 times there, and some other shard exactly 3 times.
All inputs are finite; a program needn't handle non-finite values.
Results may differ from a plain program's by a relative error of at most 0.011.
Values may be sent and summed in bfloat16 or wider, within the bound.
No kernel may reach another device: no remote copies, remote signals or barrier semaphores. Data moves between devices by JAX's collectives and lax.ppermute only.
A program may use at most 256 MiB of HBM per device.

v0:
```python
import functools

import jax
import jax.numpy as jnp
from jax import lax
from jax.experimental import pallas as pl
from jax.experimental.pallas import tpu as pltpu
from jax.sharding import PartitionSpec as P

QB = 512
MB = 128
TOPK = 2
WIN = 512
DH = 128
PIECE = 8
EDGE = 256
LOG2E = 1.4426950408889634
NEG = -1e30
BF = jnp.bfloat16
F32 = jnp.float32


def pack_kernel(blocks, heads, keys_ref, values_ref, ids_ref, out_ref):
    pieces = MB // PIECE
    for block in range(blocks):
        rows = pl.ds(block * pieces, pieces)
        for head in range(heads):
            cols = pl.ds(head * DH, DH)
            out_ref[0:pieces, block * heads + head] = keys_ref[rows, :, cols]
            out_ref[pieces : 2 * pieces, block * heads + head] = values_ref[rows, :, cols]
    for device in range(2 * pieces):
        out_ref[device, blocks * heads] = ids_ref[...]


def pack(mem_keys, mem_values, ids_tile, blocks, heads):
    rows, width = mem_keys.shape
    shape = (rows // PIECE, PIECE, width)
    return pl.pallas_call(
        functools.partial(pack_kernel, blocks, heads),
        out_shape=jax.ShapeDtypeStruct((2 * MB // PIECE, blocks * heads + 1, PIECE, DH), BF),
        in_specs=[pl.BlockSpec(memory_space=pltpu.VMEM)] * 3,
        out_specs=pl.BlockSpec(memory_space=pltpu.VMEM),
        compiler_params=pltpu.CompilerParams(vmem_limit_bytes=32 << 20),
        name="pack_pieces",
    )(mem_keys.reshape(shape), mem_values.reshape(shape), ids_tile)


def gather_kernel(wanted, group, rows_ref, store_ref, out_ref):
    first = pl.program_id(0) * group

    @pl.loop(0, group)
    def _(device):
        base = (first + device) * wanted
        for request in range(wanted):
            out_ref[device, request] = store_ref[rows_ref[base + request]]


def gather(rows, store, devices, wanted):
    group = 8
    return pl.pallas_call(
        functools.partial(gather_kernel, wanted, group),
        out_shape=jax.ShapeDtypeStruct((devices, wanted, PIECE, DH), BF),
        grid_spec=pltpu.PrefetchScalarGridSpec(
            num_scalar_prefetch=1,
            grid=(devices // group,),
            in_specs=[pl.BlockSpec(store.shape, lambda i, rows: (0, 0, 0))],
            out_specs=pl.BlockSpec((group, wanted, PIECE, DH), lambda i, rows: (i, 0, 0, 0)),
        ),
        compiler_params=pltpu.CompilerParams(vmem_limit_bytes=32 << 20),
        name="gather_pieces",
    )(rows, store)


def dot_t(a, b):
    return lax.dot_general(a, b, (((1,), (1,)), ((), ())), preferred_element_type=F32)


def dot(a, b):
    return jnp.dot(a, b, preferred_element_type=F32)


def triangle():
    row = lax.broadcasted_iota(jnp.int32, (EDGE, EDGE), 0)
    col = lax.broadcasted_iota(jnp.int32, (EDGE, EDGE), 1)
    return col <= row


def spread_lane(stat, lane, store_ref, rows):
    lanes = lax.broadcasted_iota(jnp.int32, (EDGE, DH), 1)
    store_ref[rows, :] = jnp.where(lanes == lane, stat, store_ref[rows, :])


def own_kernel(scale, q_ref, k_ref, v_ref, out_ref, lse_ref):
    head = pl.program_id(0)
    lower = triangle()
    c = scale * LOG2E
    blocks = q_ref.shape[0] // EDGE
    near = WIN // EDGE
    for i in range(blocks):
        rows = pl.ds(i * EDGE, EDGE)
        q = q_ref[rows, :]
        diag = dot_t(q, k_ref[rows, :])
        whole = i >= near
        if whole:
            edge_rows = pl.ds((i - near) * EDGE, EDGE)
            diag = jnp.where(lower, diag, dot_t(q, k_ref[edge_rows, :]))
        else:
            diag = jnp.where(lower, diag, NEG)
        inner = range(max(0, i - near + 1), i)
        parts = [dot_t(q, k_ref[pl.ds(j * EDGE, EDGE), :]) for j in inner]
        top = jnp.max(diag, axis=1, keepdims=True)
        for part in parts:
            top = jnp.maximum(top, jnp.max(part, axis=1, keepdims=True))
        p = jnp.exp2((diag - top) * c)
        total = jnp.sum(p, axis=1, keepdims=True)
        if whole:
            acc = dot(jnp.where(lower, p, 0.0).astype(BF), v_ref[rows, :])
            acc += dot(jnp.where(lower, 0.0, p).astype(BF), v_ref[edge_rows, :])
        else:
            acc = dot(p.astype(BF), v_ref[rows, :])
        for j, part in zip(inner, parts):
            p = jnp.exp2((part - top) * c)
            total += jnp.sum(p, axis=1, keepdims=True)
            acc += dot(p.astype(BF), v_ref[pl.ds(j * EDGE, EDGE), :])
        out_ref[rows, :] = acc / total
        if not whole:
            spread_lane(top * c + jnp.log2(total), head, lse_ref, rows)


def own_attention(queries, keys, values, heads, scale):
    tokens = queries.shape[0]
    column = pl.BlockSpec((tokens, DH), lambda h: (0, h))
    return pl.pallas_call(
        functools.partial(own_kernel, scale),
        out_shape=(
            jax.ShapeDtypeStruct(queries.shape, F32),
            jax.ShapeDtypeStruct((WIN, DH), F32),
        ),
        grid=(heads,),
        in_specs=[column] * 3,
        out_specs=(column, pl.BlockSpec((WIN, DH), lambda h: (0, 0))),
        compiler_params=pltpu.CompilerParams(vmem_limit_bytes=32 << 20),
        name="own_attention",
    )(queries, keys, values)


def next_kernel(scale, heads, q_ref, k_ref, v_ref, out_ref, lse_ref):
    head = pl.program_id(0)
    c = scale * LOG2E

    @pl.when(head < heads)
    def _():
        lower = triangle()
        blocks = q_ref.shape[0] // EDGE
        for i in range(blocks):
            rows = pl.ds(i * EDGE, EDGE)
            q = q_ref[rows, :]
            edge = jnp.where(lower, NEG, dot_t(q, k_ref[rows, :]))
            inner = range(i + 1, blocks)
            parts = [dot_t(q, k_ref[pl.ds(j * EDGE, EDGE), :]) for j in inner]
            top = jnp.max(edge, axis=1, keepdims=True)
            for part in parts:
                top = jnp.maximum(top, jnp.max(part, axis=1, keepdims=True))
            p = jnp.exp2((edge - top) * c)
            total = jnp.sum(p, axis=1, keepdims=True)
            acc = dot(p.astype(BF), v_ref[rows, :])
            for j, part in zip(inner, parts):
                p = jnp.exp2((part - top) * c)
                total += jnp.sum(p, axis=1, keepdims=True)
                acc += dot(p.astype(BF), v_ref[pl.ds(j * EDGE, EDGE), :])
            out_ref[rows, :] = (acc / total).astype(BF)
            spread_lane(top * c + jnp.log2(total), head, lse_ref, rows)

    @pl.when(head == heads)
    def _():
        lanes = lax.broadcasted_iota(jnp.int32, lse_ref.shape, 1)
        stat = jnp.where(lanes < heads, lse_ref[...], 0.0)
        high = stat.astype(BF)
        rest = stat - high.astype(F32)
        mid = rest.astype(BF)
        low = (rest - mid.astype(F32)).astype(BF)
        out_ref[...] = (
            high.astype(F32)
            + pltpu.roll(mid.astype(F32), heads, 1)
            + pltpu.roll(low.astype(F32), 2 * heads, 1)
        ).astype(BF)


def next_attention(queries, keys, values, heads, scale):
    column = pl.BlockSpec((WIN, DH), lambda h: (0, jnp.minimum(h, heads - 1)))
    tail = pl.BlockSpec((WIN, DH), lambda h: (keys.shape[0] // WIN - 1, jnp.minimum(h, heads - 1)))
    return pl.pallas_call(
        functools.partial(next_kernel, scale, heads),
        out_shape=jax.ShapeDtypeStruct((WIN, (heads + 1) * DH), BF),
        grid=(heads + 1,),
        in_specs=[column, tail, tail],
        out_specs=pl.BlockSpec((WIN, DH), lambda h: (0, h)),
        scratch_shapes=[pltpu.VMEM((WIN, DH), F32)],
        compiler_params=pltpu.CompilerParams(vmem_limit_bytes=32 << 20),
        name="next_attention",
    )(queries, keys, values)


def final_kernel(
    scale, heads, first_ref, gate_ref, q_ref, kv_ref, own_ref, lse_ref, back_ref, stat_ref, out_ref
):
    head = pl.program_id(0)
    c = scale * LOG2E
    gate = gate_ref[head]
    pieces = MB // PIECE
    blocks = q_ref.shape[0] // QB
    for b in range(blocks):
        rows = pl.ds(b * QB, QB)
        mine = slice(b * TOPK, (b + 1) * TOPK)
        keys = kv_ref[0:pieces, mine].astype(F32).reshape(TOPK * MB, DH).astype(BF)
        values = kv_ref[pieces : 2 * pieces, mine].astype(F32).reshape(TOPK * MB, DH).astype(BF)
        s = dot_t(q_ref[rows, :], keys)
        top = jnp.max(s, axis=1, keepdims=True)
        p = jnp.exp2((s - top) * c)
        total = jnp.sum(p, axis=1, keepdims=True)
        remote = dot(p.astype(BF), values) / total
        local = own_ref[rows, :]
        if b == 0:
            lanes = lax.broadcasted_iota(jnp.int32, (WIN, DH), 1)
            lse = jnp.sum(jnp.where(lanes == head, lse_ref[...], 0.0), axis=1, keepdims=True)
            hit = (lanes == head) | (lanes == head + heads) | (lanes == head + 2 * heads)
            other = jnp.sum(
                jnp.where(hit, stat_ref[...].astype(F32), 0.0), axis=1, keepdims=True
            )
            other = jnp.where(first_ref[0] == 0, NEG, other)
            share = 1.0 / (1.0 + jnp.exp2(other - lse))
            back = back_ref[...].astype(F32)
            local = local * share + back * (1.0 - share)
        out_ref[rows, :] = (gate * remote + (1.0 - gate) * local).astype(BF)


def final_attention(first, gate, queries, kv, own, lse, back, heads, scale):
    tokens = queries.shape[0]
    blocks = tokens // QB
    column = pl.BlockSpec((tokens, DH), lambda h, *_: (0, h))
    return pl.pallas_call(
        functools.partial(final_kernel, scale, heads),
        out_shape=jax.ShapeDtypeStruct(queries.shape, BF),
        grid_spec=pltpu.PrefetchScalarGridSpec(
            num_scalar_prefetch=2,
            grid=(heads,),
            in_specs=[
                column,
                pl.BlockSpec((kv.shape[0], blocks * TOPK, PIECE, DH), lambda h, *_: (0, h, 0, 0)),
                column,
                pl.BlockSpec((WIN, DH), lambda h, *_: (0, 0)),
                pl.BlockSpec((WIN, DH), lambda h, *_: (0, h)),
                pl.BlockSpec((WIN, DH), lambda h, *_: (0, heads)),
            ],
            out_specs=column,
        ),
        compiler_params=pltpu.CompilerParams(vmem_limit_bytes=32 << 20),
        name="final_attention",
    )(first, gate, queries, kv, own, lse, back, back)


def body(queries, token_keys, token_values, mem_keys, mem_values, retrieved, gate_bias):
    tokens = queries.shape[0]
    heads = gate_bias.shape[0]
    scale = DH ** (-0.5)
    devices = lax.axis_size("seq")
    blocks = mem_keys.shape[0] // MB
    q_blocks = tokens // QB
    wanted = q_blocks * heads * TOPK
    head_q = queries[:WIN]
    ids = retrieved.transpose(1, 0, 2).reshape(-1)
    ids_tile = jnp.zeros((PIECE * DH,), BF).at[:wanted].set(ids.astype(BF)).reshape(PIECE, DH)
    sent = pack(mem_keys, mem_values, ids_tile, blocks, heads)
    store = lax.all_to_all(sent, "seq", split_axis=0, concat_axis=0, tiled=True)
    next_q = lax.ppermute(head_q, "seq", [(i, i - 1) for i in range(1, devices)])
    own, lse = own_attention(queries, token_keys, token_values, heads, scale)
    partial = next_attention(next_q, token_keys, token_values, heads, scale)
    back = lax.ppermute(partial, "seq", [(i, i + 1) for i in range(devices - 1)])
    all_ids = store[:, blocks * heads, 0, :wanted].astype(jnp.int32)
    stride = blocks * heads + 1
    request_head = jnp.arange(wanted, dtype=jnp.int32) // (q_blocks * TOPK)
    rows = (all_ids // blocks) * stride + (all_ids % blocks) * heads + request_head[None, :]
    pieces = gather(
        rows.reshape(-1), store.reshape(devices * stride, PIECE, DH), devices, wanted
    )
    kv = lax.all_to_all(pieces, "seq", split_axis=0, concat_axis=0, tiled=True)
    gate_share = 1.0 / (1.0 + jnp.exp(-gate_bias))
    first = lax.axis_index("seq").reshape(1).astype(jnp.int32)
    return final_attention(first, gate_share, queries, kv, own, lse, back, heads, scale)


def solution(mesh):
    in_specs = (
        P("seq", "head"),
        P("seq", "head"),
        P("seq", "head"),
        P("seq", "head"),
        P("seq", "head"),
        P("seq", "head", None),
        P("head"),
    )
    return jax.shard_map(
        body, mesh=mesh, in_specs=in_specs, out_specs=P("seq", "head"), check_vma=False
    )
```

profile of v0, /device:TPU:2, one launch (start us, length us, event | category | flops | bytes accessed | tf_op | source)
XLA Modules:
  0.0 160.2 jit_solution(10652111751400837054)
XLA Ops:
  0.0 0.7 convert_bitcast_fusion
  0.9 1.5 copy-done.10
  2.4 1.5 copy-done.11
  3.9 0.3 pack_pieces.1
  4.2 1.8 %copy-done.2 = bf16[32,57,8,128]{3,2,1,0:T(8,128)(2,1)} copy-done((bf16[32,57,8,128]{3,2,1,0:T(8,128)(2,1)}, bf16[32,57,8,128]{3,2,1,0:T(8,128)(2,1)S(1)}, u32[]{:S(2)}) %copy-start.2) | copy-done | bytes 3735576
  6.0 7.7 %all-to-all-start = ((bf16[32,57,8,128]{3,2,1,0:T(8,128)(2,1)}), bf16[32,57,8,128]{3,2,1,0:T(8,128)(2,1)}, u32[]{:S(2)}, u32[]{:S(2)}) async-start(bf16[32,57,8,128]{3,2,1,0:T(8,128)(2,1)} %copy-done.2), calls=%async_computation | async-start | bytes 7471104 | tf_op jit(solution)/shard_map/all_to_all | solution.py:274
  13.7 2.9 %slice.18 = bf16[512,1792]{1,0:T(8,128)(2,1)} slice(bf16[1024,1792]{1,0:T(8,128)(2,1)} %q_ref.3), slice={[0:512], [0:1792]} | slice | bytes 3670016 | tf_op jit(solution)/shard_map/slice | solution.py:270
  16.6 4.3 %collective-permute-start = (bf16[512,1792]{1,0:T(8,128)(2,1)}, bf16[512,1792]{1,0:T(8,128)(2,1)S(1)}, u32[]{:S(2)}, u32[]{:S(2)}) collective-permute-start(bf16[512,1792]{1,0:T(8,128)(2,1)} %slice.18), channel_id=1, source_target_pairs={{4,0},{8,4},{12,8},{16,12},{20,16},{24,20},{28,24},{32,28},{36,32}... | collective-permute-start | bytes 5505032 | tf_op jit(solution)/shard_map/ppermute | solution.py:275
  21.1 37.1 %all-to-all-done = bf16[32,57,8,128]{3,2,1,0:T(8,128)(2,1)} async-done(((bf16[32,57,8,128]{3,2,1,0:T(8,128)(2,1)}), bf16[32,57,8,128]{3,2,1,0:T(8,128)(2,1)}, u32[]{:S(2)}, u32[]{:S(2)}) %all-to-all-start) | async-done | bytes 3735584 | tf_op jit(solution)/shard_map/all_to_all | solution.py:274
  58.1 0.9 fusion
  59.1 4.8 %gather_pieces.1 = bf16[32,56,8,128]{3,2,1,0:T(8,128)(2,1)S(1)} custom-call(s32[1792]{0:T(1024)S(1)} %fusion.3.rows_ref, bf16[1824,8,128]{2,1,0:T(8,128)(2,1)} %bitcast.5.store_ref), custom_call_target="tpu_custom_call" | custom-call | tf_op jit(solution)/shard_map/gather_pieces/pallas_call | solution.py:60
  63.9 1.8 %copy-done.3 = bf16[32,56,8,128]{3,2,1,0:T(8,128)(2,1)} copy-done((bf16[32,56,8,128]{3,2,1,0:T(8,128)(2,1)}, bf16[32,56,8,128]{3,2,1,0:T(8,128)(2,1)S(1)}, u32[]{:S(2)}) %copy-start.3) | copy-done | bytes 3670040
  65.8 9.2 %all-to-all-start.1 = ((bf16[32,56,8,128]{3,2,1,0:T(8,128)(2,1)}), bf16[32,56,8,128]{3,2,1,0:T(8,128)(2,1)}, u32[]{:S(2)}, u32[]{:S(2)}) async-start(bf16[32,56,8,128]{3,2,1,0:T(8,128)(2,1)} %copy-done.3), calls=%async_computation.1 | async-start | bytes 7340032 | tf_op jit(solution)/shard_map/all_to_all | solution.py:286
  75.0 4.4 %collective-permute-done.q_ref = bf16[512,1792]{1,0:T(8,128)(2,1)S(1)} collective-permute-done((bf16[512,1792]{1,0:T(8,128)(2,1)}, bf16[512,1792]{1,0:T(8,128)(2,1)S(1)}, u32[]{:S(2)}, u32[]{:S(2)}) %collective-permute-start) | collective-permute-done | bytes 1835040 | tf_op jit(solution)/shard_map/ppermute | solution.py:275
  79.4 2.0 %copy-done.4 = bf16[1024,1792]{1,0:T(8,128)(2,1)S(1)} copy-done((bf16[1024,1792]{1,0:T(8,128)(2,1)S(1)}, bf16[1024,1792]{1,0:T(8,128)(2,1)}, u32[]{:S(2)}) %copy-start.4) | copy-done | bytes 3670040
  81.4 2.0 %copy-done.6 = bf16[1024,1792]{1,0:T(8,128)(2,1)S(1)} copy-done((bf16[1024,1792]{1,0:T(8,128)(2,1)S(1)}, bf16[1024,1792]{1,0:T(8,128)(2,1)}, u32[]{:S(2)}) %copy-start.6) | copy-done | bytes 3670040
  83.5 12.5 %next_attention.1 = bf16[512,1920]{1,0:T(8,128)(2,1)} custom-call(bf16[512,1792]{1,0:T(8,128)(2,1)S(1)} %collective-permute-done.q_ref, bf16[1024,1792]{1,0:T(8,128)(2,1)S(1)} %copy-done.4, bf16[1024,1792]{1,0:T(8,128)(2,1)S(1)} %copy-done.6), custom_call_target="tpu_custom_call" | custom-call | tf_op jit(solution)/shard_map/next_attention/pallas_call | solution.py:192
  96.0 1.9 %collective-permute-start.1 = (bf16[512,1920]{1,0:T(8,128)(2,1)}, bf16[512,1920]{1,0:T(8,128)(2,1)S(1)}, u32[]{:S(2)}, u32[]{:S(2)}) collective-permute-start(bf16[512,1920]{1,0:T(8,128)(2,1)} %next_attention.1), channel_id=1, source_target_pairs={{0,4},{4,8},{8,12},{12,16},{16,20},{20,24},{24,28},{28,32},{32,36}... | collective-permute-start | bytes 5898248 | tf_op jit(solution)/shard_map/ppermute | solution.py:278
  98.0 24.4 %own_attention.1 = (f32[1024,1792]{1,0:T(8,128)S(1)}, f32[512,128]{1,0:T(8,128)S(1)}) custom-call(bf16[1024,1792]{1,0:T(8,128)(2,1)S(1)} %copy-done, bf16[1024,1792]{1,0:T(8,128)(2,1)S(1)} %copy-done.5, bf16[1024,1792]{1,0:T(8,128)(2,1)S(1)} %copy-done.7), custom_call_target="tpu_custom_call" | custom-call | tf_op jit(solution)/shard_map/own_attention/pallas_call | solution.py:133
  122.3 2.9 %copy-done.8 = f32[1024,1792]{1,0:T(8,128)} copy-done((f32[1024,1792]{1,0:T(8,128)}, f32[1024,1792]{1,0:T(8,128)S(1)}, u32[]{:S(2)}) %copy-start.8) | copy-done | bytes 7340056
  125.3 15.5 %collective-permute-done.1.back_ref.stat_ref = bf16[512,1920]{1,0:T(8,128)(2,1)S(1)} collective-permute-done((bf16[512,1920]{1,0:T(8,128)(2,1)}, bf16[512,1920]{1,0:T(8,128)(2,1)S(1)}, u32[]{:S(2)}, u32[]{:S(2)}) %collective-permute-start.1) | collective-permute-done | bytes 1966112 | tf_op jit(solution)/shard_map/ppermute | solution.py:278
  140.8 2.0 %copy-done.1 = bf16[1024,1792]{1,0:T(8,128)(2,1)S(1)} copy-done((bf16[1024,1792]{1,0:T(8,128)(2,1)S(1)}, bf16[1024,1792]{1,0:T(8,128)(2,1)}, u32[]{:S(2)}) %copy-start.1) | copy-done | bytes 3670040
  142.8 3.1 %copy-done.9 = f32[1024,1792]{1,0:T(8,128)S(1)} copy-done((f32[1024,1792]{1,0:T(8,128)S(1)}, f32[1024,1792]{1,0:T(8,128)}, u32[]{:S(2)}) %copy-start.9) | copy-done | bytes 7340056
  145.9 14.3 %final_attention.1 = bf16[1024,1792]{1,0:T(8,128)(2,1)} custom-call(s32[1]{0:T(128)} %bitcast.first_ref, f32[14]{0:T(128)S(1)} %add_divide_fusion.gate_ref, bf16[1024,1792]{1,0:T(8,128)(2,1)S(1)} %copy-done.1, bf16[32,56,8,128]{3,2,1,0:T(8,128)(2,1)} %all-to-all-done.1.kv_ref, f32[1024,1792]{1,0:T(8,128)S(1)} %copy-done.9, ...), custom_call_target="tpu_custom_call" | custom-call | tf_op jit(solution)/shard_map/final_attention/pallas_call | solution.py:241
  (27 shorter events, 0.5 us)
Async XLA Ops:
  0.9 1.5 copy-start.10
  2.4 1.5 copy-start.11
  4.2 1.9 %copy-start.2 = (bf16[32,57,8,128]{3,2,1,0:T(8,128)(2,1)}, bf16[32,57,8,128]{3,2,1,0:T(8,128)(2,1)S(1)}, u32[]{:S(2)}) copy-start(bf16[32,57,8,128]{3,2,1,0:T(8,128)(2,1)S(1)} %pack_pieces.1) | copy-start | bytes 11206660
  6.0 52.1 %all-to-all-start = ((bf16[32,57,8,128]{3,2,1,0:T(8,128)(2,1)}), bf16[32,57,8,128]{3,2,1,0:T(8,128)(2,1)}, u32[]{:S(2)}, u32[]{:S(2)}) async-start(bf16[32,57,8,128]{3,2,1,0:T(8,128)(2,1)} %copy-done.2), calls=%async_computation | async-start | bytes 7471104 | tf_op jit(solution)/shard_map/all_to_all | solution.py:274
  16.6 62.8 %collective-permute-start = (bf16[512,1792]{1,0:T(8,128)(2,1)}, bf16[512,1792]{1,0:T(8,128)(2,1)S(1)}, u32[]{:S(2)}, u32[]{:S(2)}) collective-permute-start(bf16[512,1792]{1,0:T(8,128)(2,1)} %slice.18), channel_id=1, source_target_pairs={{4,0},{8,4},{12,8},{16,12},{20,16},{24,20},{28,24},{32,28},{36,32}... | collective-permute-start | bytes 5505032 | tf_op jit(solution)/shard_map/ppermute | solution.py:275
  63.9 1.8 %copy-start.3 = (bf16[32,56,8,128]{3,2,1,0:T(8,128)(2,1)}, bf16[32,56,8,128]{3,2,1,0:T(8,128)(2,1)S(1)}, u32[]{:S(2)}) copy-start(bf16[32,56,8,128]{3,2,1,0:T(8,128)(2,1)S(1)} %gather_pieces.1) | copy-start | bytes 11010052
  65.8 75.0 %all-to-all-start.1 = ((bf16[32,56,8,128]{3,2,1,0:T(8,128)(2,1)}), bf16[32,56,8,128]{3,2,1,0:T(8,128)(2,1)}, u32[]{:S(2)}, u32[]{:S(2)}) async-start(bf16[32,56,8,128]{3,2,1,0:T(8,128)(2,1)} %copy-done.3), calls=%async_computation.1 | async-start | bytes 7340032 | tf_op jit(solution)/shard_map/all_to_all | solution.py:286
  75.0 22.9 %copy-start = (bf16[1024,1792]{1,0:T(8,128)(2,1)S(1)}, bf16[1024,1792]{1,0:T(8,128)(2,1)}, u32[]{:S(2)}) copy-start(bf16[1024,1792]{1,0:T(8,128)(2,1)} %q_ref.3) | copy-start | bytes 11010052
  79.4 2.0 %copy-start.4 = (bf16[1024,1792]{1,0:T(8,128)(2,1)S(1)}, bf16[1024,1792]{1,0:T(8,128)(2,1)}, u32[]{:S(2)}) copy-start(bf16[1024,1792]{1,0:T(8,128)(2,1)} %k_ref.3) | copy-start | bytes 11010052
  81.4 2.0 %copy-start.6 = (bf16[1024,1792]{1,0:T(8,128)(2,1)S(1)}, bf16[1024,1792]{1,0:T(8,128)(2,1)}, u32[]{:S(2)}) copy-start(bf16[1024,1792]{1,0:T(8,128)(2,1)} %v_ref.3) | copy-start | bytes 11010052
  83.5 14.5 %copy-start.5 = (bf16[1024,1792]{1,0:T(8,128)(2,1)S(1)}, bf16[1024,1792]{1,0:T(8,128)(2,1)}, u32[]{:S(2)}) copy-start(bf16[1024,1792]{1,0:T(8,128)(2,1)} %k_ref.3) | copy-start | bytes 11010052
  83.5 14.5 %copy-start.7 = (bf16[1024,1792]{1,0:T(8,128)(2,1)S(1)}, bf16[1024,1792]{1,0:T(8,128)(2,1)}, u32[]{:S(2)}) copy-start(bf16[1024,1792]{1,0:T(8,128)(2,1)} %v_ref.3) | copy-start | bytes 11010052
  96.0 44.8 %collective-permute-start.1 = (bf16[512,1920]{1,0:T(8,128)(2,1)}, bf16[512,1920]{1,0:T(8,128)(2,1)S(1)}, u32[]{:S(2)}, u32[]{:S(2)}) collective-permute-start(bf16[512,1920]{1,0:T(8,128)(2,1)} %next_attention.1), channel_id=1, source_target_pairs={{0,4},{4,8},{8,12},{12,16},{16,20},{20,24},{24,28},{28,32},{32,36}... | collective-permute-start | bytes 5898248 | tf_op jit(solution)/shard_map/ppermute | solution.py:278
  98.0 27.3 %copy-start.12 = (f32[14]{0:T(128)S(1)}, f32[14]{0:T(128)}, u32[]{:S(2)}) copy-start(f32[14]{0:T(128)} %param.15) | copy-start | bytes 172
  122.3 2.9 %copy-start.8 = (f32[1024,1792]{1,0:T(8,128)}, f32[1024,1792]{1,0:T(8,128)S(1)}, u32[]{:S(2)}) copy-start(f32[1024,1792]{1,0:T(8,128)S(1)} %get-tuple-element.19.own_ref) | copy-start | bytes 22020100
  140.8 2.0 %copy-start.1 = (bf16[1024,1792]{1,0:T(8,128)(2,1)S(1)}, bf16[1024,1792]{1,0:T(8,128)(2,1)}, u32[]{:S(2)}) copy-start(bf16[1024,1792]{1,0:T(8,128)(2,1)} %q_ref.3) | copy-start | bytes 11010052
  142.8 3.1 %copy-start.9 = (f32[1024,1792]{1,0:T(8,128)S(1)}, f32[1024,1792]{1,0:T(8,128)}, u32[]{:S(2)}) copy-start(f32[1024,1792]{1,0:T(8,128)} %copy-done.8) | copy-start | bytes 22020100
where the time goes:
time: 161 us; the launch traced here: 160 us
  waiting for transfers between devices  56.9 us (35%)
  Pallas kernels  56.2 us (35%)
  starting transfers between devices  23.1 us (14%)
  local copies, waits for them, and re-layouts  22.1 us (14%)
    all_to_all x1, waiting for transfers between devices, body(): store = lax.all_to_all(sent, 'seq', split_axis=0, concat_axis=0, tiled=True)  37.1 us
    pallas_call x1, Pallas kernels, own_attention(): pl.pallas_call(functools.partial(own_kernel, scale), out_shape=(jax.Shape...  24.4 us
    unnamed x26, local copies, waits for them, and re-layouts  18.8 us
    ppermute x1, waiting for transfers between devices, body(): lax.ppermute(partial, 'seq', [(i, i + 1) for i in range(devices - 1)])  15.5 us
    pallas_call x1, Pallas kernels, final_attention(): pl.pallas_call(functools.partial(final_kernel, scale, heads), out_shape=j...  14.3 us
    pallas_call x1, Pallas kernels, next_attention(): pl.pallas_call(functools.partial(next_kernel, scale, heads), out_shape=ja...  12.5 us
    all_to_all x1, starting transfers between devices, body(): kv = lax.all_to_all(pieces, 'seq', split_axis=0, concat_axis=0, tiled=True)  9.24 us
    all_to_all x1, starting transfers between devices, body(): store = lax.all_to_all(sent, 'seq', split_axis=0, concat_axis=0, tiled=True)  7.67 us
  transfers between devices with their start and end apart: 4, of which 3 were waited for; matrix products, arithmetic and copies ran while one was open for 2% of the time, Pallas kernels for 26%

commit v1 on v0

--- a/solution.py
+++ b/solution.py
@@ -16,6 +16,15 @@
 EDGE = 256
 LOG2E = 1.4426950408889634
 NEG = -1e30
+VMEM_LIMIT = 16 << 20
+
+
+def params():
+    return pltpu.CompilerParams(vmem_limit_bytes=VMEM_LIMIT)
+
+
+def cost(micros):
+    return pl.CostEstimate(flops=int(micros * 1e9), transcendentals=0, bytes_accessed=0)
 BF = jnp.bfloat16
 F32 = jnp.float32
 
@@ -40,7 +49,8 @@
         out_shape=jax.ShapeDtypeStruct((2 * MB // PIECE, blocks * heads + 1, PIECE, DH), BF),
         in_specs=[pl.BlockSpec(memory_space=pltpu.VMEM)] * 3,
         out_specs=pl.BlockSpec(memory_space=pltpu.VMEM),
-        compiler_params=pltpu.CompilerParams(vmem_limit_bytes=32 << 20),
+        compiler_params=params(),
+        cost_estimate=cost(2),
         name="pack_pieces",
     )(mem_keys.reshape(shape), mem_values.reshape(shape), ids_tile)
 
@@ -66,7 +76,8 @@
             in_specs=[pl.BlockSpec(store.shape, lambda i, rows: (0, 0, 0))],
             out_specs=pl.BlockSpec((group, wanted, PIECE, DH), lambda i, rows: (i, 0, 0, 0)),
         ),
-        compiler_params=pltpu.CompilerParams(vmem_limit_bytes=32 << 20),
+        compiler_params=params(),
+        cost_estimate=cost(6),
         name="gather_pieces",
     )(rows, store)
 
@@ -139,7 +150,8 @@
         grid=(heads,),
         in_specs=[column] * 3,
         out_specs=(column, pl.BlockSpec((WIN, DH), lambda h: (0, 0))),
-        compiler_params=pltpu.CompilerParams(vmem_limit_bytes=32 << 20),
+        compiler_params=params(),
+        cost_estimate=cost(20),
         name="own_attention",
     )(queries, keys, values)
 
@@ -196,57 +208,38 @@
         in_specs=[column, tail, tail],
         out_specs=pl.BlockSpec((WIN, DH), lambda h: (0, h)),
         scratch_shapes=[pltpu.VMEM((WIN, DH), F32)],
-        compiler_params=pltpu.CompilerParams(vmem_limit_bytes=32 << 20),
+        compiler_params=params(),
+        cost_estimate=cost(30),
         name="next_attention",
     )(queries, keys, values)
 
 
-def final_kernel(
-    scale, heads, first_ref, gate_ref, q_ref, kv_ref, own_ref, lse_ref, back_ref, stat_ref, out_ref
-):
+def merge_kernel(heads, first_ref, gate_ref, own_ref, lse_ref, back_ref, stat_ref, out_ref):
     head = pl.program_id(0)
-    c = scale * LOG2E
-    gate = gate_ref[head]
-    pieces = MB // PIECE
-    blocks = q_ref.shape[0] // QB
-    for b in range(blocks):
-        rows = pl.ds(b * QB, QB)
-        mine = slice(b * TOPK, (b + 1) * TOPK)
-        keys = kv_ref[0:pieces, mine].astype(F32).reshape(TOPK * MB, DH).astype(BF)
-        values = kv_ref[pieces : 2 * pieces, mine].astype(F32).reshape(TOPK * MB, DH).astype(BF)
-        s = dot_t(q_ref[rows, :], keys)
-        top = jnp.max(s, axis=1, keepdims=True)
-        p = jnp.exp2((s - top) * c)
-        total = jnp.sum(p, axis=1, keepdims=True)
-        remote = dot(p.astype(BF), values) / total
-        local = own_ref[rows, :]
-        if b == 0:
-            lanes = lax.broadcasted_iota(jnp.int32, (WIN, DH), 1)
-            lse = jnp.sum(jnp.where(lanes == head, lse_ref[...], 0.0), axis=1, keepdims=True)
-            hit = (lanes == head) | (lanes == head + heads) | (lanes == head + 2 * heads)
-            other = jnp.sum(
-                jnp.where(hit, stat_ref[...].astype(F32), 0.0), axis=1, keepdims=True
-            )
-            other = jnp.where(first_ref[0] == 0, NEG, other)
-            share = 1.0 / (1.0 + jnp.exp2(other - lse))
-            back = back_ref[...].astype(F32)
-            local = local * share + back * (1.0 - share)
-        out_ref[rows, :] = (gate * remote + (1.0 - gate) * local).astype(BF)
-
-
-def final_attention(first, gate, queries, kv, own, lse, back, heads, scale):
-    tokens = queries.shape[0]
-    blocks = tokens // QB
+    keep = 1.0 - gate_ref[head]
+    low, high = pl.ds(0, WIN), pl.ds(WIN, own_ref.shape[0] - WIN)
+    lanes = lax.broadcasted_iota(jnp.int32, (WIN, DH), 1)
+    lse = jnp.sum(jnp.where(lanes == head, lse_ref[...], 0.0), axis=1, keepdims=True)
+    hit = (lanes == head) | (lanes == head + heads) | (lanes == head + 2 * heads)
+    other = jnp.sum(jnp.where(hit, stat_ref[...].astype(F32), 0.0), axis=1, keepdims=True)
+    other = jnp.where(first_ref[0] == 0, NEG, other)
+    share = 1.0 / (1.0 + jnp.exp2(other - lse))
+    back = back_ref[...].astype(F32)
+    local = own_ref[low, :] * share + back * (1.0 - share)
+    out_ref[low, :] = (local * keep).astype(BF)
+    out_ref[high, :] = (own_ref[high, :] * keep).astype(BF)
+
+
+def merge(first, gate, own, lse, back, heads):
+    tokens = own.shape[0]
     column = pl.BlockSpec((tokens, DH), lambda h, *_: (0, h))
     return pl.pallas_call(
-        functools.partial(final_kernel, scale, heads),
-        out_shape=jax.ShapeDtypeStruct(queries.shape, BF),
+        functools.partial(merge_kernel, heads),
+        out_shape=jax.ShapeDtypeStruct(own.shape, BF),
         grid_spec=pltpu.PrefetchScalarGridSpec(
             num_scalar_prefetch=2,
             grid=(heads,),
             in_specs=[
-                column,
-                pl.BlockSpec((kv.shape[0], blocks * TOPK, PIECE, DH), lambda h, *_: (0, h, 0, 0)),
                 column,
                 pl.BlockSpec((WIN, DH), lambda h, *_: (0, 0)),
                 pl.BlockSpec((WIN, DH), lambda h, *_: (0, h)),
@@ -254,9 +247,67 @@
             ],
             out_specs=column,
         ),
-        compiler_params=pltpu.CompilerParams(vmem_limit_bytes=32 << 20),
+        compiler_params=params(),
+        cost_estimate=cost(60),
+        name="merge_local",
+    )(first, gate, own, lse, back, back)
+
+
+def final_kernel(scale, heads, gate_ref, q_ref, kv_ref, local_ref, out_ref):
+    c = scale * LOG2E
+    pieces = MB // PIECE
+    for head in range(heads):
+        cols = pl.ds(head * DH, DH)
+        mine = pl.ds(head * TOPK, TOPK)
+        keys = kv_ref[0:pieces, mine].astype(F32).reshape(TOPK * MB, DH).astype(BF)
+        values = kv_ref[pieces : 2 * pieces, mine].astype(F32).reshape(TOPK * MB, DH).astype(BF)
+        values = jnp.concatenate([values, jnp.ones_like(values)], axis=1)
+        s = dot_t(q_ref[:, cols], keys)
+        top = jnp.max(s, axis=1, keepdims=True)
+        p = jnp.exp2((s - top) * c).astype(BF)
+        acc = dot(p, values)
+        remote = acc[:, :DH] * (gate_ref[head] / acc[:, DH:])
+        out_ref[:, cols] = (remote + local_ref[:, cols].astype(F32)).astype(BF)
+
+
+def final_attention(gate, queries, kv, local, heads, scale):
+    tokens, width = queries.shape
+    rows = 256
+    per = QB // rows
+    band = pl.BlockSpec((rows, width), lambda i, *_: (i, 0))
+    return pl.pallas_call(
+        functools.partial(final_kernel, scale, heads),
+        out_shape=jax.ShapeDtypeStruct(queries.shape, BF),
+        grid_spec=pltpu.PrefetchScalarGridSpec(
+            num_scalar_prefetch=1,
+            grid=(tokens // rows,),
+            in_specs=[
+                band,
+                pl.BlockSpec((kv.shape[0], heads * TOPK, PIECE, DH), lambda i, *_: (0, i // per, 0, 0)),
+                band,
+            ],
+            out_specs=band,
+        ),
+        compiler_params=params(),
+        cost_estimate=cost(7),
         name="final_attention",
-    )(first, gate, queries, kv, own, lse, back, back)
+    )(gate, queries, kv, local)
+
+
+def copy_kernel(in_ref, out_ref):
+    out_ref[...] = in_ref[...]
+
+
+def copy_rows(array, rows):
+    block = pl.BlockSpec((256, array.shape[1]), lambda i: (i, 0))
+    return pl.pallas_call(
+        copy_kernel,
+        out_shape=jax.ShapeDtypeStruct((rows, array.shape[1]), array.dtype),
+        grid=(rows // 256,),
+        in_specs=[block],
+        out_specs=block,
+        name="copy_rows",
+    )(array)
 
 
 def body(queries, token_keys, token_values, mem_keys, mem_values, retrieved, gate_bias):
@@ -267,26 +318,30 @@
     blocks = mem_keys.shape[0] // MB
     q_blocks = tokens // QB
     wanted = q_blocks * heads * TOPK
-    head_q = queries[:WIN]
-    ids = retrieved.transpose(1, 0, 2).reshape(-1)
+    head_q = copy_rows(queries, WIN)
+    next_q = lax.ppermute(head_q, "seq", [(i, i - 1) for i in range(1, devices)])
+    ids = retrieved.reshape(-1)
     ids_tile = jnp.zeros((PIECE * DH,), BF).at[:wanted].set(ids.astype(BF)).reshape(PIECE, DH)
+    ids_tile, _ = lax.optimization_barrier((ids_tile, head_q))
     sent = pack(mem_keys, mem_values, ids_tile, blocks, heads)
     store = lax.all_to_all(sent, "seq", split_axis=0, concat_axis=0, tiled=True)
-    next_q = lax.ppermute(head_q, "seq", [(i, i - 1) for i in range(1, devices)])
+    gate_share = 1.0 / (1.0 + jnp.exp(-gate_bias))
+    first = lax.axis_index("seq").reshape(1).astype(jnp.int32)
     own, lse = own_attention(queries, token_keys, token_values, heads, scale)
     partial = next_attention(next_q, token_keys, token_values, heads, scale)
+    store, own, lse, partial = lax.optimization_barrier((store, own, lse, partial))
     back = lax.ppermute(partial, "seq", [(i, i + 1) for i in range(devices - 1)])
     all_ids = store[:, blocks * heads, 0, :wanted].astype(jnp.int32)
     stride = blocks * heads + 1
-    request_head = jnp.arange(wanted, dtype=jnp.int32) // (q_blocks * TOPK)
+    request_head = jnp.arange(wanted, dtype=jnp.int32) // TOPK % heads
     rows = (all_ids // blocks) * stride + (all_ids % blocks) * heads + request_head[None, :]
     pieces = gather(
         rows.reshape(-1), store.reshape(devices * stride, PIECE, DH), devices, wanted
     )
     kv = lax.all_to_all(pieces, "seq", split_axis=0, concat_axis=0, tiled=True)
-    gate_share = 1.0 / (1.0 + jnp.exp(-gate_bias))
-    first = lax.axis_index("seq").reshape(1).astype(jnp.int32)
-    return final_attention(first, gate_share, queries, kv, own, lse, back, heads, scale)
+    local = merge(first, gate_share, own, lse, back, heads)
+    kv, local = lax.optimization_barrier((kv, local))
+    return final_attention(gate_share, queries, kv, local, heads, scale)
 
 
 def solution(mesh):

time: 161 us -> 172 us (1.068)
  the two profiles are of different devices: /device:TPU:2 before, /device:TPU:1 now
where the time goes in v1:
time: 172 us; the launch traced here: 171 us
  Pallas kernels  63.6 us (37%)
  waiting for transfers between devices  63 us (37%)
  local copies, waits for them, and re-layouts  23.6 us (14%)
  starting transfers between devices  19.6 us (11%)
    ppermute x1, waiting for transfers between devices, body(): lax.ppermute(partial, 'seq', [(i, i + 1) for i in range(devices - 1)])  42.7 us
    pallas_call x1, Pallas kernels, own_attention(): pl.pallas_call(functools.partial(own_kernel, scale), out_shape=(jax.Shape...  24.3 us
    unnamed x30, local copies, waits for them, and re-layouts  23.2 us
    ppermute x1, waiting for transfers between devices, body(): lax.ppermute(head_q, 'seq', [(i, i - 1) for i in range(1, devices)])  20.2 us
    pallas_call x1, Pallas kernels, next_attention(): pl.pallas_call(functools.partial(next_kernel, scale, heads), out_shape=ja...  12.9 us
    pallas_call x1, Pallas kernels, merge(): pl.pallas_call(functools.partial(merge_kernel, heads), out_shape=jax.Shap...  9.88 us
    pallas_call x1, Pallas kernels, final_attention(): pl.pallas_call(functools.partial(final_kernel, scale, heads), out_shape=j...  8.84 us
    all_to_all x1, starting transfers between devices, body(): store = lax.all_to_all(sent, 'seq', split_axis=0, concat_axis=0, tiled=True)  8.09 us
  transfers between devices with their start and end apart: 4, of which 2 were waited for; matrix products, arithmetic and copies ran while one was open for 1% of the time, Pallas kernels for 31%

profile of v1, /device:TPU:1, one launch (start us, length us, event | category | flops | bytes accessed | tf_op | source)
XLA Modules:
  0.0 170.9 jit_solution(5416239877572012043)
XLA Ops:
  0.0 2.6 %copy_rows.1 = bf16[512,1792]{1,0:T(8,128)(2,1)} custom-call(bf16[1024,1792]{1,0:T(8,128)(2,1)} %q_ref.3), custom_call_target="tpu_custom_call" | custom-call | tf_op jit(solution)/shard_map/copy_rows/pallas_call | solution.py:303
  2.6 3.3 %collective-permute-start = (bf16[512,1792]{1,0:T(8,128)(2,1)}, bf16[512,1792]{1,0:T(8,128)(2,1)}, u32[]{:S(2)}, u32[]{:S(2)}) collective-permute-start(bf16[512,1792]{1,0:T(8,128)(2,1)} %copy_rows.1), channel_id=1, source_target_pairs={{4,0},{8,4},{12,8},{16,12},{20,16},{24,20},{28,24},{32,28},{36,32}... | collective-permute-start | bytes 5505032 | tf_op jit(solution)/shard_map/ppermute | solution.py:322
  6.2 1.5 copy-done.5
  8.0 1.9 %copy-done = bf16[32,57,8,128]{3,2,1,0:T(8,128)(2,1)} copy-done((bf16[32,57,8,128]{3,2,1,0:T(8,128)(2,1)}, bf16[32,57,8,128]{3,2,1,0:T(8,128)(2,1)S(1)}, u32[]{:S(2)}) %copy-start) | copy-done | bytes 3735576
  9.9 8.1 %all-to-all-start = ((bf16[32,57,8,128]{3,2,1,0:T(8,128)(2,1)}), bf16[32,57,8,128]{3,2,1,0:T(8,128)(2,1)}, u32[]{:S(2)}, u32[]{:S(2)}) async-start(bf16[32,57,8,128]{3,2,1,0:T(8,128)(2,1)} %copy-done), calls=%async_computation | async-start | bytes 7471104 | tf_op jit(solution)/shard_map/all_to_all | solution.py:327
  18.0 2.0 %copy-done.2 = bf16[1024,1792]{1,0:T(8,128)(2,1)S(1)} copy-done((bf16[1024,1792]{1,0:T(8,128)(2,1)S(1)}, bf16[1024,1792]{1,0:T(8,128)(2,1)}, u32[]{:S(2)}) %copy-start.2) | copy-done | bytes 3670040
  20.0 2.0 %copy-done.6 = bf16[1024,1792]{1,0:T(8,128)(2,1)S(1)} copy-done((bf16[1024,1792]{1,0:T(8,128)(2,1)S(1)}, bf16[1024,1792]{1,0:T(8,128)(2,1)}, u32[]{:S(2)}) %copy-start.6) | copy-done | bytes 3670040
  22.1 2.0 %copy-done.8 = bf16[1024,1792]{1,0:T(8,128)(2,1)S(1)} copy-done((bf16[1024,1792]{1,0:T(8,128)(2,1)S(1)}, bf16[1024,1792]{1,0:T(8,128)(2,1)}, u32[]{:S(2)}) %copy-start.8) | copy-done | bytes 3670040
  24.1 24.3 %own_attention.1 = (f32[1024,1792]{1,0:T(8,128)S(1)}, f32[512,128]{1,0:T(8,128)S(1)}) custom-call(bf16[1024,1792]{1,0:T(8,128)(2,1)S(1)} %copy-done.2, bf16[1024,1792]{1,0:T(8,128)(2,1)S(1)} %copy-done.6, bf16[1024,1792]{1,0:T(8,128)(2,1)S(1)} %copy-done.8), custom_call_target="tpu_custom_call" | custom-call | flops 20000000000 | tf_op jit(solution)/shard_map/own_attention/pallas_call | solution.py:144
  48.5 2.9 %copy-done.11 = f32[1024,1792]{1,0:T(8,128)} copy-done((f32[1024,1792]{1,0:T(8,128)}, f32[1024,1792]{1,0:T(8,128)S(1)}, u32[]{:S(2)}) %copy-start.11) | copy-done | bytes 7340056
  51.4 20.2 %collective-permute-done.q_ref = bf16[512,1792]{1,0:T(8,128)(2,1)} collective-permute-done((bf16[512,1792]{1,0:T(8,128)(2,1)}, bf16[512,1792]{1,0:T(8,128)(2,1)}, u32[]{:S(2)}, u32[]{:S(2)}) %collective-permute-start) | collective-permute-done | bytes 1835040 | tf_op jit(solution)/shard_map/ppermute | solution.py:322
  71.6 12.9 %next_attention.1 = bf16[512,1920]{1,0:T(8,128)(2,1)S(1)} custom-call(bf16[512,1792]{1,0:T(8,128)(2,1)} %collective-permute-done.q_ref, bf16[1024,1792]{1,0:T(8,128)(2,1)S(1)} %copy-done.7, bf16[1024,1792]{1,0:T(8,128)(2,1)S(1)} %copy-done.8), custom_call_target="tpu_custom_call" | custom-call | flops 30000001024 | tf_op jit(solution)/shard_map/next_attention/pallas_call | solution.py:204
  84.5 1.9 %collective-permute-start.1 = (bf16[512,1920]{1,0:T(8,128)(2,1)S(1)}, bf16[512,1920]{1,0:T(8,128)(2,1)}, u32[]{:S(2)}, u32[]{:S(2)}) collective-permute-start(bf16[512,1920]{1,0:T(8,128)(2,1)S(1)} %next_attention.1), channel_id=1, source_target_pairs={{0,4},{4,8},{8,12},{12,16},{16,20},{20,24},{24,28},{28,32},{32,36}... | collective-permute-start | bytes 5898248 | tf_op jit(solution)/shard_map/ppermute | solution.py:333
  86.6 0.9 convert_reduce_fusion
  87.6 4.8 %gather_pieces.1 = bf16[32,56,8,128]{3,2,1,0:T(8,128)(2,1)S(1)} custom-call(s32[1792]{0:T(1024)S(1)} %fusion.2.rows_ref, bf16[1824,8,128]{2,1,0:T(8,128)(2,1)} %bitcast.3.store_ref), custom_call_target="tpu_custom_call" | custom-call | flops 6000000000 | tf_op jit(solution)/shard_map/gather_pieces/pallas_call | solution.py:70
  92.4 1.8 %copy-done.1 = bf16[32,56,8,128]{3,2,1,0:T(8,128)(2,1)} copy-done((bf16[32,56,8,128]{3,2,1,0:T(8,128)(2,1)}, bf16[32,56,8,128]{3,2,1,0:T(8,128)(2,1)S(1)}, u32[]{:S(2)}) %copy-start.1) | copy-done | bytes 3670040
  94.3 6.3 %all-to-all-start.1 = ((bf16[32,56,8,128]{3,2,1,0:T(8,128)(2,1)}), bf16[32,56,8,128]{3,2,1,0:T(8,128)(2,1)}, u32[]{:S(2)}, u32[]{:S(2)}) async-start(bf16[32,56,8,128]{3,2,1,0:T(8,128)(2,1)} %copy-done.1), calls=%async_computation.1 | async-start | bytes 7340032 | tf_op jit(solution)/shard_map/all_to_all | solution.py:341
  100.5 42.7 %collective-permute-done.1.back_ref.stat_ref = bf16[512,1920]{1,0:T(8,128)(2,1)} collective-permute-done((bf16[512,1920]{1,0:T(8,128)(2,1)S(1)}, bf16[512,1920]{1,0:T(8,128)(2,1)}, u32[]{:S(2)}, u32[]{:S(2)}) %collective-permute-start.1) | collective-permute-done | bytes 1966112 | tf_op jit(solution)/shard_map/ppermute | solution.py:333
  143.3 3.1 %copy-done.12 = f32[1024,1792]{1,0:T(8,128)S(1)} copy-done((f32[1024,1792]{1,0:T(8,128)S(1)}, f32[1024,1792]{1,0:T(8,128)}, u32[]{:S(2)}) %copy-start.12) | copy-done | bytes 7340056
  146.3 9.9 %merge_local.1.local_ref = bf16[1024,1792]{1,0:T(8,128)(2,1)S(1)} custom-call(s32[1]{0:T(128)} %bitcast.4.first_ref, f32[14]{0:T(128)S(1)} %add_divide_fusion.gate_ref, f32[1024,1792]{1,0:T(8,128)S(1)} %copy-done.12, f32[512,128]{1,0:T(8,128)S(1)} %get-tuple-element.31.lse_ref, bf16[512,1920]{1,0:T(8,128)(2,1)} %collective-permute-done.1.back_ref.stat_ref, ...), custom_call_target="tpu_custom_call" | custom-call | flops 60000002048 | tf_op jit(solution)/shard_map/merge_local/pallas_call | solution.py:236
  156.2 1.8 %copy-done.9 = bf16[1024,1792]{1,0:T(8,128)(2,1)} copy-done((bf16[1024,1792]{1,0:T(8,128)(2,1)}, bf16[1024,1792]{1,0:T(8,128)(2,1)S(1)}, u32[]{:S(2)}) %copy-start.9) | copy-done | bytes 3670040
  158.0 2.0 %copy-done.3 = bf16[1024,1792]{1,0:T(8,128)(2,1)S(1)} copy-done((bf16[1024,1792]{1,0:T(8,128)(2,1)S(1)}, bf16[1024,1792]{1,0:T(8,128)(2,1)}, u32[]{:S(2)}) %copy-start.3) | copy-done | bytes 3670040
  160.1 2.0 %copy-done.10 = bf16[1024,1792]{1,0:T(8,128)(2,1)S(1)} copy-done((bf16[1024,1792]{1,0:T(8,128)(2,1)S(1)}, bf16[1024,1792]{1,0:T(8,128)(2,1)}, u32[]{:S(2)}) %copy-start.10) | copy-done | bytes 3670040
  162.1 8.8 %final_attention.1 = bf16[1024,1792]{1,0:T(8,128)(2,1)} custom-call(f32[14]{0:T(128)S(1)} %add_divide_fusion.gate_ref, bf16[1024,1792]{1,0:T(8,128)(2,1)S(1)} %copy-done.3, bf16[32,56,8,128]{3,2,1,0:T(8,128)(2,1)} %all-to-all-done.1.kv_ref, bf16[1024,1792]{1,0:T(8,128)(2,1)S(1)} %copy-done.10), custom_call_target="tpu_custom_call" | custom-call | flops 7000000000 | tf_op jit(solution)/shard_map/final_attention/pallas_call | solution.py:278
  (32 shorter events, 0.7 us)
Async XLA Ops:
  0.0 5.9 %copy-start.13 = (s32[2,14,2]{1,2,0:T(2,128)S(1)}, s32[2,14,2]{1,2,0:T(2,128)}, u32[]{:S(2)}) copy-start(s32[2,14,2]{1,2,0:T(2,128)} %param.14) | copy-start | bytes 676
  0.0 6.2 %copy-start.4 = (bf16[512,1792]{1,0:T(8,128)(2,1)S(1)}, bf16[512,1792]{1,0:T(8,128)(2,1)}, u32[]{:S(2)}) copy-start(bf16[512,1792]{1,0:T(8,128)(2,1)} %param.12) | copy-start | bytes 5505028
  2.6 69.0 %collective-permute-start = (bf16[512,1792]{1,0:T(8,128)(2,1)}, bf16[512,1792]{1,0:T(8,128)(2,1)}, u32[]{:S(2)}, u32[]{:S(2)}) collective-permute-start(bf16[512,1792]{1,0:T(8,128)(2,1)} %copy_rows.1), channel_id=1, source_target_pairs={{4,0},{8,4},{12,8},{16,12},{20,16},{24,20},{28,24},{32,28},{36,32}... | collective-permute-start | bytes 5505032 | tf_op jit(solution)/shard_map/ppermute | solution.py:322
  6.2 1.5 copy-start.5
  8.0 1.9 %copy-start = (bf16[32,57,8,128]{3,2,1,0:T(8,128)(2,1)}, bf16[32,57,8,128]{3,2,1,0:T(8,128)(2,1)S(1)}, u32[]{:S(2)}) copy-start(bf16[32,57,8,128]{3,2,1,0:T(8,128)(2,1)S(1)} %pack_pieces.1) | copy-start | bytes 11206660
  9.9 74.6 %all-to-all-start = ((bf16[32,57,8,128]{3,2,1,0:T(8,128)(2,1)}), bf16[32,57,8,128]{3,2,1,0:T(8,128)(2,1)}, u32[]{:S(2)}, u32[]{:S(2)}) async-start(bf16[32,57,8,128]{3,2,1,0:T(8,128)(2,1)} %copy-done), calls=%async_computation | async-start | bytes 7471104 | tf_op jit(solution)/shard_map/all_to_all | solution.py:327
  18.0 2.0 %copy-start.2 = (bf16[1024,1792]{1,0:T(8,128)(2,1)S(1)}, bf16[1024,1792]{1,0:T(8,128)(2,1)}, u32[]{:S(2)}) copy-start(bf16[1024,1792]{1,0:T(8,128)(2,1)} %q_ref.3) | copy-start | bytes 11010052
  20.0 2.0 %copy-start.6 = (bf16[1024,1792]{1,0:T(8,128)(2,1)S(1)}, bf16[1024,1792]{1,0:T(8,128)(2,1)}, u32[]{:S(2)}) copy-start(bf16[1024,1792]{1,0:T(8,128)(2,1)} %k_ref.3) | copy-start | bytes 11010052
  22.1 2.0 %copy-start.8 = (bf16[1024,1792]{1,0:T(8,128)(2,1)S(1)}, bf16[1024,1792]{1,0:T(8,128)(2,1)}, u32[]{:S(2)}) copy-start(bf16[1024,1792]{1,0:T(8,128)(2,1)} %v_ref.3) | copy-start | bytes 11010052
  24.1 47.5 %copy-start.7 = (bf16[1024,1792]{1,0:T(8,128)(2,1)S(1)}, bf16[1024,1792]{1,0:T(8,128)(2,1)}, u32[]{:S(2)}) copy-start(bf16[1024,1792]{1,0:T(8,128)(2,1)} %k_ref.3) | copy-start | bytes 11010052
  48.4 2.9 %copy-start.11 = (f32[1024,1792]{1,0:T(8,128)}, f32[1024,1792]{1,0:T(8,128)S(1)}, u32[]{:S(2)}) copy-start(f32[1024,1792]{1,0:T(8,128)S(1)} %get-tuple-element.30.own_ref) | copy-start | bytes 22020100
  51.4 35.2 %copy-start.14 = (f32[14]{0:T(128)S(1)}, f32[14]{0:T(128)}, u32[]{:S(2)}) copy-start(f32[14]{0:T(128)} %param.15) | copy-start | bytes 172
  84.5 58.7 %collective-permute-start.1 = (bf16[512,1920]{1,0:T(8,128)(2,1)S(1)}, bf16[512,1920]{1,0:T(8,128)(2,1)}, u32[]{:S(2)}, u32[]{:S(2)}) collective-permute-start(bf16[512,1920]{1,0:T(8,128)(2,1)S(1)} %next_attention.1), channel_id=1, source_target_pairs={{0,4},{4,8},{8,12},{12,16},{16,20},{20,24},{24,28},{28,32},{32,36}... | collective-permute-start | bytes 5898248 | tf_op jit(solution)/shard_map/ppermute | solution.py:333
  92.4 1.8 %copy-start.1 = (bf16[32,56,8,128]{3,2,1,0:T(8,128)(2,1)}, bf16[32,56,8,128]{3,2,1,0:T(8,128)(2,1)S(1)}, u32[]{:S(2)}) copy-start(bf16[32,56,8,128]{3,2,1,0:T(8,128)(2,1)S(1)} %gather_pieces.1) | copy-start | bytes 11010052
  94.3 63.7 %all-to-all-start.1 = ((bf16[32,56,8,128]{3,2,1,0:T(8,128)(2,1)}), bf16[32,56,8,128]{3,2,1,0:T(8,128)(2,1)}, u32[]{:S(2)}, u32[]{:S(2)}) async-start(bf16[32,56,8,128]{3,2,1,0:T(8,128)(2,1)} %copy-done.1), calls=%async_computation.1 | async-start | bytes 7340032 | tf_op jit(solution)/shard_map/all_to_all | solution.py:341
  143.3 3.1 %copy-start.12 = (f32[1024,1792]{1,0:T(8,128)S(1)}, f32[1024,1792]{1,0:T(8,128)}, u32[]{:S(2)}) copy-start(f32[1024,1792]{1,0:T(8,128)} %copy-done.11) | copy-start | bytes 22020100
  156.2 1.8 %copy-start.9 = (bf16[1024,1792]{1,0:T(8,128)(2,1)}, bf16[1024,1792]{1,0:T(8,128)(2,1)S(1)}, u32[]{:S(2)}) copy-start(bf16[1024,1792]{1,0:T(8,128)(2,1)S(1)} %merge_local.1.local_ref) | copy-start | bytes 11010052
  158.0 2.0 %copy-start.3 = (bf16[1024,1792]{1,0:T(8,128)(2,1)S(1)}, bf16[1024,1792]{1,0:T(8,128)(2,1)}, u32[]{:S(2)}) copy-start(bf16[1024,1792]{1,0:T(8,128)(2,1)} %q_ref.3) | copy-start | bytes 11010052
  160.0 2.0 %copy-start.10 = (bf16[1024,1792]{1,0:T(8,128)(2,1)S(1)}, bf16[1024,1792]{1,0:T(8,128)(2,1)}, u32[]{:S(2)}) copy-start(bf16[1024,1792]{1,0:T(8,128)(2,1)} %copy-done.9) | copy-start | bytes 11010052

commit v2 on v1

v2 whole, which is shorter than its diff:
```python
import functools

import jax
import jax.numpy as jnp
from jax import lax
from jax.experimental import pallas as pl
from jax.experimental.pallas import tpu as pltpu
from jax.sharding import PartitionSpec as P

QB = 512
MB = 128
TOPK = 2
WIN = 512
DH = 128
PIECE = 8
EDGE = 256
FORWARD = 5
LOG2E = 1.4426950408889634
NEG = -1e30
VMEM_LIMIT = 24 << 20
BF = jnp.bfloat16
F32 = jnp.float32
ANY = pl.BlockSpec(memory_space=pl.ANY)
WHOLE = pl.BlockSpec(memory_space=pltpu.VMEM)
SMALL = pl.BlockSpec(memory_space=pltpu.SMEM)


def params():
    return pltpu.CompilerParams(vmem_limit_bytes=VMEM_LIMIT)


def cost(micros):
    return pl.CostEstimate(flops=int(micros * 1e9), transcendentals=0, bytes_accessed=0)


def in_hbm(array):
    return pltpu.with_memory_space_constraint(array, pltpu.HBM)


def copy_all(copies):
    for copy in copies:
        copy.start()
    for copy in copies:
        copy.wait()


def edges_kernel(q_ref, k_ref, v_ref, back_ref, ahead_ref, sems):
    split = FORWARD * DH
    tail = pl.ds(k_ref.shape[0] - WIN, WIN)
    width = q_ref.shape[1] - split
    copy_all(
        [
            pltpu.make_async_copy(
                q_ref.at[pl.ds(0, WIN), pl.ds(split, width)], back_ref, sems.at[0]
            ),
            pltpu.make_async_copy(
                k_ref.at[tail, pl.ds(0, split)], ahead_ref.at[:, pl.ds(0, split)], sems.at[1]
            ),
            pltpu.make_async_copy(
                v_ref.at[tail, pl.ds(0, split)], ahead_ref.at[:, pl.ds(split, split)], sems.at[2]
            ),
        ]
    )


def edges(queries, keys, values):
    split = FORWARD * DH
    return pl.pallas_call(
        edges_kernel,
        out_shape=(
            pltpu.HBM((WIN, queries.shape[1] - split), BF),
            pltpu.HBM((WIN, 2 * split), BF),
        ),
        in_specs=[ANY] * 3,
        out_specs=(ANY, ANY),
        scratch_shapes=[pltpu.SemaphoreType.DMA((3,))],
        cost_estimate=cost(2),
        name="cut_edges",
    )(queries, keys, values)


def pack_kernel(blocks, heads, keys_ref, values_ref, ids_ref, out_ref, sems):
    pieces = MB // PIECE
    copies = []
    for half, source in enumerate((keys_ref, values_ref)):
        for block in range(blocks):
            copies.append(
                pltpu.make_async_copy(
                    source.at[pl.ds(block * pieces, pieces)],
                    out_ref.at[pl.ds(half * pieces, pieces), pl.ds(block * heads, heads)],
                    sems.at[len(copies)],
                )
            )
    copies.append(
        pltpu.make_async_copy(ids_ref, out_ref.at[:, pl.ds(blocks * heads, 1)], sems.at[len(copies)])
    )
    copy_all(copies)


def tiles(array):
    rows, width = array.shape
    return array.reshape(rows // PIECE, PIECE, width // DH, DH).transpose(0, 2, 1, 3)


def pack(mem_keys, mem_values, ids_tile, blocks, heads):
    devices = 2 * MB // PIECE
    return pl.pallas_call(
        functools.partial(pack_kernel, blocks, heads),
        out_shape=pltpu.HBM((devices, blocks * heads + 1, PIECE, DH), BF),
        in_specs=[ANY] * 3,
        out_specs=ANY,
        scratch_shapes=[pltpu.SemaphoreType.DMA((2 * blocks + 1,))],
        cost_estimate=cost(2),
        name="pack_pieces",
    )(
        in_hbm(tiles(mem_keys)),
        in_hbm(tiles(mem_values)),
        jnp.broadcast_to(ids_tile, (devices, 1, PIECE, DH)),
    )


def gather_kernel(wanted, group, rows_ref, store_ref, out_ref):
    first = pl.program_id(0) * group

    @pl.loop(0, group)
    def _(device):
        base = (first + device) * wanted
        for request in range(wanted):
            out_ref[device, request] = store_ref[rows_ref[base + request]]


def gather(rows, store, devices, wanted):
    group = 4
    return pl.pallas_call(
        functools.partial(gather_kernel, wanted, group),
        out_shape=pltpu.HBM((devices, wanted, PIECE, DH), BF),
        grid_spec=pltpu.PrefetchScalarGridSpec(
            num_scalar_prefetch=1,
            grid=(devices // group,),
            in_specs=[pl.BlockSpec(store.shape, lambda i, rows: (0, 0, 0))],
            out_specs=pl.BlockSpec((group, wanted, PIECE, DH), lambda i, rows: (i, 0, 0, 0)),
        ),
        compiler_params=params(),
        cost_estimate=cost(6),
        name="gather_pieces",
    )(rows, store)


def dot_t(a, b):
    return lax.dot_general(a, b, (((1,), (1,)), ((), ())), preferred_element_type=F32)


def dot(a, b):
    return jnp.dot(a, b, preferred_element_type=F32)


def with_ones(values):
    return jnp.concatenate([values, jnp.ones_like(values)], axis=1)


def triangle():
    row = lax.broadcasted_iota(jnp.int32, (EDGE, EDGE), 0)
    col = lax.broadcasted_iota(jnp.int32, (EDGE, EDGE), 1)
    return col <= row


def own_kernel(scale, heads, q_ref, k_ref, v_ref, low_ref, lse_ref, out_ref):
    lower = triangle()
    c = scale * LOG2E
    lanes = lax.broadcasted_iota(jnp.int32, (EDGE, DH), 1)
    for head in range(heads):
        cols = pl.ds(head * DH, DH)
        for i in range(WIN // EDGE):
            rows = pl.ds(i * EDGE, EDGE)
            seen = pl.ds(0, (i + 1) * EDGE)
            s = dot_t(q_ref[rows, cols], k_ref[seen, cols])
            diag = jnp.where(lower, s[:, i * EDGE :], NEG)
            if i:
                s = jnp.concatenate([s[:, : i * EDGE], diag], axis=1)
            else:
                s = diag
            top = jnp.max(s, axis=1, keepdims=True)
            p = jnp.exp2((s - top) * c).astype(BF)
            acc = dot(p, with_ones(v_ref[seen, cols]))
            total = acc[:, DH:]
            low_ref[rows, cols] = acc[:, :DH] / total
            lse_ref[rows, :] = jnp.where(lanes == head, top * c + jnp.log2(total), lse_ref[rows, :])
        for i in range(WIN // EDGE, q_ref.shape[0] // EDGE):
            rows = pl.ds(i * EDGE, EDGE)
            seen = pl.ds(i * EDGE - WIN, WIN + EDGE)
            s = dot_t(q_ref[rows, cols], k_ref[seen, cols])
            ends = jnp.where(lower, s[:, WIN:], s[:, :EDGE])
            mid = s[:, EDGE:WIN]
            top = jnp.maximum(
                jnp.max(ends, axis=1, keepdims=True), jnp.max(mid, axis=1, keepdims=True)
            )
            ends = jnp.exp2((ends - top) * c)
            mid = jnp.exp2((mid - top) * c).astype(BF)
            first = jnp.where(lower, 0.0, ends).astype(BF)
            last = jnp.where(lower, ends, 0.0).astype(BF)
            acc = dot(jnp.concatenate([first, mid, last], axis=1), with_ones(v_ref[seen, cols]))
            out_ref[rows, cols] = (acc[:, :DH] / acc[:, DH:]).astype(BF)


def own_attention(queries, keys, values, heads, scale):
    tokens, width = queries.shape
    return pl.pallas_call(
        functools.partial(own_kernel, scale, heads),
        out_shape=(
            jax.ShapeDtypeStruct((WIN, width), F32),
            jax.ShapeDtypeStruct((WIN, DH), F32),
            jax.ShapeDtypeStruct((tokens, width), BF),
        ),
        in_specs=[WHOLE] * 3,
        out_specs=(WHOLE,) * 3,
        compiler_params=params(),
        cost_estimate=cost(20),
        name="own_attention",
    )(queries, keys, values)


def edge_kernel(scale, q_heads, k_heads, v_heads, tail, q_ref, k_ref, v_ref, out_ref, lse_ref):
    lower = triangle()
    c = scale * LOG2E
    lanes = lax.broadcasted_iota(jnp.int32, (EDGE, DH), 1)
    count = len(q_heads)
    lse_ref[...] = jnp.zeros_like(lse_ref)
    for slot in range(count):
        q_cols = pl.ds(q_heads[slot] * DH, DH)
        k_cols = pl.ds(k_heads[slot] * DH, DH)
        v_cols = pl.ds(v_heads[slot] * DH, DH)
        for i in range(WIN // EDGE):
            rows = pl.ds(i * EDGE, EDGE)
            seen = pl.ds(tail + i * EDGE, WIN - i * EDGE)
            s = dot_t(q_ref[rows, q_cols], k_ref[seen, k_cols])
            edge = jnp.where(lower, NEG, s[:, :EDGE])
            if s.shape[1] > EDGE:
                s = jnp.concatenate([edge, s[:, EDGE:]], axis=1)
            else:
                s = edge
            top = jnp.max(s, axis=1, keepdims=True)
            p = jnp.exp2((s - top) * c).astype(BF)
            acc = dot(p, with_ones(v_ref[seen, v_cols]))
            total = acc[:, DH:]
            out_ref[rows, pl.ds(slot * DH, DH)] = (acc[:, :DH] / total).astype(BF)
            lse_ref[rows, :] = jnp.where(lanes == slot, top * c + jnp.log2(total), lse_ref[rows, :])
    stat = lse_ref[...]
    high = stat.astype(BF).astype(F32)
    mid = (stat - high).astype(BF).astype(F32)
    low = (stat - high - mid).astype(BF).astype(F32)
    packed = high + pltpu.roll(mid, count, 1) + pltpu.roll(low, 2 * count, 1)
    out_ref[:, pl.ds(count * DH, DH)] = packed.astype(BF)


def edge_attention(queries, keys, values, q_heads, k_heads, v_heads, tail, scale, micros, name):
    return pl.pallas_call(
        functools.partial(edge_kernel, scale, q_heads, k_heads, v_heads, tail),
        out_shape=jax.ShapeDtypeStruct((WIN, (len(q_heads) + 1) * DH), BF),
        in_specs=[WHOLE] * 3,
        out_specs=WHOLE,
        scratch_shapes=[pltpu.VMEM((WIN, DH), F32)],
        compiler_params=params(),
        cost_estimate=cost(micros),
        name=name,
    )(queries, keys, values)


def merge_kernel(heads, first_ref, low_ref, lse_ref, near_ref, far_ref, into_ref, out_ref):
    del into_ref
    for i in range(WIN // EDGE):
        rows = pl.ds(i * EDGE, EDGE)
        for head in range(heads):
            near = head < FORWARD
            ref, count, slot = (
                (near_ref, FORWARD, head) if near else (far_ref, heads - FORWARD, head - FORWARD)
            )
            stat = ref[rows, pl.ds(count * DH, DH)].astype(F32)
            other = (
                stat[:, slot : slot + 1]
                + stat[:, count + slot : count + slot + 1]
                + stat[:, 2 * count + slot : 2 * count + slot + 1]
            )
            other = jnp.where(first_ref[0] == 0, NEG, other)
            share = 1.0 / (1.0 + jnp.exp2(other - lse_ref[rows, head : head + 1]))
            cols = pl.ds(head * DH, DH)
            there = ref[rows, pl.ds(slot * DH, DH)].astype(F32)
            out_ref[rows, cols] = (low_ref[rows, cols] * share + there * (1.0 - share)).astype(BF)


def merge(first, low, lse, near, far, local, heads):
    width = low.shape[1]
    whole = lambda array: pl.BlockSpec(array.shape, lambda i: (0, 0))
    return pl.pallas_call(
        functools.partial(merge_kernel, heads),
        out_shape=pltpu.HBM(local.shape, BF),
        grid=(1,),
        in_specs=[SMALL, whole(low), whole(lse), whole(near), whole(far), ANY],
        out_specs=pl.BlockSpec((WIN, width), lambda i: (0, 0)),
        input_output_aliases={5: 0},
        compiler_params=params(),
        cost_estimate=cost(60),
        name="merge_local",
    )(first, low, lse, near, far, in_hbm(local))


def final_kernel(scale, heads, gate_ref, q_ref, kv_ref, local_ref, out_ref):
    c = scale * LOG2E
    pieces = MB // PIECE
    for head in range(heads):
        cols = pl.ds(head * DH, DH)
        mine = pl.ds(head * TOPK, TOPK)
        keys = kv_ref[0:pieces, mine].astype(F32).reshape(TOPK * MB, DH).astype(BF)
        values = kv_ref[pieces : 2 * pieces, mine].astype(F32).reshape(TOPK * MB, DH).astype(BF)
        s = dot_t(q_ref[:, cols], keys)
        top = jnp.max(s, axis=1, keepdims=True)
        p = jnp.exp2((s - top) * c).astype(BF)
        acc = dot(p, with_ones(values))
        gate = gate_ref[head]
        remote = acc[:, :DH] * (gate / acc[:, DH:])
        local = local_ref[:, cols].astype(F32)
        out_ref[:, cols] = (remote + (1.0 - gate) * local).astype(BF)


def final_attention(gate, queries, kv, local, heads, scale):
    tokens, width = queries.shape
    rows = 256
    per = QB // rows
    band = pl.BlockSpec((rows, width), lambda i, *_: (i, 0))
    return pl.pallas_call(
        functools.partial(final_kernel, scale, heads),
        out_shape=jax.ShapeDtypeStruct(queries.shape, BF),
        grid_spec=pltpu.PrefetchScalarGridSpec(
            num_scalar_prefetch=1,
            grid=(tokens // rows,),
            in_specs=[
                band,
                pl.BlockSpec((kv.shape[0], heads * TOPK, PIECE, DH), lambda i, *_: (0, i // per, 0, 0)),
                band,
            ],
            out_specs=band,
        ),
        compiler_params=params(),
        cost_estimate=cost(7),
        name="final_attention",
    )(gate, queries, kv, local)


def body(queries, token_keys, token_values, mem_keys, mem_values, retrieved, gate_bias):
    tokens = queries.shape[0]
    heads = gate_bias.shape[0]
    scale = DH ** (-0.5)
    devices = lax.axis_size("seq")
    blocks = mem_keys.shape[0] // MB
    q_blocks = tokens // QB
    wanted = q_blocks * heads * TOPK
    far_heads = list(range(FORWARD, heads))
    near_heads = list(range(FORWARD))
    upward = [(i, i + 1) for i in range(devices - 1)]
    downward = [(i, i - 1) for i in range(1, devices)]
    back_q, ahead_kv = edges(queries, token_keys, token_values)
    far_q = lax.ppermute(back_q, "seq", downward)
    near_kv = lax.ppermute(ahead_kv, "seq", upward)
    ids = retrieved.reshape(-1)
    ids_tile = jnp.zeros((PIECE * DH,), BF).at[:wanted].set(ids.astype(BF)).reshape(PIECE, DH)
    ids_tile, _ = lax.optimization_barrier((ids_tile, back_q))
    sent = pack(mem_keys, mem_values, ids_tile, blocks, heads)
    store = lax.all_to_all(sent, "seq", split_axis=0, concat_axis=0, tiled=True)
    gate_share = 1.0 / (1.0 + jnp.exp(-gate_bias))
    first = lax.axis_index("seq").reshape(1).astype(jnp.int32)
    low, lse, local = own_attention(queries, token_keys, token_values, heads, scale)
    far_part = edge_attention(
        far_q,
        token_keys,
        token_values,
        list(range(len(far_heads))),
        far_heads,
        far_heads,
        tokens - WIN,
        scale,
        60,
        "far_attention",
    )
    store, low, lse, local, far_part = lax.optimization_barrier((store, low, lse, local, far_part))
    far = lax.ppermute(far_part, "seq", upward)
    all_ids = store[:, blocks * heads, 0, :wanted].astype(jnp.int32)
    stride = blocks * heads + 1
    request_head = jnp.arange(wanted, dtype=jnp.int32) // TOPK % heads
    rows = (all_ids // blocks) * stride + (all_ids % blocks) * heads + request_head[None, :]
    pieces = gather(rows.reshape(-1), store.reshape(devices * stride, PIECE, DH), devices, wanted)
    pieces, late_q = lax.optimization_barrier((pieces, queries))
    kv = lax.all_to_all(pieces, "seq", split_axis=0, concat_axis=0, tiled=True)
    near = edge_attention(
        late_q,
        near_kv,
        near_kv,
        near_heads,
        near_heads,
        [FORWARD + head for head in near_heads],
        0,
        scale,
        5,
        "near_attention",
    )
    local = merge(first, low, lse, near, far, local, heads)
    kv, local = lax.optimization_barrier((kv, local))
    return final_attention(gate_share, in_hbm(queries), in_hbm(kv), in_hbm(local), heads, scale)


def solution(mesh):
    in_specs = (
        P("seq", "head"),
        P("seq", "head"),
        P("seq", "head"),
        P("seq", "head"),
        P("seq", "head"),
        P("seq", "head", None),
        P("head"),
    )
    return jax.shard_map(
        body, mesh=mesh, in_specs=in_specs, out_specs=P("seq", "head"), check_vma=False
    )
```

time: 172 us -> 328 us (1.91)
  Pallas kernels: 63.6 us -> 237 us
  waiting for transfers between devices: 63 us -> 50.8 us
  local copies, waits for them, and re-layouts: 23.6 us -> 15.3 us
  starting transfers between devices: 19.6 us -> 23.3 us
    pallas_call x5 -> x6, Pallas kernels: 50 us -> 220 us  [the longest x1 114 us: pack(): pl.pallas_call(functools.partial(pack_kernel, blocks, heads), out_shape=p...]
    ppermute x2 -> x3, waiting for transfers between devices: 62.9 us -> 38.1 us  [the longest x1 38.1 us: body(): far = lax.ppermute(far_part, 'seq', upward)]
    all_to_all x1, waiting for transfers between devices: 0.01 us -> 12.7 us  [body(): store = lax.all_to_all(sent, 'seq', split_axis=0, concat_axis=0, tiled=True)]
    unnamed x30 -> x26, local copies, waits for them, and re-layouts: 23.2 us -> 14.3 us
    ppermute x2 -> x3, starting transfers between devices: 5.24 us -> 11.3 us  [the longest x1 4.48 us: body(): far = lax.ppermute(far_part, 'seq', upward)]
  transfers between devices with their start and end apart: 4 -> 5, of which waited for: 2 -> 2; matrix products, arithmetic and copies ran while one was open for 1% -> 1% of each run, Pallas kernels for 31% -> 46%
where the time goes in v2:
time: 328 us
  Pallas kernels  237 us (72%)
  waiting for transfers between devices  50.8 us (15%)
  starting transfers between devices  23.3 us (7%)
  local copies, waits for them, and re-layouts  15.3 us (5%)
    pallas_call x1, Pallas kernels, pack(): pl.pallas_call(functools.partial(pack_kernel, blocks, heads), out_shape=p...  114 us
    pallas_call x1, Pallas kernels, edges(): pl.pallas_call(edges_kernel, out_shape=(pltpu.HBM((WIN, queries.shape[1]...  76.6 us
    ppermute x1, waiting for transfers between devices, body(): far = lax.ppermute(far_part, 'seq', upward)  38.1 us
    pallas_call x1, Pallas kernels, own_attention(): pl.pallas_call(functools.partial(own_kernel, scale, heads), out_shape=(ja...  14.7 us
    unnamed x26, local copies, waits for them, and re-layouts  14.3 us
    all_to_all x1, waiting for transfers between devices, body(): store = lax.all_to_all(sent, 'seq', split_axis=0, concat_axis=0, tiled=True)  12.7 us
    pallas_call x1, Pallas kernels, final_attention(): pl.pallas_call(functools.partial(final_kernel, scale, heads), out_shape=j...  10.1 us
    pallas_call x1, Pallas kernels, merge(): pl.pallas_call(functools.partial(merge_kernel, heads), out_shape=pltpu.HB...  8.83 us
  transfers between devices with their start and end apart: 5, of which 2 were waited for; matrix products, arithmetic and copies ran while one was open for 1% of the time, Pallas kernels for 46%

profile of v2, /device:TPU:1, one launch (start us, length us, event | category | flops | bytes accessed | tf_op | source)
XLA Modules:
  0.0 327.6 jit_solution(3423605170507976228)
XLA Ops:
  0.0 76.6 %cut_edges.1 = (bf16[512,1152]{1,0:T(8,128)(2,1)}, bf16[512,1280]{1,0:T(8,128)(2,1)}) custom-call(bf16[1024,1792]{1,0:T(8,128)(2,1)} %q_ref.6, bf16[1024,1792]{1,0:T(8,128)(2,1)} %k_ref.5, bf16[1024,1792]{1,0:T(8,128)(2,1)} %v_ref.5), custom_call_target="tpu_custom_call" | custom-call | flops 2000000000 | tf_op jit(solution)/shard_map/cut_edges/pallas_call | solution.py:68
  76.6 3.3 %collective-permute-start = (bf16[512,1152]{1,0:T(8,128)(2,1)}, bf16[512,1152]{1,0:T(8,128)(2,1)S(1)}, u32[]{:S(2)}, u32[]{:S(2)}) collective-permute-start(bf16[512,1152]{1,0:T(8,128)(2,1)} %get-tuple-element.32), channel_id=1, source_target_pairs={{4,0},{8,4},{12,8},{16,12},{20,16},{24,20},{28,24},{32,28},{36,32}... | collective-permute-start | bytes 3538952 | tf_op jit(solution)/shard_map/ppermute | solution.py:361
  80.8 114.3 %pack_pieces.1 = bf16[32,57,8,128]{3,2,1,0:T(8,128)(2,1)} custom-call(bf16[64,14,8,128]{3,2,1,0:T(8,128)(2,1)} %bitcast.10, bf16[64,14,8,128]{3,2,1,0:T(8,128)(2,1)} %bitcast.11, bf16[32,1,8,128]{3,2,1,0:T(8,128)(2,1)} %broadcast_in_dim.2.ids_ref), custom_call_target="tpu_custom_call" | custom-call | flops 2000000000 | tf_op jit(solution)/shard_map/pack_pieces/pallas_call | solution.py:107
  195.2 7.3 %all-to-all-start = ((bf16[32,57,8,128]{3,2,1,0:T(8,128)(2,1)}), bf16[32,57,8,128]{3,2,1,0:T(8,128)(2,1)}, u32[]{:S(2)}, u32[]{:S(2)}) async-start(bf16[32,57,8,128]{3,2,1,0:T(8,128)(2,1)} %pack_pieces.1), calls=%async_computation | async-start | bytes 7471104 | tf_op jit(solution)/shard_map/all_to_all | solution.py:367
  202.5 3.5 %collective-permute-start.1 = (bf16[512,1280]{1,0:T(8,128)(2,1)}, bf16[512,1280]{1,0:T(8,128)(2,1)S(1)}, u32[]{:S(2)}, u32[]{:S(2)}) collective-permute-start(bf16[512,1280]{1,0:T(8,128)(2,1)} %get-tuple-element.42), channel_id=1, source_target_pairs={{0,4},{4,8},{8,12},{12,16},{16,20},{20,24},{24,28},{28,32},{32,36}... | collective-permute-start | bytes 3932168 | tf_op jit(solution)/shard_map/ppermute | solution.py:362
  206.2 2.0 copy-done
  208.3 2.0 copy-done.2
  210.3 2.0 copy-done.4
  212.3 14.7 %own_attention.1 = (f32[512,1792]{1,0:T(8,128)S(1)}, f32[512,128]{1,0:T(8,128)S(1)}, bf16[1024,1792]{1,0:T(8,128)(2,1)S(1)}) custom-call(bf16[1024,1792]{1,0:T(8,128)(2,1)S(1)} %copy-done.4, bf16[1024,1792]{1,0:T(8,128)(2,1)S(1)} %copy-done, bf16[1024,1792]{1,0:T(8,128)(2,1)S(1)} %copy-done.2), custom_call_target="tpu_custom_call" | custom-call | flops 20000000000 | tf_op jit(solution)/shard_map/own_attention/pallas_call | solution.py:207
  227.0 1.9 copy-done.8
  229.0 1.9 copy-done.9
  230.9 1.0 copy-done.6
  231.9 1.3 copy-done.7
  233.2 3.5 %far_attention.1 = bf16[512,1280]{1,0:T(8,128)(2,1)S(1)} custom-call(bf16[512,1152]{1,0:T(8,128)(2,1)S(1)} %copy-done.7, bf16[1024,1792]{1,0:T(8,128)(2,1)S(1)} %copy-done.1, bf16[1024,1792]{1,0:T(8,128)(2,1)S(1)} %copy-done.3), custom_call_target="tpu_custom_call" | custom-call | flops 60000002048 | tf_op jit(solution)/shard_map/far_attention/pallas_call | solution.py:256
  236.6 12.7 %all-to-all-done = bf16[32,57,8,128]{3,2,1,0:T(8,128)(2,1)} async-done(((bf16[32,57,8,128]{3,2,1,0:T(8,128)(2,1)}), bf16[32,57,8,128]{3,2,1,0:T(8,128)(2,1)}, u32[]{:S(2)}, u32[]{:S(2)}) %all-to-all-start) | async-done | bytes 3735584 | tf_op jit(solution)/shard_map/all_to_all | solution.py:367
  249.3 4.5 %collective-permute-start.2 = (bf16[512,1280]{1,0:T(8,128)(2,1)S(1)}, bf16[512,1280]{1,0:T(8,128)(2,1)}, u32[]{:S(2)}, u32[]{:S(2)}) collective-permute-start(bf16[512,1280]{1,0:T(8,128)(2,1)S(1)} %far_attention.1), channel_id=1, source_target_pairs={{0,4},{4,8},{8,12},{12,16},{16,20},{20,24},{24,28},{28,32},{32,36}... | collective-permute-start | bytes 3932168 | tf_op jit(solution)/shard_map/ppermute | solution.py:384
  253.8 0.9 convert_reduce_fusion
  254.8 7.1 %gather_pieces.1 = bf16[32,56,8,128]{3,2,1,0:T(8,128)(2,1)} custom-call(s32[1792]{0:T(1024)S(1)} %fusion.2.rows_ref, bf16[1824,8,128]{2,1,0:T(8,128)(2,1)} %bitcast.5.store_ref), custom_call_target="tpu_custom_call" | custom-call | flops 6000000000 | tf_op jit(solution)/shard_map/gather_pieces/pallas_call | solution.py:134
  261.9 4.6 %all-to-all-start.1 = ((bf16[32,56,8,128]{3,2,1,0:T(8,128)(2,1)}), bf16[32,56,8,128]{3,2,1,0:T(8,128)(2,1)}, u32[]{:S(2)}, u32[]{:S(2)}) async-start(bf16[32,56,8,128]{3,2,1,0:T(8,128)(2,1)} %gather_pieces.1), calls=%async_computation.1 | async-start | bytes 7340032 | tf_op jit(solution)/shard_map/all_to_all | solution.py:391
  266.5 2.0 copy-done.5
  268.6 2.1 near_attention.1.near_ref
  270.6 38.1 %collective-permute-done.2.far_ref = bf16[512,1280]{1,0:T(8,128)(2,1)} collective-permute-done((bf16[512,1280]{1,0:T(8,128)(2,1)S(1)}, bf16[512,1280]{1,0:T(8,128)(2,1)}, u32[]{:S(2)}, u32[]{:S(2)}) %collective-permute-start.2) | collective-permute-done | bytes 1310752 | tf_op jit(solution)/shard_map/ppermute | solution.py:384
  308.7 8.8 %merge_local.1.local_ref = bf16[1024,1792]{1,0:T(8,128)(2,1)} custom-call(s32[1]{0:T(128)} %bitcast.6.first_ref, f32[512,1792]{1,0:T(8,128)S(1)} %copy-done.10, f32[512,128]{1,0:T(8,128)S(1)} %get-tuple-element.40.lse_ref, bf16[512,768]{1,0:T(8,128)(2,1)S(1)} %near_attention.1.near_ref, ...), custom_call_target="tpu_custom_call", output_to_operand_aliasing={{}: (5, {})} | custom-call | flops 60000002048 | tf_op jit(solution)/shard_map/merge_local/pallas_call | solution.py:293
  317.6 10.1 %final_attention.1 = bf16[1024,1792]{1,0:T(8,128)(2,1)} custom-call(f32[14]{0:T(128)S(1)} %add_divide_fusion.gate_ref, bf16[1024,1792]{1,0:T(8,128)(2,1)} %q_ref.6, bf16[32,56,8,128]{3,2,1,0:T(8,128)(2,1)} %all-to-all-done.1.kv_ref, bf16[1024,1792]{1,0:T(8,128)(2,1)} %merge_local.1.local_ref), custom_call_target="tpu_custom_call" | custom-call | flops 7000000000 | tf_op jit(solution)/shard_map/final_attention/pallas_call | solution.py:329
  (32 shorter events, 1.1 us)
Async XLA Ops:
  0.0 79.9 %copy-start.11 = (s32[2,14,2]{1,2,0:T(2,128)S(1)}, s32[2,14,2]{1,2,0:T(2,128)}, u32[]{:S(2)}) copy-start(s32[2,14,2]{1,2,0:T(2,128)} %param.14) | copy-start | bytes 676
  76.6 154.3 %collective-permute-start = (bf16[512,1152]{1,0:T(8,128)(2,1)}, bf16[512,1152]{1,0:T(8,128)(2,1)S(1)}, u32[]{:S(2)}, u32[]{:S(2)}) collective-permute-start(bf16[512,1152]{1,0:T(8,128)(2,1)} %get-tuple-element.32), channel_id=1, source_target_pairs={{4,0},{8,4},{12,8},{16,12},{20,16},{24,20},{28,24},{32,28},{36,32}... | collective-permute-start | bytes 3538952 | tf_op jit(solution)/shard_map/ppermute | solution.py:361
  195.2 11.0 %copy-start.12 = (f32[14]{0:T(128)S(1)}, f32[14]{0:T(128)}, u32[]{:S(2)}) copy-start(f32[14]{0:T(128)} %param.15) | copy-start | bytes 172
  195.2 54.2 %all-to-all-start = ((bf16[32,57,8,128]{3,2,1,0:T(8,128)(2,1)}), bf16[32,57,8,128]{3,2,1,0:T(8,128)(2,1)}, u32[]{:S(2)}, u32[]{:S(2)}) async-start(bf16[32,57,8,128]{3,2,1,0:T(8,128)(2,1)} %pack_pieces.1), calls=%async_computation | async-start | bytes 7471104 | tf_op jit(solution)/shard_map/all_to_all | solution.py:367
  202.5 64.0 %collective-permute-start.1 = (bf16[512,1280]{1,0:T(8,128)(2,1)}, bf16[512,1280]{1,0:T(8,128)(2,1)S(1)}, u32[]{:S(2)}, u32[]{:S(2)}) collective-permute-start(bf16[512,1280]{1,0:T(8,128)(2,1)} %get-tuple-element.42), channel_id=1, source_target_pairs={{0,4},{4,8},{8,12},{12,16},{16,20},{20,24},{24,28},{28,32},{32,36}... | collective-permute-start | bytes 3932168 | tf_op jit(solution)/shard_map/ppermute | solution.py:362
  206.2 2.0 copy-start
  208.3 2.0 copy-start.2
  210.3 2.0 copy-start.4
  212.3 19.5 %copy-start.1 = (bf16[1024,1792]{1,0:T(8,128)(2,1)S(1)}, bf16[1024,1792]{1,0:T(8,128)(2,1)}, u32[]{:S(2)}) copy-start(bf16[1024,1792]{1,0:T(8,128)(2,1)} %k_ref.5) | copy-start | bytes 11010052
  212.3 19.5 %copy-start.3 = (bf16[1024,1792]{1,0:T(8,128)(2,1)S(1)}, bf16[1024,1792]{1,0:T(8,128)(2,1)}, u32[]{:S(2)}) copy-start(bf16[1024,1792]{1,0:T(8,128)(2,1)} %v_ref.5) | copy-start | bytes 11010052
  227.0 1.9 copy-start.8
  229.0 1.9 copy-start.9
  230.9 1.0 copy-start.6
  231.9 1.3 copy-start.7
  249.3 59.4 %collective-permute-start.2 = (bf16[512,1280]{1,0:T(8,128)(2,1)S(1)}, bf16[512,1280]{1,0:T(8,128)(2,1)}, u32[]{:S(2)}, u32[]{:S(2)}) collective-permute-start(bf16[512,1280]{1,0:T(8,128)(2,1)S(1)} %far_attention.1), channel_id=1, source_target_pairs={{0,4},{4,8},{8,12},{12,16},{16,20},{20,24},{24,28},{28,32},{32,36}... | collective-permute-start | bytes 3932168 | tf_op jit(solution)/shard_map/ppermute | solution.py:384
  261.9 55.7 %all-to-all-start.1 = ((bf16[32,56,8,128]{3,2,1,0:T(8,128)(2,1)}), bf16[32,56,8,128]{3,2,1,0:T(8,128)(2,1)}, u32[]{:S(2)}, u32[]{:S(2)}) async-start(bf16[32,56,8,128]{3,2,1,0:T(8,128)(2,1)} %gather_pieces.1), calls=%async_computation.1 | async-start | bytes 7340032 | tf_op jit(solution)/shard_map/all_to_all | solution.py:391
  266.5 2.0 copy-start.5
  268.6 40.2 %copy-start.10 = (f32[512,1792]{1,0:T(8,128)S(1)}, f32[512,1792]{1,0:T(8,128)}, u32[]{:S(2)}) copy-start(f32[512,1792]{1,0:T(8,128)} %copy-done.9) | copy-start | bytes 11010052

commit v3 on v2

--- a/solution.py
+++ b/solution.py
@@ -68,33 +68,41 @@
     return pl.pallas_call(
         edges_kernel,
         out_shape=(
-            pltpu.HBM((WIN, queries.shape[1] - split), BF),
-            pltpu.HBM((WIN, 2 * split), BF),
+            jax.ShapeDtypeStruct((WIN, queries.shape[1] - split), BF),
+            jax.ShapeDtypeStruct((WIN, 2 * split), BF),
         ),
         in_specs=[ANY] * 3,
-        out_specs=(ANY, ANY),
+        out_specs=(WHOLE, WHOLE),
         scratch_shapes=[pltpu.SemaphoreType.DMA((3,))],
+        compiler_params=params(),
         cost_estimate=cost(2),
         name="cut_edges",
-    )(queries, keys, values)
-
-
-def pack_kernel(blocks, heads, keys_ref, values_ref, ids_ref, out_ref, sems):
+    )(in_hbm(queries), in_hbm(keys), in_hbm(values))
+
+
+def pack_kernel(blocks, heads, keys_ref, values_ref, ids_ref, out_ref, stage, in_sems, out_sems):
     pieces = MB // PIECE
-    copies = []
+    loads, stores = [], []
     for half, source in enumerate((keys_ref, values_ref)):
         for block in range(blocks):
-            copies.append(
-                pltpu.make_async_copy(
-                    source.at[pl.ds(block * pieces, pieces)],
-                    out_ref.at[pl.ds(half * pieces, pieces), pl.ds(block * heads, heads)],
-                    sems.at[len(copies)],
-                )
-            )
-    copies.append(
-        pltpu.make_async_copy(ids_ref, out_ref.at[:, pl.ds(blocks * heads, 1)], sems.at[len(copies)])
-    )
-    copy_all(copies)
+            slot = len(loads)
+            here = stage.at[pl.ds(slot * pieces, pieces)]
+            there = out_ref.at[pl.ds(half * pieces, pieces), pl.ds(block * heads, heads)]
+            rows = pl.ds(block * pieces, pieces)
+            loads.append(pltpu.make_async_copy(source.at[rows], here, in_sems.at[slot]))
+            stores.append(pltpu.make_async_copy(here, there, out_sems.at[slot]))
+    ids_store = pltpu.make_async_copy(
+        ids_ref, out_ref.at[:, pl.ds(blocks * heads, 1)], out_sems.at[2 * blocks]
+    )
+    for load in loads:
+        load.start()
+    ids_store.start()
+    for load, store in zip(loads, stores):
+        load.wait()
+        store.start()
+    for store in stores:
+        store.wait()
+    ids_store.wait()
 
 
 def tiles(array):
@@ -107,9 +115,14 @@
     return pl.pallas_call(
         functools.partial(pack_kernel, blocks, heads),
         out_shape=pltpu.HBM((devices, blocks * heads + 1, PIECE, DH), BF),
-        in_specs=[ANY] * 3,
+        in_specs=[ANY, ANY, WHOLE],
         out_specs=ANY,
-        scratch_shapes=[pltpu.SemaphoreType.DMA((2 * blocks + 1,))],
+        scratch_shapes=[
+            pltpu.VMEM((2 * blocks * MB // PIECE, heads, PIECE, DH), BF),
+            pltpu.SemaphoreType.DMA((2 * blocks,)),
+            pltpu.SemaphoreType.DMA((2 * blocks + 1,)),
+        ],
+        compiler_params=params(),
         cost_estimate=cost(2),
         name="pack_pieces",
     )(
@@ -265,26 +278,29 @@
     )(queries, keys, values)
 
 
+def unpacked(stat, count):
+    return stat + pltpu.roll(stat, DH - count, 1) + pltpu.roll(stat, DH - 2 * count, 1)
+
+
 def merge_kernel(heads, first_ref, low_ref, lse_ref, near_ref, far_ref, into_ref, out_ref):
     del into_ref
+    lanes = lax.broadcasted_iota(jnp.int32, (EDGE, DH), 1)
+    behind = heads - FORWARD
     for i in range(WIN // EDGE):
         rows = pl.ds(i * EDGE, EDGE)
+        near_stat = unpacked(near_ref[rows, pl.ds(FORWARD * DH, DH)].astype(F32), FORWARD)
+        far_stat = unpacked(far_ref[rows, pl.ds(behind * DH, DH)].astype(F32), behind)
+        other = jnp.where(lanes < FORWARD, near_stat, pltpu.roll(far_stat, FORWARD, 1))
+        other = jnp.where(first_ref[0] == 0, NEG, other)
+        own = jnp.where(lanes < heads, lse_ref[rows, :], 0.0)
+        shares = 1.0 / (1.0 + jnp.exp2(other - own))
         for head in range(heads):
-            near = head < FORWARD
-            ref, count, slot = (
-                (near_ref, FORWARD, head) if near else (far_ref, heads - FORWARD, head - FORWARD)
-            )
-            stat = ref[rows, pl.ds(count * DH, DH)].astype(F32)
-            other = (
-                stat[:, slot : slot + 1]
-                + stat[:, count + slot : count + slot + 1]
-                + stat[:, 2 * count + slot : 2 * count + slot + 1]
-            )
-            other = jnp.where(first_ref[0] == 0, NEG, other)
-            share = 1.0 / (1.0 + jnp.exp2(other - lse_ref[rows, head : head + 1]))
+            ref, slot = (near_ref, head) if head < FORWARD else (far_ref, head - FORWARD)
+            share = shares[:, head : head + 1]
             cols = pl.ds(head * DH, DH)
+            mine = low_ref[rows, cols]
             there = ref[rows, pl.ds(slot * DH, DH)].astype(F32)
-            out_ref[rows, cols] = (low_ref[rows, cols] * share + there * (1.0 - share)).astype(BF)
+            out_ref[rows, cols] = (there + (mine - there) * share).astype(BF)
 
 
 def merge(first, low, lse, near, far, local, heads):
@@ -380,17 +396,8 @@
         60,
         "far_attention",
     )
-    store, low, lse, local, far_part = lax.optimization_barrier((store, low, lse, local, far_part))
-    far = lax.ppermute(far_part, "seq", upward)
-    all_ids = store[:, blocks * heads, 0, :wanted].astype(jnp.int32)
-    stride = blocks * heads + 1
-    request_head = jnp.arange(wanted, dtype=jnp.int32) // TOPK % heads
-    rows = (all_ids // blocks) * stride + (all_ids % blocks) * heads + request_head[None, :]
-    pieces = gather(rows.reshape(-1), store.reshape(devices * stride, PIECE, DH), devices, wanted)
-    pieces, late_q = lax.optimization_barrier((pieces, queries))
-    kv = lax.all_to_all(pieces, "seq", split_axis=0, concat_axis=0, tiled=True)
     near = edge_attention(
-        late_q,
+        queries,
         near_kv,
         near_kv,
         near_heads,
@@ -398,9 +405,19 @@
         [FORWARD + head for head in near_heads],
         0,
         scale,
-        5,
+        60,
         "near_attention",
     )
+    store, low, lse, local, far_part, near = lax.optimization_barrier(
+        (store, low, lse, local, far_part, near)
+    )
+    far = lax.ppermute(far_part, "seq", upward)
+    all_ids = store[:, blocks * heads, 0, :wanted].astype(jnp.int32)
+    stride = blocks * heads + 1
+    request_head = jnp.arange(wanted, dtype=jnp.int32) // TOPK % heads
+    rows = (all_ids // blocks) * stride + (all_ids % blocks) * heads + request_head[None, :]
+    pieces = gather(rows.reshape(-1), store.reshape(devices * stride, PIECE, DH), devices, wanted)
+    kv = lax.all_to_all(pieces, "seq", split_axis=0, concat_axis=0, tiled=True)
     local = merge(first, low, lse, near, far, local, heads)
     kv, local = lax.optimization_barrier((kv, local))
     return final_attention(gate_share, in_hbm(queries), in_hbm(kv), in_hbm(local), heads, scale)

time: 328 us -> 153 us (0.47)
  Pallas kernels: 237 us -> 47.4 us
  waiting for transfers between devices: 50.8 us -> 65.4 us
  starting transfers between devices: 23.3 us -> 28.1 us
  local copies, waits for them, and re-layouts: 15.3 us -> 10.6 us
    pallas_call x1, Pallas kernels: 114 us -> 3.12 us  [pack(): pl.pallas_call(functools.partial(pack_kernel, blocks, heads), out_shape=p...]
    pallas_call x1, Pallas kernels: 76.6 us -> 1.68 us  [edges(): pl.pallas_call(edges_kernel, out_shape=(jax.ShapeDtypeStruct((WIN, querie...]
    all_to_all x1, waiting for transfers between devices: 0.01 us -> 39.6 us  [body(): kv = lax.all_to_all(pieces, 'seq', split_axis=0, concat_axis=0, tiled=True)]
    ppermute x1, waiting for transfers between devices: 38.1 us -> 0.01 us  [body(): far = lax.ppermute(far_part, 'seq', upward)]
    ppermute x1, waiting for transfers between devices: 0.01 us -> 25.8 us  [body(): near_kv = lax.ppermute(ahead_kv, 'seq', upward)]
    all_to_all x1, waiting for transfers between devices: 12.7 us -> 0.01 us  [body(): store = lax.all_to_all(sent, 'seq', split_axis=0, concat_axis=0, tiled=True)]
    pallas_call x1, Pallas kernels: 8.83 us -> 3.18 us  [merge(): pl.pallas_call(functools.partial(merge_kernel, heads), out_shape=pltpu.HB...]
    all_to_all x1, starting transfers between devices: 4.61 us -> 8.97 us  [body(): kv = lax.all_to_all(pieces, 'seq', split_axis=0, concat_axis=0, tiled=True)]
  transfers between devices with their start and end apart: 5 -> 5, of which waited for: 2 -> 2; matrix products, arithmetic and copies ran while one was open for 1% -> 1% of each run, Pallas kernels for 46% -> 23%
where the time goes in v3:
time: 153 us
  waiting for transfers between devices  65.4 us (43%)
  Pallas kernels  47.4 us (31%)
  starting transfers between devices  28.1 us (18%)
  local copies, waits for them, and re-layouts  10.6 us (7%)
    all_to_all x1, waiting for transfers between devices, body(): kv = lax.all_to_all(pieces, 'seq', split_axis=0, concat_axis=0, tiled=True)  39.6 us
    ppermute x1, waiting for transfers between devices, body(): near_kv = lax.ppermute(ahead_kv, 'seq', upward)  25.8 us
    pallas_call x1, Pallas kernels, own_attention(): pl.pallas_call(functools.partial(own_kernel, scale, heads), out_shape=(ja...  14.6 us
    unnamed x24, local copies, waits for them, and re-layouts  10.2 us
    pallas_call x1, Pallas kernels, final_attention(): pl.pallas_call(functools.partial(final_kernel, scale, heads), out_shape=j...  10.1 us
    all_to_all x1, starting transfers between devices, body(): kv = lax.all_to_all(pieces, 'seq', split_axis=0, concat_axis=0, tiled=True)  8.97 us
    all_to_all x1, starting transfers between devices, body(): store = lax.all_to_all(sent, 'seq', split_axis=0, concat_axis=0, tiled=True)  7.92 us
    pallas_call x2, Pallas kernels, edge_attention(): pl.pallas_call(functools.partial(edge_kernel, scale, q_heads, k_heads, v_...  7.66 us
  transfers between devices with their start and end apart: 5, of which 2 were waited for; matrix products, arithmetic and copies ran while one was open for 1% of the time, Pallas kernels for 23%

profile of v3, /device:TPU:1, one launch (start us, length us, event | category | flops | bytes accessed | tf_op | source)
XLA Modules:
  0.0 152.8 jit_solution(15649115908722522703)
XLA Ops:
  0.0 1.7 %cut_edges.1 = (bf16[512,1152]{1,0:T(8,128)(2,1)S(1)}, bf16[512,1280]{1,0:T(8,128)(2,1)S(1)}) custom-call(bf16[1024,1792]{1,0:T(8,128)(2,1)} %q_ref.7, bf16[1024,1792]{1,0:T(8,128)(2,1)} %k_ref.5, bf16[1024,1792]{1,0:T(8,128)(2,1)} %v_ref.5), custom_call_target="tpu_custom_call" | custom-call | flops 2000000000 | tf_op jit(solution)/shard_map/cut_edges/pallas_call | solution.py:68
  1.7 3.3 %collective-permute-start = (bf16[512,1152]{1,0:T(8,128)(2,1)S(1)}, bf16[512,1152]{1,0:T(8,128)(2,1)}, u32[]{:S(2)}, u32[]{:S(2)}) collective-permute-start(bf16[512,1152]{1,0:T(8,128)(2,1)S(1)} %get-tuple-element.31), channel_id=1, source_target_pairs={{4,0},{8,4},{12,8},{16,12},{20,16},{24,20},{28,24},{32,28},{36,32}... | collective-permute-start | bytes 3538952 | tf_op jit(solution)/shard_map/ppermute | solution.py:377
  5.1 0.1 copy.10
  5.2 0.1 convert_element_type.14
  5.3 3.1 %pack_pieces.1 = bf16[32,57,8,128]{3,2,1,0:T(8,128)(2,1)} custom-call(bf16[64,14,8,128]{3,2,1,0:T(8,128)(2,1)} %bitcast.10, bf16[64,14,8,128]{3,2,1,0:T(8,128)(2,1)} %bitcast.11, bf16[32,1,8,128]{3,2,1,0:T(8,128)(2,1)S(1)} %broadcast_in_dim.2.ids_ref), custom_call_target="tpu_custom_call" | custom-call | flops 2000000000 | tf_op jit(solution)/shard_map/pack_pieces/pallas_call | solution.py:115
  8.4 7.9 %all-to-all-start = ((bf16[32,57,8,128]{3,2,1,0:T(8,128)(2,1)}), bf16[32,57,8,128]{3,2,1,0:T(8,128)(2,1)}, u32[]{:S(2)}, u32[]{:S(2)}) async-start(bf16[32,57,8,128]{3,2,1,0:T(8,128)(2,1)} %pack_pieces.1), calls=%async_computation | async-start | bytes 7471104 | tf_op jit(solution)/shard_map/all_to_all | solution.py:383
  16.4 3.5 %collective-permute-start.1 = (bf16[512,1280]{1,0:T(8,128)(2,1)S(1)}, bf16[512,1280]{1,0:T(8,128)(2,1)S(1)}, u32[]{:S(2)}, u32[]{:S(2)}) collective-permute-start(bf16[512,1280]{1,0:T(8,128)(2,1)S(1)} %get-tuple-element.36), channel_id=1, source_target_pairs={{0,4},{4,8},{8,12},{12,16},{16,20},{20,24},{24,28},{28,32},{32,36}... | collective-permute-start | bytes 3932168 | tf_op jit(solution)/shard_map/ppermute | solution.py:378
  19.9 2.0 %copy-done = bf16[1024,1792]{1,0:T(8,128)(2,1)S(1)} copy-done((bf16[1024,1792]{1,0:T(8,128)(2,1)S(1)}, bf16[1024,1792]{1,0:T(8,128)(2,1)}, u32[]{:S(2)}) %copy-start) | copy-done | bytes 3670040
  22.0 2.0 %copy-done.2 = bf16[1024,1792]{1,0:T(8,128)(2,1)S(1)} copy-done((bf16[1024,1792]{1,0:T(8,128)(2,1)S(1)}, bf16[1024,1792]{1,0:T(8,128)(2,1)}, u32[]{:S(2)}) %copy-start.2) | copy-done | bytes 3670040
  24.0 2.0 %copy-done.4 = bf16[1024,1792]{1,0:T(8,128)(2,1)S(1)} copy-done((bf16[1024,1792]{1,0:T(8,128)(2,1)S(1)}, bf16[1024,1792]{1,0:T(8,128)(2,1)}, u32[]{:S(2)}) %copy-start.4) | copy-done | bytes 3670040
  26.0 14.6 %own_attention.1 = (f32[512,1792]{1,0:T(8,128)S(1)}, f32[512,128]{1,0:T(8,128)S(1)}, bf16[1024,1792]{1,0:T(8,128)(2,1)S(1)}) custom-call(bf16[1024,1792]{1,0:T(8,128)(2,1)S(1)} %copy-done.4, bf16[1024,1792]{1,0:T(8,128)(2,1)S(1)} %copy-done, bf16[1024,1792]{1,0:T(8,128)(2,1)S(1)} %copy-done.2), custom_call_target="tpu_custom_call" | custom-call | flops 20000000000 | tf_op jit(solution)/shard_map/own_attention/pallas_call | solution.py:220
  40.7 5.6 %far_attention.1 = bf16[512,1280]{1,0:T(8,128)(2,1)S(1)} custom-call(bf16[512,1152]{1,0:T(8,128)(2,1)} %collective-permute-done.q_ref, bf16[1024,1792]{1,0:T(8,128)(2,1)S(1)} %copy-done.1, bf16[1024,1792]{1,0:T(8,128)(2,1)S(1)} %copy-done.3), custom_call_target="tpu_custom_call" | custom-call | flops 60000002048 | tf_op jit(solution)/shard_map/far_attention/pallas_call | solution.py:269
  46.4 25.8 %collective-permute-done.1.k_ref.v_ref = bf16[512,1280]{1,0:T(8,128)(2,1)S(1)} collective-permute-done((bf16[512,1280]{1,0:T(8,128)(2,1)S(1)}, bf16[512,1280]{1,0:T(8,128)(2,1)S(1)}, u32[]{:S(2)}, u32[]{:S(2)}) %collective-permute-start.1) | collective-permute-done | bytes 1310752 | tf_op jit(solution)/shard_map/ppermute | solution.py:378
  72.2 2.1 %near_attention.1.near_ref = bf16[512,768]{1,0:T(8,128)(2,1)S(1)} custom-call(bf16[1024,1792]{1,0:T(8,128)(2,1)S(1)} %copy-done.4, bf16[512,1280]{1,0:T(8,128)(2,1)S(1)} %collective-permute-done.1.k_ref.v_ref, bf16[512,1280]{1,0:T(8,128)(2,1)S(1)} %collective-permute-done.1.k_ref.v_ref), custom_call_target="tpu_custom_call" | custom-call | flops 60000002048 | tf_op jit(solution)/shard_map/near_attention/pallas_call | solution.py:269
  74.3 0.9 copy-done.8
  75.1 4.4 %collective-permute-start.2 = (bf16[512,1280]{1,0:T(8,128)(2,1)S(1)}, bf16[512,1280]{1,0:T(8,128)(2,1)S(1)}, u32[]{:S(2)}, u32[]{:S(2)}) collective-permute-start(bf16[512,1280]{1,0:T(8,128)(2,1)S(1)} %far_attention.1), channel_id=1, source_target_pairs={{0,4},{4,8},{8,12},{12,16},{16,20},{20,24},{24,28},{28,32},{32,36}... | collective-permute-start | bytes 3932168 | tf_op jit(solution)/shard_map/ppermute | solution.py:414
  79.7 0.9 convert_reduce_fusion
  80.7 7.1 %gather_pieces.1 = bf16[32,56,8,128]{3,2,1,0:T(8,128)(2,1)} custom-call(s32[1792]{0:T(1024)S(1)} %fusion.2.rows_ref, bf16[1824,8,128]{2,1,0:T(8,128)(2,1)} %bitcast.5.store_ref), custom_call_target="tpu_custom_call" | custom-call | flops 6000000000 | tf_op jit(solution)/shard_map/gather_pieces/pallas_call | solution.py:147
  87.7 9.0 %all-to-all-start.1 = ((bf16[32,56,8,128]{3,2,1,0:T(8,128)(2,1)}), bf16[32,56,8,128]{3,2,1,0:T(8,128)(2,1)}, u32[]{:S(2)}, u32[]{:S(2)}) async-start(bf16[32,56,8,128]{3,2,1,0:T(8,128)(2,1)} %gather_pieces.1), calls=%async_computation.1 | async-start | bytes 7340032 | tf_op jit(solution)/shard_map/all_to_all | solution.py:420
  96.7 2.0 %copy-done.7 = f32[512,1792]{1,0:T(8,128)S(1)} copy-done((f32[512,1792]{1,0:T(8,128)S(1)}, f32[512,1792]{1,0:T(8,128)}, u32[]{:S(2)}) %copy-start.7) | copy-done | bytes 3670040
  98.8 1.1 copy-done.9
  99.9 3.2 %merge_local.1.local_ref = bf16[1024,1792]{1,0:T(8,128)(2,1)} custom-call(s32[1]{0:T(128)} %bitcast.6.first_ref, f32[512,1792]{1,0:T(8,128)S(1)} %copy-done.7, f32[512,128]{1,0:T(8,128)S(1)} %get-tuple-element.39.lse_ref, bf16[512,768]{1,0:T(8,128)(2,1)S(1)} %copy-done.9, ...), custom_call_target="tpu_custom_call", output_to_operand_aliasing={{}: (5, {})} | custom-call | flops 60000002048 | tf_op jit(solution)/shard_map/merge_local/pallas_call | solution.py:309
  103.1 39.6 %all-to-all-done.1.kv_ref = bf16[32,56,8,128]{3,2,1,0:T(8,128)(2,1)} async-done(((bf16[32,56,8,128]{3,2,1,0:T(8,128)(2,1)}), bf16[32,56,8,128]{3,2,1,0:T(8,128)(2,1)}, u32[]{:S(2)}, u32[]{:S(2)}) %all-to-all-start.1) | async-done | bytes 3670048 | tf_op jit(solution)/shard_map/all_to_all | solution.py:420
  142.7 10.1 %final_attention.1 = bf16[1024,1792]{1,0:T(8,128)(2,1)} custom-call(f32[14]{0:T(128)S(1)} %add_divide_fusion.gate_ref, bf16[1024,1792]{1,0:T(8,128)(2,1)} %q_ref.7, bf16[32,56,8,128]{3,2,1,0:T(8,128)(2,1)} %all-to-all-done.1.kv_ref, bf16[1024,1792]{1,0:T(8,128)(2,1)} %merge_local.1.local_ref), custom_call_target="tpu_custom_call" | custom-call | flops 7000000000 | tf_op jit(solution)/shard_map/final_attention/pallas_call | solution.py:345
  (30 shorter events, 0.3 us)
Async XLA Ops:
  0.0 5.0 %copy-start.10 = (s32[2,14,2]{1,2,0:T(2,128)S(1)}, s32[2,14,2]{1,2,0:T(2,128)}, u32[]{:S(2)}) copy-start(s32[2,14,2]{1,2,0:T(2,128)} %param.14) | copy-start | bytes 676
  1.7 39.0 %collective-permute-start = (bf16[512,1152]{1,0:T(8,128)(2,1)S(1)}, bf16[512,1152]{1,0:T(8,128)(2,1)}, u32[]{:S(2)}, u32[]{:S(2)}) collective-permute-start(bf16[512,1152]{1,0:T(8,128)(2,1)S(1)} %get-tuple-element.31), channel_id=1, source_target_pairs={{4,0},{8,4},{12,8},{16,12},{20,16},{24,20},{28,24},{32,28},{36,32}... | collective-permute-start | bytes 3538952 | tf_op jit(solution)/shard_map/ppermute | solution.py:377
  8.4 66.7 %all-to-all-start = ((bf16[32,57,8,128]{3,2,1,0:T(8,128)(2,1)}), bf16[32,57,8,128]{3,2,1,0:T(8,128)(2,1)}, u32[]{:S(2)}, u32[]{:S(2)}) async-start(bf16[32,57,8,128]{3,2,1,0:T(8,128)(2,1)} %pack_pieces.1), calls=%async_computation | async-start | bytes 7471104 | tf_op jit(solution)/shard_map/all_to_all | solution.py:383
  16.4 55.8 %collective-permute-start.1 = (bf16[512,1280]{1,0:T(8,128)(2,1)S(1)}, bf16[512,1280]{1,0:T(8,128)(2,1)S(1)}, u32[]{:S(2)}, u32[]{:S(2)}) collective-permute-start(bf16[512,1280]{1,0:T(8,128)(2,1)S(1)} %get-tuple-element.36), channel_id=1, source_target_pairs={{0,4},{4,8},{8,12},{12,16},{16,20},{20,24},{24,28},{28,32},{32,36}... | collective-permute-start | bytes 3932168 | tf_op jit(solution)/shard_map/ppermute | solution.py:378
  19.9 2.0 %copy-start = (bf16[1024,1792]{1,0:T(8,128)(2,1)S(1)}, bf16[1024,1792]{1,0:T(8,128)(2,1)}, u32[]{:S(2)}) copy-start(bf16[1024,1792]{1,0:T(8,128)(2,1)} %k_ref.5) | copy-start | bytes 11010052
  22.0 2.0 %copy-start.2 = (bf16[1024,1792]{1,0:T(8,128)(2,1)S(1)}, bf16[1024,1792]{1,0:T(8,128)(2,1)}, u32[]{:S(2)}) copy-start(bf16[1024,1792]{1,0:T(8,128)(2,1)} %v_ref.5) | copy-start | bytes 11010052
  24.0 2.0 %copy-start.4 = (bf16[1024,1792]{1,0:T(8,128)(2,1)S(1)}, bf16[1024,1792]{1,0:T(8,128)(2,1)}, u32[]{:S(2)}) copy-start(bf16[1024,1792]{1,0:T(8,128)(2,1)} %q_ref.7) | copy-start | bytes 11010052
  26.0 14.7 %copy-start.1 = (bf16[1024,1792]{1,0:T(8,128)(2,1)S(1)}, bf16[1024,1792]{1,0:T(8,128)(2,1)}, u32[]{:S(2)}) copy-start(bf16[1024,1792]{1,0:T(8,128)(2,1)} %k_ref.5) | copy-start | bytes 11010052
  26.0 14.7 %copy-start.3 = (bf16[1024,1792]{1,0:T(8,128)(2,1)S(1)}, bf16[1024,1792]{1,0:T(8,128)(2,1)}, u32[]{:S(2)}) copy-start(bf16[1024,1792]{1,0:T(8,128)(2,1)} %v_ref.5) | copy-start | bytes 11010052
  40.7 5.7 %copy-start.5 = (bf16[1024,1792]{1,0:T(8,128)(2,1)}, bf16[1024,1792]{1,0:T(8,128)(2,1)S(1)}, u32[]{:S(2)}) copy-start(bf16[1024,1792]{1,0:T(8,128)(2,1)S(1)} %get-tuple-element.42.into_ref) | copy-start | bytes 11010052
  40.7 5.7 %copy-start.6 = (f32[512,1792]{1,0:T(8,128)}, f32[512,1792]{1,0:T(8,128)S(1)}, u32[]{:S(2)}) copy-start(f32[512,1792]{1,0:T(8,128)S(1)} %get-tuple-element.38.low_ref) | copy-start | bytes 11010052
  46.4 33.3 %copy-start.11 = (f32[14]{0:T(128)S(1)}, f32[14]{0:T(128)}, u32[]{:S(2)}) copy-start(f32[14]{0:T(128)} %param.15) | copy-start | bytes 172
  74.2 0.9 copy-start.8
  75.1 21.6 %collective-permute-start.2 = (bf16[512,1280]{1,0:T(8,128)(2,1)S(1)}, bf16[512,1280]{1,0:T(8,128)(2,1)S(1)}, u32[]{:S(2)}, u32[]{:S(2)}) collective-permute-start(bf16[512,1280]{1,0:T(8,128)(2,1)S(1)} %far_attention.1), channel_id=1, source_target_pairs={{0,4},{4,8},{8,12},{12,16},{16,20},{20,24},{24,28},{28,32},{32,36}... | collective-permute-start | bytes 3932168 | tf_op jit(solution)/shard_map/ppermute | solution.py:414
  87.7 55.0 %all-to-all-start.1 = ((bf16[32,56,8,128]{3,2,1,0:T(8,128)(2,1)}), bf16[32,56,8,128]{3,2,1,0:T(8,128)(2,1)}, u32[]{:S(2)}, u32[]{:S(2)}) async-start(bf16[32,56,8,128]{3,2,1,0:T(8,128)(2,1)} %gather_pieces.1), calls=%async_computation.1 | async-start | bytes 7340032 | tf_op jit(solution)/shard_map/all_to_all | solution.py:420
  96.7 2.0 %copy-start.7 = (f32[512,1792]{1,0:T(8,128)S(1)}, f32[512,1792]{1,0:T(8,128)}, u32[]{:S(2)}) copy-start(f32[512,1792]{1,0:T(8,128)} %copy-done.6) | copy-start | bytes 11010052
  98.8 1.1 copy-start.9

commit v4 on v3

--- a/solution.py
+++ b/solution.py
@@ -15,9 +15,10 @@
 PIECE = 8
 EDGE = 256
 FORWARD = 5
+HALVES = 2
 LOG2E = 1.4426950408889634
 NEG = -1e30
-VMEM_LIMIT = 24 << 20
+VMEM_LIMIT = 40 << 20
 BF = jnp.bfloat16
 F32 = jnp.float32
 ANY = pl.BlockSpec(memory_space=pl.ANY)
@@ -132,31 +133,69 @@
     )
 
 
-def gather_kernel(wanted, group, rows_ref, store_ref, out_ref):
-    first = pl.program_id(0) * group
-
-    @pl.loop(0, group)
-    def _(device):
-        base = (first + device) * wanted
-        for request in range(wanted):
-            out_ref[device, request] = store_ref[rows_ref[base + request]]
-
-
-def gather(rows, store, devices, wanted):
-    group = 4
-    return pl.pallas_call(
-        functools.partial(gather_kernel, wanted, group),
+def gather_kernel(
+    blocks, heads, wanted, store_ref, out_ref, ids, rows_v, rows_s, store, stage, ids_sem, sems, out_sems
+):
+    devices, stride = store_ref.shape[:2]
+    parts = sems.shape[0]
+    groups = out_sems.shape[0]
+    size = devices // groups
+    ids_load = pltpu.make_async_copy(store_ref.at[:, stride - 1], ids, ids_sem.at[0])
+    ids_load.start()
+    loads, stores = [], []
+    for part in range(parts):
+        span = pl.ds(part * (devices // parts), devices // parts)
+        loads.append(pltpu.make_async_copy(store_ref.at[span], store.at[span], sems.at[part]))
+    for group in range(groups):
+        span = pl.ds(group * size, size)
+        stores.append(pltpu.make_async_copy(stage.at[span], out_ref.at[span], out_sems.at[group]))
+    for load in loads:
+        load.start()
+    ids_load.wait()
+    row = lax.broadcasted_iota(jnp.int32, (devices, PIECE, DH), 1)
+    block = jnp.sum(jnp.where(row == 0, ids[...].astype(F32), 0.0), axis=1).astype(jnp.int32)
+    lane = lax.broadcasted_iota(jnp.int32, (devices, DH), 1)
+    head = lane // TOPK % heads
+    rows_v[...] = block // blocks * stride + block % blocks * heads + head
+    rows_copy = pltpu.make_async_copy(rows_v, rows_s, ids_sem.at[1])
+    rows_copy.start()
+    rows_copy.wait()
+    for load in loads:
+        load.wait()
+    flat = store.reshape(devices * stride, PIECE, DH)
+    for group in range(groups):
+
+        @pl.loop(group * size, (group + 1) * size)
+        def _(device):
+            for request in range(wanted):
+                stage[device, request] = flat[rows_s[device, request]]
+
+        stores[group].start()
+    for store_copy in stores:
+        store_copy.wait()
+
+
+def gather(store, blocks, heads, wanted):
+    devices = store.shape[0]
+    return pl.pallas_call(
+        functools.partial(gather_kernel, blocks, heads, wanted),
         out_shape=pltpu.HBM((devices, wanted, PIECE, DH), BF),
-        grid_spec=pltpu.PrefetchScalarGridSpec(
-            num_scalar_prefetch=1,
-            grid=(devices // group,),
-            in_specs=[pl.BlockSpec(store.shape, lambda i, rows: (0, 0, 0))],
-            out_specs=pl.BlockSpec((group, wanted, PIECE, DH), lambda i, rows: (i, 0, 0, 0)),
-        ),
+        in_specs=[ANY],
+        out_specs=ANY,
+        scratch_shapes=[
+            pltpu.VMEM((devices, PIECE, DH), BF),
+            pltpu.VMEM((devices, DH), jnp.int32),
+            pltpu.SMEM((devices, DH), jnp.int32),
+            pltpu.VMEM(store.shape, BF),
+            pltpu.VMEM((devices, wanted, PIECE, DH), BF),
+            pltpu.SemaphoreType.DMA((2,)),
+            pltpu.SemaphoreType.DMA((4,)),
+            pltpu.SemaphoreType.DMA((8,)),
+        ],
         compiler_params=params(),
         cost_estimate=cost(6),
         name="gather_pieces",
-    )(rows, store)
+    )(in_hbm(store))
 
 
 def dot_t(a, b):
@@ -227,21 +266,21 @@
         in_specs=[WHOLE] * 3,
         out_specs=(WHOLE,) * 3,
         compiler_params=params(),
-        cost_estimate=cost(20),
+        cost_estimate=cost(1),
         name="own_attention",
     )(queries, keys, values)
 
 
-def edge_kernel(scale, q_heads, k_heads, v_heads, tail, q_ref, k_ref, v_ref, out_ref, lse_ref):
+def edge_part(scale, slots, tail, q_ref, k_ref, v_ref, out_ref, lse_ref):
     lower = triangle()
     c = scale * LOG2E
     lanes = lax.broadcasted_iota(jnp.int32, (EDGE, DH), 1)
-    count = len(q_heads)
+    count = len(slots)
     lse_ref[...] = jnp.zeros_like(lse_ref)
-    for slot in range(count):
-        q_cols = pl.ds(q_heads[slot] * DH, DH)
-        k_cols = pl.ds(k_heads[slot] * DH, DH)
-        v_cols = pl.ds(v_heads[slot] * DH, DH)
+    for slot, (q_head, k_head, v_head) in enumerate(slots):
+        q_cols = pl.ds(q_head * DH, DH)
+        k_cols = pl.ds(k_head * DH, DH)
+        v_cols = pl.ds(v_head * DH, DH)
         for i in range(WIN // EDGE):
             rows = pl.ds(i * EDGE, EDGE)
             seen = pl.ds(tail + i * EDGE, WIN - i * EDGE)
@@ -265,17 +304,30 @@
     out_ref[:, pl.ds(count * DH, DH)] = packed.astype(BF)
 
 
-def edge_attention(queries, keys, values, q_heads, k_heads, v_heads, tail, scale, micros, name):
-    return pl.pallas_call(
-        functools.partial(edge_kernel, scale, q_heads, k_heads, v_heads, tail),
-        out_shape=jax.ShapeDtypeStruct((WIN, (len(q_heads) + 1) * DH), BF),
-        in_specs=[WHOLE] * 3,
-        out_specs=WHOLE,
+def edge_kernel(
+    scale, heads, far_q_ref, near_kv_ref, q_ref, k_ref, v_ref, far_ref, near_ref, lse_ref
+):
+    far = [(head - FORWARD, head, head) for head in range(FORWARD, heads)]
+    near = [(head, head, FORWARD + head) for head in range(FORWARD)]
+    tail = k_ref.shape[0] - WIN
+    edge_part(scale, far, tail, far_q_ref, k_ref, v_ref, far_ref, lse_ref)
+    edge_part(scale, near, 0, q_ref, near_kv_ref, near_kv_ref, near_ref, lse_ref)
+
+
+def edge_attention(far_q, near_kv, queries, keys, values, heads, scale):
+    return pl.pallas_call(
+        functools.partial(edge_kernel, scale, heads),
+        out_shape=(
+            jax.ShapeDtypeStruct((WIN, (heads - FORWARD + 1) * DH), BF),
+            jax.ShapeDtypeStruct((WIN, (FORWARD + 1) * DH), BF),
+        ),
+        in_specs=[WHOLE] * 5,
+        out_specs=(WHOLE,) * 2,
         scratch_shapes=[pltpu.VMEM((WIN, DH), F32)],
         compiler_params=params(),
-        cost_estimate=cost(micros),
-        name=name,
-    )(queries, keys, values)
+        cost_estimate=cost(60),
+        name="edge_attention",
+    )(far_q, near_kv, queries, keys, values)
 
 
 def unpacked(stat, count):
@@ -319,46 +371,74 @@
     )(first, low, lse, near, far, in_hbm(local))
 
 
-def final_kernel(scale, heads, gate_ref, q_ref, kv_ref, local_ref, out_ref):
+def final_kernel(
+    scale, heads, gate_ref, q_hbm, kv_hbm, local_hbm, out_hbm, q_ref, kv_ref, local_ref, out_ref, sems, out_sems
+):
     c = scale * LOG2E
     pieces = MB // PIECE
-    for head in range(heads):
-        cols = pl.ds(head * DH, DH)
-        mine = pl.ds(head * TOPK, TOPK)
-        keys = kv_ref[0:pieces, mine].astype(F32).reshape(TOPK * MB, DH).astype(BF)
-        values = kv_ref[pieces : 2 * pieces, mine].astype(F32).reshape(TOPK * MB, DH).astype(BF)
-        s = dot_t(q_ref[:, cols], keys)
-        top = jnp.max(s, axis=1, keepdims=True)
-        p = jnp.exp2((s - top) * c).astype(BF)
-        acc = dot(p, with_ones(values))
-        gate = gate_ref[head]
-        remote = acc[:, :DH] * (gate / acc[:, DH:])
-        local = local_ref[:, cols].astype(F32)
-        out_ref[:, cols] = (remote + (1.0 - gate) * local).astype(BF)
+    blocks = q_hbm.shape[0] // QB
+    step = heads // HALVES
+    chunks = [(block, half) for block in range(blocks) for half in range(HALVES)]
+    loads, stores = [], []
+    for index, (block, half) in enumerate(chunks):
+        area = (pl.ds(block * QB, QB), pl.ds(half * step * DH, step * DH))
+        mine = (slice(None), pl.ds((block * heads + half * step) * TOPK, step * TOPK))
+        loads.append(
+            [
+                pltpu.make_async_copy(source.at[where], target.at[where], sems.at[index, kind])
+                for kind, (source, target, where) in enumerate(
+                    ((kv_hbm, kv_ref, mine), (q_hbm, q_ref, area), (local_hbm, local_ref, area))
+                )
+            ]
+        )
+        stores.append(pltpu.make_async_copy(out_ref.at[area], out_hbm.at[area], out_sems.at[index]))
+    for index in range(2):
+        for load in loads[index]:
+            load.start()
+    for index, (block, half) in enumerate(chunks):
+        for load in loads[index]:
+            load.wait()
+        if index + 2 < len(chunks):
+            for load in loads[index + 2]:
+                load.start()
+        rows = pl.ds(block * QB, QB)
+        for head in range(half * step, (half + 1) * step):
+            cols = pl.ds(head * DH, DH)
+            mine = pl.ds((block * heads + head) * TOPK, TOPK)
+            keys = kv_ref[0:pieces, mine].astype(F32).reshape(TOPK * MB, DH).astype(BF)
+            values = kv_ref[pieces : 2 * pieces, mine].astype(F32).reshape(TOPK * MB, DH).astype(BF)
+            s = dot_t(q_ref[rows, cols], keys)
+            top = jnp.max(s, axis=1, keepdims=True)
+            p = jnp.exp2((s - top) * c).astype(BF)
+            acc = dot(p, with_ones(values))
+            gate = gate_ref[head]
+            remote = acc[:, :DH] * (gate / acc[:, DH:])
+            local = local_ref[rows, cols].astype(F32)
+            out_ref[rows, cols] = (remote + (1.0 - gate) * local).astype(BF)
+        stores[index].start()
+    for store in stores:
+        store.wait()
 
 
 def final_attention(gate, queries, kv, local, heads, scale):
-    tokens, width = queries.shape
-    rows = 256
-    per = QB // rows
-    band = pl.BlockSpec((rows, width), lambda i, *_: (i, 0))
+    chunks = queries.shape[0] // QB * HALVES
     return pl.pallas_call(
         functools.partial(final_kernel, scale, heads),
-        out_shape=jax.ShapeDtypeStruct(queries.shape, BF),
-        grid_spec=pltpu.PrefetchScalarGridSpec(
-            num_scalar_prefetch=1,
-            grid=(tokens // rows,),
-            in_specs=[
-                band,
-                pl.BlockSpec((kv.shape[0], heads * TOPK, PIECE, DH), lambda i, *_: (0, i // per, 0, 0)),
-                band,
-            ],
-            out_specs=band,
-        ),
+        out_shape=pltpu.HBM(queries.shape, BF),
+        in_specs=[SMALL, ANY, ANY, ANY],
+        out_specs=ANY,
+        scratch_shapes=[
+            pltpu.VMEM(queries.shape, BF),
+            pltpu.VMEM(kv.shape, BF),
+            pltpu.VMEM(queries.shape, BF),
+            pltpu.VMEM(queries.shape, BF),
+            pltpu.SemaphoreType.DMA((chunks, 3)),
+            pltpu.SemaphoreType.DMA((chunks,)),
+        ],
         compiler_params=params(),
         cost_estimate=cost(7),
         name="final_attention",
-    )(gate, queries, kv, local)
+    )(gate, in_hbm(queries), in_hbm(kv), in_hbm(local))
 
 
 def body(queries, token_keys, token_values, mem_keys, mem_values, retrieved, gate_bias):
@@ -369,8 +449,6 @@
     blocks = mem_keys.shape[0] // MB
     q_blocks = tokens // QB
     wanted = q_blocks * heads * TOPK
-    far_heads = list(range(FORWARD, heads))
-    near_heads = list(range(FORWARD))
     upward = [(i, i + 1) for i in range(devices - 1)]
     downward = [(i, i - 1) for i in range(1, devices)]
     back_q, ahead_kv = edges(queries, token_keys, token_values)
@@ -384,43 +462,18 @@
     gate_share = 1.0 / (1.0 + jnp.exp(-gate_bias))
     first = lax.axis_index("seq").reshape(1).astype(jnp.int32)
     low, lse, local = own_attention(queries, token_keys, token_values, heads, scale)
-    far_part = edge_attention(
-        far_q,
-        token_keys,
-        token_values,
-        list(range(len(far_heads))),
-        far_heads,
-        far_heads,
-        tokens - WIN,
-        scale,
-        60,
-        "far_attention",
-    )
-    near = edge_attention(
-        queries,
-        near_kv,
-        near_kv,
-        near_heads,
-        near_heads,
-        [FORWARD + head for head in near_heads],
-        0,
-        scale,
-        60,
-        "near_attention",
+    far_part, near = edge_attention(
+        far_q, near_kv, queries, token_keys, token_values, heads, scale
     )
     store, low, lse, local, far_part, near = lax.optimization_barrier(
         (store, low, lse, local, far_part, near)
     )
     far = lax.ppermute(far_part, "seq", upward)
-    all_ids = store[:, blocks * heads, 0, :wanted].astype(jnp.int32)
-    stride = blocks * heads + 1
-    request_head = jnp.arange(wanted, dtype=jnp.int32) // TOPK % heads
-    rows = (all_ids // blocks) * stride + (all_ids % blocks) * heads + request_head[None, :]
-    pieces = gather(rows.reshape(-1), store.reshape(devices * stride, PIECE, DH), devices, wanted)
+    pieces = gather(store, blocks, heads, wanted)
     kv = lax.all_to_all(pieces, "seq", split_axis=0, concat_axis=0, tiled=True)
     local = merge(first, low, lse, near, far, local, heads)
     kv, local = lax.optimization_barrier((kv, local))
-    return final_attention(gate_share, in_hbm(queries), in_hbm(kv), in_hbm(local), heads, scale)
+    return final_attention(gate_share, queries, kv, local, heads, scale)
 
 
 def solution(mesh):

time: 153 us -> 141 us (0.922)
  waiting for transfers between devices: 65.4 us -> 57.4 us
  starting transfers between devices: 28.1 us -> 24.1 us
    ppermute x1, waiting for transfers between devices: 25.8 us -> 0.01 us  [body(): near_kv = lax.ppermute(ahead_kv, 'seq', upward)]
    all_to_all x1, waiting for transfers between devices: 0.01 us -> 15.3 us  [body(): store = lax.all_to_all(sent, 'seq', split_axis=0, concat_axis=0, tiled=True)]
    pallas_call x1, Pallas kernels: 14.6 us -> 17.9 us  [own_attention(): pl.pallas_call(functools.partial(own_kernel, scale, heads), out_shape=(ja...]
    pallas_call x4 -> x3, Pallas kernels: 24.8 us -> 21.9 us  [the longest x1 8.66 us: final_attention(): pl.pallas_call(functools.partial(final_kernel, scale, heads), out_shape=p...]
    ppermute x1, starting transfers between devices: 4.38 us -> 1.91 us  [body(): far = lax.ppermute(far_part, 'seq', upward)]
    ppermute x1, waiting for transfers between devices: 0.01 us -> 2.37 us  [body(): far_q = lax.ppermute(back_q, 'seq', downward)]
    unnamed x24 -> x18, local copies, waits for them, and re-layouts: 10.2 us -> 9.93 us
  transfers between devices with their start and end apart: 5 -> 5, of which waited for: 2 -> 4; matrix products, arithmetic and copies ran while one was open for 1% -> 0% of each run, Pallas kernels for 23% -> 27%
where the time goes in v4:
time: 141 us
  waiting for transfers between devices  57.4 us (41%)
  Pallas kernels  48.8 us (35%)
  starting transfers between devices  24.1 us (17%)
  local copies, waits for them, and re-layouts  10.2 us (7%)
    all_to_all x1, waiting for transfers between devices, body(): kv = lax.all_to_all(pieces, 'seq', split_axis=0, concat_axis=0, tiled=True)  38.8 us
    pallas_call x1, Pallas kernels, own_attention(): pl.pallas_call(functools.partial(own_kernel, scale, heads), out_shape=(ja...  17.9 us
    all_to_all x1, waiting for transfers between devices, body(): store = lax.all_to_all(sent, 'seq', split_axis=0, concat_axis=0, tiled=True)  15.3 us
    unnamed x18, local copies, waits for them, and re-layouts  9.93 us
    pallas_call x1, Pallas kernels, final_attention(): pl.pallas_call(functools.partial(final_kernel, scale, heads), out_shape=p...  8.66 us
    all_to_all x1, starting transfers between devices, body(): kv = lax.all_to_all(pieces, 'seq', split_axis=0, concat_axis=0, tiled=True)  7.98 us
    all_to_all x1, starting transfers between devices, body(): store = lax.all_to_all(sent, 'seq', split_axis=0, concat_axis=0, tiled=True)  7.7 us
    pallas_call x1, Pallas kernels, edge_attention(): pl.pallas_call(functools.partial(edge_kernel, scale, heads), out_shape=(j...  7.64 us
  transfers between devices with their start and end apart: 5, of which 4 were waited for; matrix products, arithmetic and copies ran while one was open for 0% of the time, Pallas kernels for 27%

profile of v4, /device:TPU:1, one launch (start us, length us, event | category | flops | bytes accessed | tf_op | source)
XLA Modules:
  0.0 140.8 jit_solution(10686413925535422382)
XLA Ops:
  0.0 2.7 %cut_edges.1 = (bf16[512,1152]{1,0:T(8,128)(2,1)}, bf16[512,1280]{1,0:T(8,128)(2,1)S(1)}) custom-call(bf16[1024,1792]{1,0:T(8,128)(2,1)} %q_hbm.1, bf16[1024,1792]{1,0:T(8,128)(2,1)} %k_ref.5, bf16[1024,1792]{1,0:T(8,128)(2,1)} %v_ref.5), custom_call_target="tpu_custom_call" | custom-call | flops 2000000000 | tf_op jit(solution)/shard_map/cut_edges/pallas_call | solution.py:69
  2.7 4.6 %collective-permute-start.1 = (bf16[512,1280]{1,0:T(8,128)(2,1)S(1)}, bf16[512,1280]{1,0:T(8,128)(2,1)S(1)}, u32[]{:S(2)}, u32[]{:S(2)}) collective-permute-start(bf16[512,1280]{1,0:T(8,128)(2,1)S(1)} %get-tuple-element.38), channel_id=1, source_target_pairs={{0,4},{4,8},{8,12},{12,16},{16,20},{20,24},{24,28},{28,32},{32,36}... | collective-permute-start | bytes 3932168 | tf_op jit(solution)/shard_map/ppermute | solution.py:456
  7.3 1.9 %collective-permute-start = (bf16[512,1152]{1,0:T(8,128)(2,1)}, bf16[512,1152]{1,0:T(8,128)(2,1)}, u32[]{:S(2)}, u32[]{:S(2)}) collective-permute-start(bf16[512,1152]{1,0:T(8,128)(2,1)} %get-tuple-element.33), channel_id=1, source_target_pairs={{4,0},{8,4},{12,8},{16,12},{20,16},{24,20},{28,24},{32,28},{36,32}... | collective-permute-start | bytes 3538952 | tf_op jit(solution)/shard_map/ppermute | solution.py:455
  9.3 0.1 copy.10
  9.4 0.1 convert_element_type.7
  9.5 3.1 %pack_pieces.1 = bf16[32,57,8,128]{3,2,1,0:T(8,128)(2,1)} custom-call(bf16[64,14,8,128]{3,2,1,0:T(8,128)(2,1)} %bitcast.9, bf16[64,14,8,128]{3,2,1,0:T(8,128)(2,1)} %bitcast.10, bf16[32,1,8,128]{3,2,1,0:T(8,128)(2,1)S(1)} %broadcast_in_dim.4.ids_ref), custom_call_target="tpu_custom_call" | custom-call | flops 2000000000 | tf_op jit(solution)/shard_map/pack_pieces/pallas_call | solution.py:116
  12.6 7.7 %all-to-all-start = ((bf16[32,57,8,128]{3,2,1,0:T(8,128)(2,1)}), bf16[32,57,8,128]{3,2,1,0:T(8,128)(2,1)}, u32[]{:S(2)}, u32[]{:S(2)}) async-start(bf16[32,57,8,128]{3,2,1,0:T(8,128)(2,1)} %pack_pieces.1), calls=%async_computation | async-start | bytes 7471104 | tf_op jit(solution)/shard_map/all_to_all | solution.py:461
  20.4 2.0 %copy-done.1 = bf16[1024,1792]{1,0:T(8,128)(2,1)S(1)} copy-done((bf16[1024,1792]{1,0:T(8,128)(2,1)S(1)}, bf16[1024,1792]{1,0:T(8,128)(2,1)}, u32[]{:S(2)}) %copy-start.1) | copy-done | bytes 3670040
  22.4 17.9 %own_attention.1 = (f32[512,1792]{1,0:T(8,128)S(1)}, f32[512,128]{1,0:T(8,128)S(1)}, bf16[1024,1792]{1,0:T(8,128)(2,1)S(1)}) custom-call(bf16[1024,1792]{1,0:T(8,128)(2,1)S(1)} %copy-done.1, bf16[1024,1792]{1,0:T(8,128)(2,1)} %k_ref.5, bf16[1024,1792]{1,0:T(8,128)(2,1)} %v_ref.5), custom_call_target="tpu_custom_call" | custom-call | flops 1000000000 | tf_op jit(solution)/shard_map/own_attention/pallas_call | solution.py:259
  40.3 1.9 %copy-done.2 = f32[512,1792]{1,0:T(8,128)} copy-done((f32[512,1792]{1,0:T(8,128)}, f32[512,1792]{1,0:T(8,128)S(1)}, u32[]{:S(2)}) %copy-start.2) | copy-done | bytes 3670040
  42.2 1.9 %copy-done.4 = bf16[1024,1792]{1,0:T(8,128)(2,1)} copy-done((bf16[1024,1792]{1,0:T(8,128)(2,1)}, bf16[1024,1792]{1,0:T(8,128)(2,1)S(1)}, u32[]{:S(2)}) %copy-start.4) | copy-done | bytes 3670040
  44.1 2.4 %collective-permute-done.far_q_ref = bf16[512,1152]{1,0:T(8,128)(2,1)} collective-permute-done((bf16[512,1152]{1,0:T(8,128)(2,1)}, bf16[512,1152]{1,0:T(8,128)(2,1)}, u32[]{:S(2)}, u32[]{:S(2)}) %collective-permute-start) | collective-permute-done | bytes 1179680 | tf_op jit(solution)/shard_map/ppermute | solution.py:455
  46.5 7.6 %edge_attention.1 = (bf16[512,1280]{1,0:T(8,128)(2,1)S(1)}, bf16[512,768]{1,0:T(8,128)(2,1)S(1)}) custom-call(bf16[512,1152]{1,0:T(8,128)(2,1)} %collective-permute-done.far_q_ref, bf16[512,1280]{1,0:T(8,128)(2,1)S(1)} %collective-permute-done.1.near_kv_ref, bf16[1024,1792]{1,0:T(8,128)(2,1)S(1)} %copy-done.1, bf16[1024,1792]{1,0:T(8,128)(2,1)S(1)} %copy-done, ...), custom_call_target="tpu_custom_call" | custom-call | flops 60000002048 | tf_op jit(solution)/shard_map/edge_attention/pallas_call | solution.py:318
  54.2 0.9 copy-done.5
  55.0 15.3 %all-to-all-done.store_ref = bf16[32,57,8,128]{3,2,1,0:T(8,128)(2,1)} async-done(((bf16[32,57,8,128]{3,2,1,0:T(8,128)(2,1)}), bf16[32,57,8,128]{3,2,1,0:T(8,128)(2,1)}, u32[]{:S(2)}, u32[]{:S(2)}) %all-to-all-start) | async-done | bytes 3735584 | tf_op jit(solution)/shard_map/all_to_all | solution.py:461
  70.3 1.9 %collective-permute-start.2 = (bf16[512,1280]{1,0:T(8,128)(2,1)S(1)}, bf16[512,1280]{1,0:T(8,128)(2,1)S(1)}, u32[]{:S(2)}, u32[]{:S(2)}) collective-permute-start(bf16[512,1280]{1,0:T(8,128)(2,1)S(1)} %get-tuple-element.45), channel_id=1, source_target_pairs={{0,4},{4,8},{8,12},{12,16},{16,20},{20,24},{24,28},{28,32},{32,36}... | collective-permute-start | bytes 3932168 | tf_op jit(solution)/shard_map/ppermute | solution.py:471
  72.3 5.6 %gather_pieces.1 = bf16[32,56,8,128]{3,2,1,0:T(8,128)(2,1)} custom-call(bf16[32,57,8,128]{3,2,1,0:T(8,128)(2,1)} %all-to-all-done.store_ref), custom_call_target="tpu_custom_call" | custom-call | flops 6000000000 | tf_op jit(solution)/shard_map/gather_pieces/pallas_call | solution.py:180
  77.9 8.0 %all-to-all-start.1 = ((bf16[32,56,8,128]{3,2,1,0:T(8,128)(2,1)}), bf16[32,56,8,128]{3,2,1,0:T(8,128)(2,1)}, u32[]{:S(2)}, u32[]{:S(2)}) async-start(bf16[32,56,8,128]{3,2,1,0:T(8,128)(2,1)} %gather_pieces.1), calls=%async_computation.1 | async-start | bytes 7340032 | tf_op jit(solution)/shard_map/all_to_all | solution.py:473
  85.9 0.9 collective-permute-done.2.far_ref
  86.8 2.0 %copy-done.3 = f32[512,1792]{1,0:T(8,128)S(1)} copy-done((f32[512,1792]{1,0:T(8,128)S(1)}, f32[512,1792]{1,0:T(8,128)}, u32[]{:S(2)}) %copy-start.3) | copy-done | bytes 3670040
  88.8 1.1 copy-done.6
  90.0 3.2 %merge_local.1.local_hbm = bf16[1024,1792]{1,0:T(8,128)(2,1)} custom-call(s32[1]{0:T(128)} %bitcast.5.first_ref, f32[512,1792]{1,0:T(8,128)S(1)} %copy-done.3, f32[512,128]{1,0:T(8,128)S(1)} %get-tuple-element.43.lse_ref, bf16[512,768]{1,0:T(8,128)(2,1)S(1)} %copy-done.6, ...), custom_call_target="tpu_custom_call", output_to_operand_aliasing={{}: (5, {})} | custom-call | flops 60000002048 | tf_op jit(solution)/shard_map/merge_local/pallas_call | solution.py:361
  93.1 38.8 %all-to-all-done.1.kv_hbm = bf16[32,56,8,128]{3,2,1,0:T(8,128)(2,1)} async-done(((bf16[32,56,8,128]{3,2,1,0:T(8,128)(2,1)}), bf16[32,56,8,128]{3,2,1,0:T(8,128)(2,1)}, u32[]{:S(2)}, u32[]{:S(2)}) %all-to-all-start.1) | async-done | bytes 3670048 | tf_op jit(solution)/shard_map/all_to_all | solution.py:473
  132.0 8.7 %final_attention.1 = bf16[1024,1792]{1,0:T(8,128)(2,1)} custom-call(f32[14]{0:T(128)S(1)} %add_divide_fusion.gate_ref, bf16[1024,1792]{1,0:T(8,128)(2,1)} %q_hbm.1, bf16[32,56,8,128]{3,2,1,0:T(8,128)(2,1)} %all-to-all-done.1.kv_hbm, bf16[1024,1792]{1,0:T(8,128)(2,1)} %merge_local.1.local_hbm), custom_call_target="tpu_custom_call" | custom-call | flops 7000000000 | tf_op jit(solution)/shard_map/final_attention/pallas_call | solution.py:425
  (17 shorter events, 0.1 us)
Async XLA Ops:
  0.0 9.2 %copy-start.7 = (s32[2,14,2]{1,2,0:T(2,128)S(1)}, s32[2,14,2]{1,2,0:T(2,128)}, u32[]{:S(2)}) copy-start(s32[2,14,2]{1,2,0:T(2,128)} %param.14) | copy-start | bytes 676
  2.7 43.8 %collective-permute-start.1 = (bf16[512,1280]{1,0:T(8,128)(2,1)S(1)}, bf16[512,1280]{1,0:T(8,128)(2,1)S(1)}, u32[]{:S(2)}, u32[]{:S(2)}) collective-permute-start(bf16[512,1280]{1,0:T(8,128)(2,1)S(1)} %get-tuple-element.38), channel_id=1, source_target_pairs={{0,4},{4,8},{8,12},{12,16},{16,20},{20,24},{24,28},{28,32},{32,36}... | collective-permute-start | bytes 3932168 | tf_op jit(solution)/shard_map/ppermute | solution.py:456
  7.3 39.2 %collective-permute-start = (bf16[512,1152]{1,0:T(8,128)(2,1)}, bf16[512,1152]{1,0:T(8,128)(2,1)}, u32[]{:S(2)}, u32[]{:S(2)}) collective-permute-start(bf16[512,1152]{1,0:T(8,128)(2,1)} %get-tuple-element.33), channel_id=1, source_target_pairs={{4,0},{8,4},{12,8},{16,12},{20,16},{24,20},{28,24},{32,28},{36,32}... | collective-permute-start | bytes 3538952 | tf_op jit(solution)/shard_map/ppermute | solution.py:455
  12.6 57.7 %all-to-all-start = ((bf16[32,57,8,128]{3,2,1,0:T(8,128)(2,1)}), bf16[32,57,8,128]{3,2,1,0:T(8,128)(2,1)}, u32[]{:S(2)}, u32[]{:S(2)}) async-start(bf16[32,57,8,128]{3,2,1,0:T(8,128)(2,1)} %pack_pieces.1), calls=%async_computation | async-start | bytes 7471104 | tf_op jit(solution)/shard_map/all_to_all | solution.py:461
  20.4 2.0 %copy-start.1 = (bf16[1024,1792]{1,0:T(8,128)(2,1)S(1)}, bf16[1024,1792]{1,0:T(8,128)(2,1)}, u32[]{:S(2)}) copy-start(bf16[1024,1792]{1,0:T(8,128)(2,1)} %q_hbm.1) | copy-start | bytes 11010052
  22.4 24.1 %copy-start = (bf16[1024,1792]{1,0:T(8,128)(2,1)S(1)}, bf16[1024,1792]{1,0:T(8,128)(2,1)}, u32[]{:S(2)}) copy-start(bf16[1024,1792]{1,0:T(8,128)(2,1)} %k_ref.5) | copy-start | bytes 11010052
  40.3 1.9 %copy-start.2 = (f32[512,1792]{1,0:T(8,128)}, f32[512,1792]{1,0:T(8,128)S(1)}, u32[]{:S(2)}) copy-start(f32[512,1792]{1,0:T(8,128)S(1)} %get-tuple-element.42.low_ref) | copy-start | bytes 11010052
  42.2 1.9 %copy-start.4 = (bf16[1024,1792]{1,0:T(8,128)(2,1)}, bf16[1024,1792]{1,0:T(8,128)(2,1)S(1)}, u32[]{:S(2)}) copy-start(bf16[1024,1792]{1,0:T(8,128)(2,1)S(1)} %get-tuple-element.46.into_ref) | copy-start | bytes 11010052
  44.1 28.1 %copy-start.8 = (f32[14]{0:T(128)S(1)}, f32[14]{0:T(128)}, u32[]{:S(2)}) copy-start(f32[14]{0:T(128)} %param.15) | copy-start | bytes 172
  54.2 0.9 copy-start.5
  70.3 16.4 %collective-permute-start.2 = (bf16[512,1280]{1,0:T(8,128)(2,1)S(1)}, bf16[512,1280]{1,0:T(8,128)(2,1)S(1)}, u32[]{:S(2)}, u32[]{:S(2)}) collective-permute-start(bf16[512,1280]{1,0:T(8,128)(2,1)S(1)} %get-tuple-element.45), channel_id=1, source_target_pairs={{0,4},{4,8},{8,12},{12,16},{16,20},{20,24},{24,28},{28,32},{32,36}... | collective-permute-start | bytes 3932168 | tf_op jit(solution)/shard_map/ppermute | solution.py:471
  77.9 54.1 %all-to-all-start.1 = ((bf16[32,56,8,128]{3,2,1,0:T(8,128)(2,1)}), bf16[32,56,8,128]{3,2,1,0:T(8,128)(2,1)}, u32[]{:S(2)}, u32[]{:S(2)}) async-start(bf16[32,56,8,128]{3,2,1,0:T(8,128)(2,1)} %gather_pieces.1), calls=%async_computation.1 | async-start | bytes 7340032 | tf_op jit(solution)/shard_map/all_to_all | solution.py:473
  86.8 2.0 %copy-start.3 = (f32[512,1792]{1,0:T(8,128)S(1)}, f32[512,1792]{1,0:T(8,128)}, u32[]{:S(2)}) copy-start(f32[512,1792]{1,0:T(8,128)} %copy-done.2) | copy-start | bytes 11010052
  88.8 1.1 copy-start.6

commit v5 on v4

--- a/solution.py
+++ b/solution.py
@@ -18,7 +18,6 @@
 HALVES = 2
 LOG2E = 1.4426950408889634
 NEG = -1e30
-VMEM_LIMIT = 40 << 20
 BF = jnp.bfloat16
 F32 = jnp.float32
 ANY = pl.BlockSpec(memory_space=pl.ANY)
@@ -26,8 +25,8 @@
 SMALL = pl.BlockSpec(memory_space=pltpu.SMEM)
 
 
-def params():
-    return pltpu.CompilerParams(vmem_limit_bytes=VMEM_LIMIT)
+def params(mebibytes):
+    return pltpu.CompilerParams(vmem_limit_bytes=mebibytes << 20)
 
 
 def cost(micros):
@@ -38,98 +37,97 @@
     return pltpu.with_memory_space_constraint(array, pltpu.HBM)
 
 
-def copy_all(copies):
-    for copy in copies:
-        copy.start()
-    for copy in copies:
-        copy.wait()
-
-
-def edges_kernel(q_ref, k_ref, v_ref, back_ref, ahead_ref, sems):
-    split = FORWARD * DH
-    tail = pl.ds(k_ref.shape[0] - WIN, WIN)
-    width = q_ref.shape[1] - split
-    copy_all(
-        [
-            pltpu.make_async_copy(
-                q_ref.at[pl.ds(0, WIN), pl.ds(split, width)], back_ref, sems.at[0]
-            ),
-            pltpu.make_async_copy(
-                k_ref.at[tail, pl.ds(0, split)], ahead_ref.at[:, pl.ds(0, split)], sems.at[1]
-            ),
-            pltpu.make_async_copy(
-                v_ref.at[tail, pl.ds(0, split)], ahead_ref.at[:, pl.ds(split, split)], sems.at[2]
-            ),
-        ]
-    )
-
-
-def edges(queries, keys, values):
-    split = FORWARD * DH
-    return pl.pallas_call(
-        edges_kernel,
-        out_shape=(
-            jax.ShapeDtypeStruct((WIN, queries.shape[1] - split), BF),
-            jax.ShapeDtypeStruct((WIN, 2 * split), BF),
-        ),
-        in_specs=[ANY] * 3,
-        out_specs=(WHOLE, WHOLE),
-        scratch_shapes=[pltpu.SemaphoreType.DMA((3,))],
-        compiler_params=params(),
-        cost_estimate=cost(2),
-        name="cut_edges",
-    )(in_hbm(queries), in_hbm(keys), in_hbm(values))
-
-
-def pack_kernel(blocks, heads, keys_ref, values_ref, ids_ref, out_ref, stage, in_sems, out_sems):
+def tiles(array):
+    rows, width = array.shape
+    return array.reshape(rows // PIECE, PIECE, width // DH, DH).transpose(0, 2, 1, 3)
+
+
+def prepare_kernel(
+    blocks,
+    heads,
+    keys_ref,
+    values_ref,
+    ids_ref,
+    q_ref,
+    k_ref,
+    v_ref,
+    sent_ref,
+    back_ref,
+    ahead_ref,
+    stage,
+    in_sems,
+    out_sems,
+    cut_sems,
+):
     pieces = MB // PIECE
     loads, stores = [], []
     for half, source in enumerate((keys_ref, values_ref)):
         for block in range(blocks):
             slot = len(loads)
             here = stage.at[pl.ds(slot * pieces, pieces)]
-            there = out_ref.at[pl.ds(half * pieces, pieces), pl.ds(block * heads, heads)]
+            there = sent_ref.at[pl.ds(half * pieces, pieces), pl.ds(block * heads, heads)]
             rows = pl.ds(block * pieces, pieces)
             loads.append(pltpu.make_async_copy(source.at[rows], here, in_sems.at[slot]))
             stores.append(pltpu.make_async_copy(here, there, out_sems.at[slot]))
     ids_store = pltpu.make_async_copy(
-        ids_ref, out_ref.at[:, pl.ds(blocks * heads, 1)], out_sems.at[2 * blocks]
-    )
+        ids_ref, sent_ref.at[:, pl.ds(blocks * heads, 1)], out_sems.at[2 * blocks]
+    )
+    split = FORWARD * DH
+    tail = pl.ds(k_ref.shape[0] - WIN, WIN)
+    cuts = [
+        pltpu.make_async_copy(
+            k_ref.at[tail, pl.ds(0, split)], ahead_ref.at[:, pl.ds(0, split)], cut_sems.at[0]
+        ),
+        pltpu.make_async_copy(
+            v_ref.at[tail, pl.ds(0, split)], ahead_ref.at[:, pl.ds(split, split)], cut_sems.at[1]
+        ),
+        pltpu.make_async_copy(
+            q_ref.at[pl.ds(0, WIN), pl.ds(split, q_ref.shape[1] - split)], back_ref, cut_sems.at[2]
+        ),
+    ]
     for load in loads:
         load.start()
+    for cut in cuts:
+        cut.start()
     ids_store.start()
     for load, store in zip(loads, stores):
         load.wait()
         store.start()
+    for cut in cuts:
+        cut.wait()
     for store in stores:
         store.wait()
     ids_store.wait()
 
 
-def tiles(array):
-    rows, width = array.shape
-    return array.reshape(rows // PIECE, PIECE, width // DH, DH).transpose(0, 2, 1, 3)
-
-
-def pack(mem_keys, mem_values, ids_tile, blocks, heads):
+def prepare(mem_keys, mem_values, ids_tile, queries, keys, values, blocks, heads):
     devices = 2 * MB // PIECE
-    return pl.pallas_call(
-        functools.partial(pack_kernel, blocks, heads),
-        out_shape=pltpu.HBM((devices, blocks * heads + 1, PIECE, DH), BF),
-        in_specs=[ANY, ANY, WHOLE],
-        out_specs=ANY,
+    split = FORWARD * DH
+    return pl.pallas_call(
+        functools.partial(prepare_kernel, blocks, heads),
+        out_shape=(
+            pltpu.HBM((devices, blocks * heads + 1, PIECE, DH), BF),
+            jax.ShapeDtypeStruct((WIN, queries.shape[1] - split), BF),
+            jax.ShapeDtypeStruct((WIN, 2 * split), BF),
+        ),
+        in_specs=[ANY, ANY, WHOLE, ANY, ANY, ANY],
+        out_specs=(ANY, WHOLE, WHOLE),
         scratch_shapes=[
             pltpu.VMEM((2 * blocks * MB // PIECE, heads, PIECE, DH), BF),
             pltpu.SemaphoreType.DMA((2 * blocks,)),
             pltpu.SemaphoreType.DMA((2 * blocks + 1,)),
+            pltpu.SemaphoreType.DMA((3,)),
         ],
-        compiler_params=params(),
+        compiler_params=params(8),
         cost_estimate=cost(2),
-        name="pack_pieces",
+        name="prepare",
     )(
         in_hbm(tiles(mem_keys)),
         in_hbm(tiles(mem_values)),
         jnp.broadcast_to(ids_tile, (devices, 1, PIECE, DH)),
+        in_hbm(queries),
+        in_hbm(keys),
+        in_hbm(values),
     )
 
 
@@ -192,7 +190,7 @@
             pltpu.SemaphoreType.DMA((4,)),
             pltpu.SemaphoreType.DMA((8,)),
         ],
-        compiler_params=params(),
+        compiler_params=params(16),
         cost_estimate=cost(6),
         name="gather_pieces",
     )(in_hbm(store))
@@ -265,7 +263,7 @@
         ),
         in_specs=[WHOLE] * 3,
         out_specs=(WHOLE,) * 3,
-        compiler_params=params(),
+        compiler_params=params(30),
         cost_estimate=cost(1),
         name="own_attention",
     )(queries, keys, values)
@@ -324,7 +322,7 @@
         in_specs=[WHOLE] * 5,
         out_specs=(WHOLE,) * 2,
         scratch_shapes=[pltpu.VMEM((WIN, DH), F32)],
-        compiler_params=params(),
+        compiler_params=params(24),
         cost_estimate=cost(60),
         name="edge_attention",
     )(far_q, near_kv, queries, keys, values)
@@ -365,7 +363,7 @@
         in_specs=[SMALL, whole(low), whole(lse), whole(near), whole(far), ANY],
         out_specs=pl.BlockSpec((WIN, width), lambda i: (0, 0)),
         input_output_aliases={5: 0},
-        compiler_params=params(),
+        compiler_params=params(16),
         cost_estimate=cost(60),
         name="merge_local",
     )(first, low, lse, near, far, in_hbm(local))
@@ -435,7 +433,7 @@
             pltpu.SemaphoreType.DMA((chunks, 3)),
             pltpu.SemaphoreType.DMA((chunks,)),
         ],
-        compiler_params=params(),
+        compiler_params=params(24),
         cost_estimate=cost(7),
         name="final_attention",
     )(gate, in_hbm(queries), in_hbm(kv), in_hbm(local))
@@ -451,13 +449,13 @@
     wanted = q_blocks * heads * TOPK
     upward = [(i, i + 1) for i in range(devices - 1)]
     downward = [(i, i - 1) for i in range(1, devices)]
-    back_q, ahead_kv = edges(queries, token_keys, token_values)
+    ids = retrieved.reshape(-1)
+    ids_tile = jnp.zeros((PIECE * DH,), BF).at[:wanted].set(ids.astype(BF)).reshape(PIECE, DH)
+    sent, back_q, ahead_kv = prepare(
+        mem_keys, mem_values, ids_tile, queries, token_keys, token_values, blocks, heads
+    )
     far_q = lax.ppermute(back_q, "seq", downward)
     near_kv = lax.ppermute(ahead_kv, "seq", upward)
-    ids = retrieved.reshape(-1)
-    ids_tile = jnp.zeros((PIECE * DH,), BF).at[:wanted].set(ids.astype(BF)).reshape(PIECE, DH)
-    ids_tile, _ = lax.optimization_barrier((ids_tile, back_q))
-    sent = pack(mem_keys, mem_values, ids_tile, blocks, heads)
     store = lax.all_to_all(sent, "seq", split_axis=0, concat_axis=0, tiled=True)
     gate_share = 1.0 / (1.0 + jnp.exp(-gate_bias))
     first = lax.axis_index("seq").reshape(1).astype(jnp.int32)

time: 141 us -> 148 us (1.050)
  waiting for transfers between devices: 57.4 us -> 63.9 us
  Pallas kernels: 48.8 us -> 44.1 us
  local copies, waits for them, and re-layouts: 10.2 us -> 14.2 us
    ppermute x1, waiting for transfers between devices: 2.37 us -> 24.2 us  [body(): far_q = lax.ppermute(back_q, 'seq', downward)]
    all_to_all x1, waiting for transfers between devices: 15.3 us -> 0.01 us  [body(): store = lax.all_to_all(sent, 'seq', split_axis=0, concat_axis=0, tiled=True)]
    unnamed x18 -> x22, local copies, waits for them, and re-layouts: 9.93 us -> 14 us
    pallas_call x1, Pallas kernels: 17.9 us -> 14.6 us  [own_attention(): pl.pallas_call(functools.partial(own_kernel, scale, heads), out_shape=(ja...]
    pallas_call x2 -> x1, Pallas kernels: 5.82 us -> 5.57 us  [prepare(): pl.pallas_call(functools.partial(prepare_kernel, blocks, heads), out_shap...]
  transfers between devices with their start and end apart: 5 -> 5, of which waited for: 4 -> 3; matrix products, arithmetic and copies ran while one was open for 0% -> 0% of each run, Pallas kernels for 27% -> 20%
where the time goes in v5:
time: 148 us; the launch traced here: 147 us
  waiting for transfers between devices  63.9 us (43%)
  Pallas kernels  44.1 us (30%)
  starting transfers between devices  24.1 us (16%)
  local copies, waits for them, and re-layouts  14.2 us (10%)
    all_to_all x1, waiting for transfers between devices, body(): kv = lax.all_to_all(pieces, 'seq', split_axis=0, concat_axis=0, tiled=True)  38.8 us
    ppermute x1, waiting for transfers between devices, body(): far_q = lax.ppermute(back_q, 'seq', downward)  24.2 us
    pallas_call x1, Pallas kernels, own_attention(): pl.pallas_call(functools.partial(own_kernel, scale, heads), out_shape=(ja...  14.6 us
    unnamed x22, local copies, waits for them, and re-layouts  14 us
    pallas_call x1, Pallas kernels, final_attention(): pl.pallas_call(functools.partial(final_kernel, scale, heads), out_shape=p...  8.66 us
    all_to_all x1, starting transfers between devices, body(): kv = lax.all_to_all(pieces, 'seq', split_axis=0, concat_axis=0, tiled=True)  7.95 us
    all_to_all x1, starting transfers between devices, body(): store = lax.all_to_all(sent, 'seq', split_axis=0, concat_axis=0, tiled=True)  7.7 us
    pallas_call x1, Pallas kernels, edge_attention(): pl.pallas_call(functools.partial(edge_kernel, scale, heads), out_shape=(j...  6.51 us
  transfers between devices with their start and end apart: 5, of which 3 were waited for; matrix products, arithmetic and copies ran while one was open for 0% of the time, Pallas kernels for 20%

profile of v5, /device:TPU:1, one launch (start us, length us, event | category | flops | bytes accessed | tf_op | source)
XLA Modules:
  0.0 147.4 jit_solution(8998368678397412109)
XLA Ops:
  0.0 0.7 convert_element_type.6
  0.8 0.1 convert_element_type.7
  0.9 5.6 %prepare.1 = (bf16[32,57,8,128]{3,2,1,0:T(8,128)(2,1)}, bf16[512,1152]{1,0:T(8,128)(2,1)}, bf16[512,1280]{1,0:T(8,128)(2,1)S(1)}) custom-call(bf16[64,14,8,128]{3,2,1,0:T(8,128)(2,1)} %bitcast.9, bf16[64,14,8,128]{3,2,1,0:T(8,128)(2,1)} %bitcast.10, bf16[32,1,8,128]{3,2,1,0:T(8,128)(2,1)S(1)} %broadcast_in_dim.4.ids_ref, bf16[1024,1792]{1,0:T(8,128)(2,1)} %q_hbm.1, ...), custom_call_target="tpu_custom_call" | custom-call | flops 2000000000 | tf_op jit(solution)/shard_map/prepare/pallas_call | solution.py:106
  6.5 4.6 %collective-permute-start.1 = (bf16[512,1280]{1,0:T(8,128)(2,1)S(1)}, bf16[512,1280]{1,0:T(8,128)(2,1)S(1)}, u32[]{:S(2)}, u32[]{:S(2)}) collective-permute-start(bf16[512,1280]{1,0:T(8,128)(2,1)S(1)} %get-tuple-element.38), channel_id=1, source_target_pairs={{0,4},{4,8},{8,12},{12,16},{16,20},{20,24},{24,28},{28,32},{32,36}... | collective-permute-start | bytes 3932168 | tf_op jit(solution)/shard_map/ppermute | solution.py:458
  11.1 1.9 %collective-permute-start = (bf16[512,1152]{1,0:T(8,128)(2,1)}, bf16[512,1152]{1,0:T(8,128)(2,1)}, u32[]{:S(2)}, u32[]{:S(2)}) collective-permute-start(bf16[512,1152]{1,0:T(8,128)(2,1)} %get-tuple-element.37), channel_id=1, source_target_pairs={{4,0},{8,4},{12,8},{16,12},{20,16},{24,20},{28,24},{32,28},{36,32}... | collective-permute-start | bytes 3538952 | tf_op jit(solution)/shard_map/ppermute | solution.py:457
  13.1 7.7 %all-to-all-start = ((bf16[32,57,8,128]{3,2,1,0:T(8,128)(2,1)}), bf16[32,57,8,128]{3,2,1,0:T(8,128)(2,1)}, u32[]{:S(2)}, u32[]{:S(2)}) async-start(bf16[32,57,8,128]{3,2,1,0:T(8,128)(2,1)} %get-tuple-element.33), calls=%async_computation | async-start | bytes 7471104 | tf_op jit(solution)/shard_map/all_to_all | solution.py:459
  20.8 2.0 %copy-done = bf16[1024,1792]{1,0:T(8,128)(2,1)S(1)} copy-done((bf16[1024,1792]{1,0:T(8,128)(2,1)S(1)}, bf16[1024,1792]{1,0:T(8,128)(2,1)}, u32[]{:S(2)}) %copy-start) | copy-done | bytes 3670040
  22.8 2.0 %copy-done.2 = bf16[1024,1792]{1,0:T(8,128)(2,1)S(1)} copy-done((bf16[1024,1792]{1,0:T(8,128)(2,1)S(1)}, bf16[1024,1792]{1,0:T(8,128)(2,1)}, u32[]{:S(2)}) %copy-start.2) | copy-done | bytes 3670040
  24.8 2.0 %copy-done.4 = bf16[1024,1792]{1,0:T(8,128)(2,1)S(1)} copy-done((bf16[1024,1792]{1,0:T(8,128)(2,1)S(1)}, bf16[1024,1792]{1,0:T(8,128)(2,1)}, u32[]{:S(2)}) %copy-start.4) | copy-done | bytes 3670040
  26.9 14.6 %own_attention.1 = (f32[512,1792]{1,0:T(8,128)S(1)}, f32[512,128]{1,0:T(8,128)S(1)}, bf16[1024,1792]{1,0:T(8,128)(2,1)S(1)}) custom-call(bf16[1024,1792]{1,0:T(8,128)(2,1)S(1)} %copy-done.4, bf16[1024,1792]{1,0:T(8,128)(2,1)S(1)} %copy-done, bf16[1024,1792]{1,0:T(8,128)(2,1)S(1)} %copy-done.2), custom_call_target="tpu_custom_call" | custom-call | flops 1000000000 | tf_op jit(solution)/shard_map/own_attention/pallas_call | solution.py:257
  41.5 1.9 %copy-done.5 = f32[512,1792]{1,0:T(8,128)} copy-done((f32[512,1792]{1,0:T(8,128)}, f32[512,1792]{1,0:T(8,128)S(1)}, u32[]{:S(2)}) %copy-start.5) | copy-done | bytes 3670040
  43.4 1.9 %copy-done.7 = bf16[1024,1792]{1,0:T(8,128)(2,1)} copy-done((bf16[1024,1792]{1,0:T(8,128)(2,1)}, bf16[1024,1792]{1,0:T(8,128)(2,1)S(1)}, u32[]{:S(2)}) %copy-start.7) | copy-done | bytes 3670040
  45.4 24.2 %collective-permute-done.far_q_ref = bf16[512,1152]{1,0:T(8,128)(2,1)} collective-permute-done((bf16[512,1152]{1,0:T(8,128)(2,1)}, bf16[512,1152]{1,0:T(8,128)(2,1)}, u32[]{:S(2)}, u32[]{:S(2)}) %collective-permute-start) | collective-permute-done | bytes 1179680 | tf_op jit(solution)/shard_map/ppermute | solution.py:457
  69.6 6.5 %edge_attention.1 = (bf16[512,1280]{1,0:T(8,128)(2,1)S(1)}, bf16[512,768]{1,0:T(8,128)(2,1)S(1)}) custom-call(bf16[512,1152]{1,0:T(8,128)(2,1)} %collective-permute-done.far_q_ref, bf16[512,1280]{1,0:T(8,128)(2,1)S(1)} %collective-permute-done.1.near_kv_ref, bf16[1024,1792]{1,0:T(8,128)(2,1)S(1)} %copy-done.4, bf16[1024,1792]{1,0:T(8,128)(2,1)S(1)} %copy-done.1, ...), custom_call_target="tpu_custom_call" | custom-call | flops 60000002048 | tf_op jit(solution)/shard_map/edge_attention/pallas_call | solution.py:316
  76.1 0.9 copy-done.8
  77.0 1.9 %collective-permute-start.2 = (bf16[512,1280]{1,0:T(8,128)(2,1)S(1)}, bf16[512,1280]{1,0:T(8,128)(2,1)S(1)}, u32[]{:S(2)}, u32[]{:S(2)}) collective-permute-start(bf16[512,1280]{1,0:T(8,128)(2,1)S(1)} %get-tuple-element.45), channel_id=1, source_target_pairs={{0,4},{4,8},{8,12},{12,16},{16,20},{20,24},{24,28},{28,32},{32,36}... | collective-permute-start | bytes 3932168 | tf_op jit(solution)/shard_map/ppermute | solution.py:469
  78.9 5.6 %gather_pieces.1 = bf16[32,56,8,128]{3,2,1,0:T(8,128)(2,1)} custom-call(bf16[32,57,8,128]{3,2,1,0:T(8,128)(2,1)} %all-to-all-done.store_ref), custom_call_target="tpu_custom_call" | custom-call | flops 6000000000 | tf_op jit(solution)/shard_map/gather_pieces/pallas_call | solution.py:178
  84.5 8.0 %all-to-all-start.1 = ((bf16[32,56,8,128]{3,2,1,0:T(8,128)(2,1)}), bf16[32,56,8,128]{3,2,1,0:T(8,128)(2,1)}, u32[]{:S(2)}, u32[]{:S(2)}) async-start(bf16[32,56,8,128]{3,2,1,0:T(8,128)(2,1)} %gather_pieces.1), calls=%async_computation.1 | async-start | bytes 7340032 | tf_op jit(solution)/shard_map/all_to_all | solution.py:471
  92.5 1.0 collective-permute-done.2.far_ref
  93.4 2.0 %copy-done.6 = f32[512,1792]{1,0:T(8,128)S(1)} copy-done((f32[512,1792]{1,0:T(8,128)S(1)}, f32[512,1792]{1,0:T(8,128)}, u32[]{:S(2)}) %copy-start.6) | copy-done | bytes 3670040
  95.5 1.1 copy-done.9
  96.6 3.2 %merge_local.1.local_hbm = bf16[1024,1792]{1,0:T(8,128)(2,1)} custom-call(s32[1]{0:T(128)} %bitcast.5.first_ref, f32[512,1792]{1,0:T(8,128)S(1)} %copy-done.6, f32[512,128]{1,0:T(8,128)S(1)} %get-tuple-element.43.lse_ref, bf16[512,768]{1,0:T(8,128)(2,1)S(1)} %copy-done.9, ...), custom_call_target="tpu_custom_call", output_to_operand_aliasing={{}: (5, {})} | custom-call | flops 60000002048 | tf_op jit(solution)/shard_map/merge_local/pallas_call | solution.py:359
  99.8 38.8 %all-to-all-done.1.kv_hbm = bf16[32,56,8,128]{3,2,1,0:T(8,128)(2,1)} async-done(((bf16[32,56,8,128]{3,2,1,0:T(8,128)(2,1)}), bf16[32,56,8,128]{3,2,1,0:T(8,128)(2,1)}, u32[]{:S(2)}, u32[]{:S(2)}) %all-to-all-start.1) | async-done | bytes 3670048 | tf_op jit(solution)/shard_map/all_to_all | solution.py:471
  138.6 8.7 %final_attention.1 = bf16[1024,1792]{1,0:T(8,128)(2,1)} custom-call(f32[14]{0:T(128)S(1)} %add_divide_fusion.gate_ref, bf16[1024,1792]{1,0:T(8,128)(2,1)} %q_hbm.1, bf16[32,56,8,128]{3,2,1,0:T(8,128)(2,1)} %all-to-all-done.1.kv_hbm, bf16[1024,1792]{1,0:T(8,128)(2,1)} %merge_local.1.local_hbm), custom_call_target="tpu_custom_call" | custom-call | flops 7000000000 | tf_op jit(solution)/shard_map/final_attention/pallas_call | solution.py:423
  (20 shorter events, 0.2 us)
Async XLA Ops:
  6.5 63.0 %collective-permute-start.1 = (bf16[512,1280]{1,0:T(8,128)(2,1)S(1)}, bf16[512,1280]{1,0:T(8,128)(2,1)S(1)}, u32[]{:S(2)}, u32[]{:S(2)}) collective-permute-start(bf16[512,1280]{1,0:T(8,128)(2,1)S(1)} %get-tuple-element.38), channel_id=1, source_target_pairs={{0,4},{4,8},{8,12},{12,16},{16,20},{20,24},{24,28},{28,32},{32,36}... | collective-permute-start | bytes 3932168 | tf_op jit(solution)/shard_map/ppermute | solution.py:458
  11.1 58.4 %collective-permute-start = (bf16[512,1152]{1,0:T(8,128)(2,1)}, bf16[512,1152]{1,0:T(8,128)(2,1)}, u32[]{:S(2)}, u32[]{:S(2)}) collective-permute-start(bf16[512,1152]{1,0:T(8,128)(2,1)} %get-tuple-element.37), channel_id=1, source_target_pairs={{4,0},{8,4},{12,8},{16,12},{20,16},{24,20},{28,24},{32,28},{36,32}... | collective-permute-start | bytes 3538952 | tf_op jit(solution)/shard_map/ppermute | solution.py:457
  13.1 63.9 %all-to-all-start = ((bf16[32,57,8,128]{3,2,1,0:T(8,128)(2,1)}), bf16[32,57,8,128]{3,2,1,0:T(8,128)(2,1)}, u32[]{:S(2)}, u32[]{:S(2)}) async-start(bf16[32,57,8,128]{3,2,1,0:T(8,128)(2,1)} %get-tuple-element.33), calls=%async_computation | async-start | bytes 7471104 | tf_op jit(solution)/shard_map/all_to_all | solution.py:459
  20.8 2.0 %copy-start = (bf16[1024,1792]{1,0:T(8,128)(2,1)S(1)}, bf16[1024,1792]{1,0:T(8,128)(2,1)}, u32[]{:S(2)}) copy-start(bf16[1024,1792]{1,0:T(8,128)(2,1)} %k_ref.5) | copy-start | bytes 11010052
  22.8 2.0 %copy-start.2 = (bf16[1024,1792]{1,0:T(8,128)(2,1)S(1)}, bf16[1024,1792]{1,0:T(8,128)(2,1)}, u32[]{:S(2)}) copy-start(bf16[1024,1792]{1,0:T(8,128)(2,1)} %v_ref.5) | copy-start | bytes 11010052
  24.8 2.0 %copy-start.4 = (bf16[1024,1792]{1,0:T(8,128)(2,1)S(1)}, bf16[1024,1792]{1,0:T(8,128)(2,1)}, u32[]{:S(2)}) copy-start(bf16[1024,1792]{1,0:T(8,128)(2,1)} %q_hbm.1) | copy-start | bytes 11010052
  26.9 42.7 %copy-start.1 = (bf16[1024,1792]{1,0:T(8,128)(2,1)S(1)}, bf16[1024,1792]{1,0:T(8,128)(2,1)}, u32[]{:S(2)}) copy-start(bf16[1024,1792]{1,0:T(8,128)(2,1)} %k_ref.5) | copy-start | bytes 11010052
  26.9 42.7 %copy-start.3 = (bf16[1024,1792]{1,0:T(8,128)(2,1)S(1)}, bf16[1024,1792]{1,0:T(8,128)(2,1)}, u32[]{:S(2)}) copy-start(bf16[1024,1792]{1,0:T(8,128)(2,1)} %v_ref.5) | copy-start | bytes 11010052
  41.5 1.9 %copy-start.5 = (f32[512,1792]{1,0:T(8,128)}, f32[512,1792]{1,0:T(8,128)S(1)}, u32[]{:S(2)}) copy-start(f32[512,1792]{1,0:T(8,128)S(1)} %get-tuple-element.42.low_ref) | copy-start | bytes 11010052
  43.4 1.9 %copy-start.7 = (bf16[1024,1792]{1,0:T(8,128)(2,1)}, bf16[1024,1792]{1,0:T(8,128)(2,1)S(1)}, u32[]{:S(2)}) copy-start(bf16[1024,1792]{1,0:T(8,128)(2,1)S(1)} %get-tuple-element.46.into_ref) | copy-start | bytes 11010052
  45.4 33.5 %copy-start.10 = (f32[14]{0:T(128)S(1)}, f32[14]{0:T(128)}, u32[]{:S(2)}) copy-start(f32[14]{0:T(128)} %param.15) | copy-start | bytes 172
  76.1 0.9 copy-start.8
  77.0 16.4 %collective-permute-start.2 = (bf16[512,1280]{1,0:T(8,128)(2,1)S(1)}, bf16[512,1280]{1,0:T(8,128)(2,1)S(1)}, u32[]{:S(2)}, u32[]{:S(2)}) collective-permute-start(bf16[512,1280]{1,0:T(8,128)(2,1)S(1)} %get-tuple-element.45), channel_id=1, source_target_pairs={{0,4},{4,8},{8,12},{12,16},{16,20},{20,24},{24,28},{28,32},{32,36}... | collective-permute-start | bytes 3932168 | tf_op jit(solution)/shard_map/ppermute | solution.py:469
  84.5 54.1 %all-to-all-start.1 = ((bf16[32,56,8,128]{3,2,1,0:T(8,128)(2,1)}), bf16[32,56,8,128]{3,2,1,0:T(8,128)(2,1)}, u32[]{:S(2)}, u32[]{:S(2)}) async-start(bf16[32,56,8,128]{3,2,1,0:T(8,128)(2,1)} %gather_pieces.1), calls=%async_computation.1 | async-start | bytes 7340032 | tf_op jit(solution)/shard_map/all_to_all | solution.py:471
  93.4 2.0 %copy-start.6 = (f32[512,1792]{1,0:T(8,128)S(1)}, f32[512,1792]{1,0:T(8,128)}, u32[]{:S(2)}) copy-start(f32[512,1792]{1,0:T(8,128)} %copy-done.5) | copy-start | bytes 11010052
  95.5 1.1 copy-start.9

commit v6 on v4

--- a/solution.py
+++ b/solution.py
@@ -18,7 +18,6 @@
 HALVES = 2
 LOG2E = 1.4426950408889634
 NEG = -1e30
-VMEM_LIMIT = 40 << 20
 BF = jnp.bfloat16
 F32 = jnp.float32
 ANY = pl.BlockSpec(memory_space=pl.ANY)
@@ -26,8 +25,8 @@
 SMALL = pl.BlockSpec(memory_space=pltpu.SMEM)
 
 
-def params():
-    return pltpu.CompilerParams(vmem_limit_bytes=VMEM_LIMIT)
+def params(mebibytes):
+    return pltpu.CompilerParams(vmem_limit_bytes=mebibytes << 20)
 
 
 def cost(micros):
@@ -45,40 +44,31 @@
         copy.wait()
 
 
-def edges_kernel(q_ref, k_ref, v_ref, back_ref, ahead_ref, sems):
-    split = FORWARD * DH
-    tail = pl.ds(k_ref.shape[0] - WIN, WIN)
-    width = q_ref.shape[1] - split
-    copy_all(
-        [
-            pltpu.make_async_copy(
-                q_ref.at[pl.ds(0, WIN), pl.ds(split, width)], back_ref, sems.at[0]
-            ),
-            pltpu.make_async_copy(
-                k_ref.at[tail, pl.ds(0, split)], ahead_ref.at[:, pl.ds(0, split)], sems.at[1]
-            ),
-            pltpu.make_async_copy(
-                v_ref.at[tail, pl.ds(0, split)], ahead_ref.at[:, pl.ds(split, split)], sems.at[2]
-            ),
-        ]
-    )
-
-
-def edges(queries, keys, values):
-    split = FORWARD * DH
-    return pl.pallas_call(
-        edges_kernel,
-        out_shape=(
-            jax.ShapeDtypeStruct((WIN, queries.shape[1] - split), BF),
-            jax.ShapeDtypeStruct((WIN, 2 * split), BF),
-        ),
-        in_specs=[ANY] * 3,
-        out_specs=(WHOLE, WHOLE),
-        scratch_shapes=[pltpu.SemaphoreType.DMA((3,))],
-        compiler_params=params(),
+def cut_kernel(areas, *refs):
+    out_ref, sems = refs[-2:]
+    width = out_ref.shape[1] // len(areas)
+    copies = [
+        pltpu.make_async_copy(
+            ref.at[pl.ds(row, WIN), pl.ds(col, width)],
+            out_ref.at[:, pl.ds(index * width, width)],
+            sems.at[index],
+        )
+        for index, (ref, (row, col)) in enumerate(zip(refs, areas))
+    ]
+    copy_all(copies)
+
+
+def cut(arrays, areas, width, name):
+    return pl.pallas_call(
+        functools.partial(cut_kernel, areas),
+        out_shape=jax.ShapeDtypeStruct((WIN, width), BF),
+        in_specs=[ANY] * len(arrays),
+        out_specs=WHOLE,
+        scratch_shapes=[pltpu.SemaphoreType.DMA((len(arrays),))],
+        compiler_params=params(4),
         cost_estimate=cost(2),
-        name="cut_edges",
-    )(in_hbm(queries), in_hbm(keys), in_hbm(values))
+        name=name,
+    )(*map(in_hbm, arrays))
 
 
 def pack_kernel(blocks, heads, keys_ref, values_ref, ids_ref, out_ref, stage, in_sems, out_sems):
@@ -123,7 +113,7 @@
             pltpu.SemaphoreType.DMA((2 * blocks,)),
             pltpu.SemaphoreType.DMA((2 * blocks + 1,)),
         ],
-        compiler_params=params(),
+        compiler_params=params(8),
         cost_estimate=cost(2),
         name="pack_pieces",
     )(
@@ -192,7 +182,7 @@
             pltpu.SemaphoreType.DMA((4,)),
             pltpu.SemaphoreType.DMA((8,)),
         ],
-        compiler_params=params(),
+        compiler_params=params(16),
         cost_estimate=cost(6),
         name="gather_pieces",
     )(in_hbm(store))
@@ -265,8 +255,8 @@
         ),
         in_specs=[WHOLE] * 3,
         out_specs=(WHOLE,) * 3,
-        compiler_params=params(),
-        cost_estimate=cost(1),
+        compiler_params=params(30),
+        cost_estimate=cost(20),
         name="own_attention",
     )(queries, keys, values)
 
@@ -304,30 +294,27 @@
     out_ref[:, pl.ds(count * DH, DH)] = packed.astype(BF)
 
 
-def edge_kernel(
-    scale, heads, far_q_ref, near_kv_ref, q_ref, k_ref, v_ref, far_ref, near_ref, lse_ref
-):
-    far = [(head - FORWARD, head, head) for head in range(FORWARD, heads)]
-    near = [(head, head, FORWARD + head) for head in range(FORWARD)]
-    tail = k_ref.shape[0] - WIN
-    edge_part(scale, far, tail, far_q_ref, k_ref, v_ref, far_ref, lse_ref)
-    edge_part(scale, near, 0, q_ref, near_kv_ref, near_kv_ref, near_ref, lse_ref)
-
-
-def edge_attention(far_q, near_kv, queries, keys, values, heads, scale):
-    return pl.pallas_call(
-        functools.partial(edge_kernel, scale, heads),
-        out_shape=(
-            jax.ShapeDtypeStruct((WIN, (heads - FORWARD + 1) * DH), BF),
-            jax.ShapeDtypeStruct((WIN, (FORWARD + 1) * DH), BF),
-        ),
-        in_specs=[WHOLE] * 5,
-        out_specs=(WHOLE,) * 2,
+def far_kernel(scale, heads, q_ref, k_ref, v_ref, out_ref, lse_ref):
+    slots = [(head - FORWARD, head, head) for head in range(FORWARD, heads)]
+    edge_part(scale, slots, k_ref.shape[0] - WIN, q_ref, k_ref, v_ref, out_ref, lse_ref)
+
+
+def near_kernel(scale, q_ref, kv_ref, out_ref, lse_ref):
+    slots = [(head, head, FORWARD + head) for head in range(FORWARD)]
+    edge_part(scale, slots, 0, q_ref, kv_ref, kv_ref, out_ref, lse_ref)
+
+
+def edge_attention(kernel, arrays, count, micros, name):
+    return pl.pallas_call(
+        kernel,
+        out_shape=jax.ShapeDtypeStruct((WIN, (count + 1) * DH), BF),
+        in_specs=[WHOLE] * len(arrays),
+        out_specs=WHOLE,
         scratch_shapes=[pltpu.VMEM((WIN, DH), F32)],
-        compiler_params=params(),
-        cost_estimate=cost(60),
-        name="edge_attention",
-    )(far_q, near_kv, queries, keys, values)
+        compiler_params=params(24),
+        cost_estimate=cost(micros),
+        name=name,
+    )(*arrays)
 
 
 def unpacked(stat, count):
@@ -365,7 +352,7 @@
         in_specs=[SMALL, whole(low), whole(lse), whole(near), whole(far), ANY],
         out_specs=pl.BlockSpec((WIN, width), lambda i: (0, 0)),
         input_output_aliases={5: 0},
-        compiler_params=params(),
+        compiler_params=params(16),
         cost_estimate=cost(60),
         name="merge_local",
     )(first, low, lse, near, far, in_hbm(local))
@@ -435,7 +422,7 @@
             pltpu.SemaphoreType.DMA((chunks, 3)),
             pltpu.SemaphoreType.DMA((chunks,)),
         ],
-        compiler_params=params(),
+        compiler_params=params(24),
         cost_estimate=cost(7),
         name="final_attention",
     )(gate, in_hbm(queries), in_hbm(kv), in_hbm(local))
@@ -451,26 +438,36 @@
     wanted = q_blocks * heads * TOPK
     upward = [(i, i + 1) for i in range(devices - 1)]
     downward = [(i, i - 1) for i in range(1, devices)]
-    back_q, ahead_kv = edges(queries, token_keys, token_values)
+    split = FORWARD * DH
+    back_q = cut([queries], [(0, split)], heads * DH - split, "cut_queries")
     far_q = lax.ppermute(back_q, "seq", downward)
-    near_kv = lax.ppermute(ahead_kv, "seq", upward)
     ids = retrieved.reshape(-1)
     ids_tile = jnp.zeros((PIECE * DH,), BF).at[:wanted].set(ids.astype(BF)).reshape(PIECE, DH)
     ids_tile, _ = lax.optimization_barrier((ids_tile, back_q))
     sent = pack(mem_keys, mem_values, ids_tile, blocks, heads)
+    sent, late_keys, late_values = lax.optimization_barrier((sent, token_keys, token_values))
+    tail = tokens - WIN
+    ahead_kv = cut([late_keys, late_values], [(tail, 0)] * 2, 2 * split, "cut_tails")
+    near_kv = lax.ppermute(ahead_kv, "seq", upward)
     store = lax.all_to_all(sent, "seq", split_axis=0, concat_axis=0, tiled=True)
     gate_share = 1.0 / (1.0 + jnp.exp(-gate_bias))
     first = lax.axis_index("seq").reshape(1).astype(jnp.int32)
     low, lse, local = own_attention(queries, token_keys, token_values, heads, scale)
-    far_part, near = edge_attention(
-        far_q, near_kv, queries, token_keys, token_values, heads, scale
-    )
-    store, low, lse, local, far_part, near = lax.optimization_barrier(
-        (store, low, lse, local, far_part, near)
-    )
+    far_part = edge_attention(
+        functools.partial(far_kernel, scale, heads),
+        (far_q, token_keys, token_values),
+        heads - FORWARD,
+        60,
+        "far_attention",
+    )
+    store, low, lse, local, far_part = lax.optimization_barrier((store, low, lse, local, far_part))
     far = lax.ppermute(far_part, "seq", upward)
     pieces = gather(store, blocks, heads, wanted)
+    pieces, late_q = lax.optimization_barrier((pieces, queries))
     kv = lax.all_to_all(pieces, "seq", split_axis=0, concat_axis=0, tiled=True)
+    near = edge_attention(
+        functools.partial(near_kernel, scale), (late_q, near_kv), FORWARD, 5, "near_attention"
+    )
     local = merge(first, low, lse, near, far, local, heads)
     kv, local = lax.optimization_barrier((kv, local))
     return final_attention(gate_share, queries, kv, local, heads, scale)

time: 141 us -> 141 us (level)
  Pallas kernels: 48.8 us -> 47.1 us
    ppermute x1, waiting for transfers between devices: 0.93 us -> 27.8 us  [body(): far = lax.ppermute(far_part, 'seq', upward)]
    all_to_all x1, waiting for transfers between devices: 38.8 us -> 12 us  [body(): kv = lax.all_to_all(pieces, 'seq', split_axis=0, concat_axis=0, tiled=True)]
    pallas_call x1, Pallas kernels: 17.9 us -> 14.7 us  [own_attention(): pl.pallas_call(functools.partial(own_kernel, scale, heads), out_shape=(ja...]
    all_to_all x1, waiting for transfers between devices: 15.3 us -> 18.3 us  [body(): store = lax.all_to_all(sent, 'seq', split_axis=0, concat_axis=0, tiled=True)]
    ppermute x1, waiting for transfers between devices: 2.37 us -> 0.01 us  [body(): far_q = lax.ppermute(back_q, 'seq', downward)]
    unnamed x18 -> x20, local copies, waits for them, and re-layouts: 9.93 us -> 8.99 us
    pallas_call x2 -> x4, Pallas kernels: 10.3 us -> 10.6 us  [the longest x2 6.79 us: edge_attention(): pl.pallas_call(kernel, out_shape=jax.ShapeDtypeStruct((WIN, (count + 1) *...]
  transfers between devices with their start and end apart: 5 -> 5, of which waited for: 4 -> 3; matrix products, arithmetic and copies ran while one was open for 0% -> 0% of each run, Pallas kernels for 27% -> 26%
where the time goes in v6:
time: 141 us; the launch traced here: 140 us
  waiting for transfers between devices  58.1 us (41%)
  Pallas kernels  47.1 us (33%)
  starting transfers between devices  25 us (18%)
  local copies, waits for them, and re-layouts  9.23 us (7%)
    ppermute x1, waiting for transfers between devices, body(): far = lax.ppermute(far_part, 'seq', upward)  27.8 us
    all_to_all x1, waiting for transfers between devices, body(): store = lax.all_to_all(sent, 'seq', split_axis=0, concat_axis=0, tiled=True)  18.3 us
    pallas_call x1, Pallas kernels, own_attention(): pl.pallas_call(functools.partial(own_kernel, scale, heads), out_shape=(ja...  14.7 us
    all_to_all x1, waiting for transfers between devices, body(): kv = lax.all_to_all(pieces, 'seq', split_axis=0, concat_axis=0, tiled=True)  12 us
    unnamed x20, local copies, waits for them, and re-layouts  8.99 us
    pallas_call x1, Pallas kernels, final_attention(): pl.pallas_call(functools.partial(final_kernel, scale, heads), out_shape=p...  8.66 us
    all_to_all x1, starting transfers between devices, body(): kv = lax.all_to_all(pieces, 'seq', split_axis=0, concat_axis=0, tiled=True)  8.04 us
    all_to_all x1, starting transfers between devices, body(): store = lax.all_to_all(sent, 'seq', split_axis=0, concat_axis=0, tiled=True)  7.92 us
  transfers between devices with their start and end apart: 5, of which 3 were waited for; matrix products, arithmetic and copies ran while one was open for 0% of the time, Pallas kernels for 26%

profile of v6, /device:TPU:1, one launch (start us, length us, event | category | flops | bytes accessed | tf_op | source)
XLA Modules:
  0.0 139.8 jit_solution(16517736571844321856)
XLA Ops:
  0.0 2.3 %cut_queries.1 = bf16[512,1152]{1,0:T(8,128)(2,1)} custom-call(bf16[1024,1792]{1,0:T(8,128)(2,1)} %q_hbm.1), custom_call_target="tpu_custom_call" | custom-call | flops 2000000000 | tf_op jit(solution)/shard_map/cut_queries/pallas_call | solution.py:62
  2.3 3.3 %collective-permute-start = (bf16[512,1152]{1,0:T(8,128)(2,1)}, bf16[512,1152]{1,0:T(8,128)(2,1)}, u32[]{:S(2)}, u32[]{:S(2)}) collective-permute-start(bf16[512,1152]{1,0:T(8,128)(2,1)} %cut_queries.1), channel_id=1, source_target_pairs={{4,0},{8,4},{12,8},{16,12},{20,16},{24,20},{28,24},{32,28},{36,32}... | collective-permute-start | bytes 3538952 | tf_op jit(solution)/shard_map/ppermute | solution.py:443
  5.7 0.1 copy.10
  5.8 0.1 convert_element_type.7
  5.9 3.1 %pack_pieces.1 = bf16[32,57,8,128]{3,2,1,0:T(8,128)(2,1)} custom-call(bf16[64,14,8,128]{3,2,1,0:T(8,128)(2,1)} %bitcast.9, bf16[64,14,8,128]{3,2,1,0:T(8,128)(2,1)} %bitcast.10, bf16[32,1,8,128]{3,2,1,0:T(8,128)(2,1)S(1)} %broadcast_in_dim.4.ids_ref), custom_call_target="tpu_custom_call" | custom-call | flops 2000000000 | tf_op jit(solution)/shard_map/pack_pieces/pallas_call | solution.py:106
  9.1 7.9 %all-to-all-start = ((bf16[32,57,8,128]{3,2,1,0:T(8,128)(2,1)}), bf16[32,57,8,128]{3,2,1,0:T(8,128)(2,1)}, u32[]{:S(2)}, u32[]{:S(2)}) async-start(bf16[32,57,8,128]{3,2,1,0:T(8,128)(2,1)} %pack_pieces.1), calls=%async_computation | async-start | bytes 7471104 | tf_op jit(solution)/shard_map/all_to_all | solution.py:452
  17.0 1.5 %cut_tails.1 = bf16[512,1280]{1,0:T(8,128)(2,1)S(1)} custom-call(bf16[1024,1792]{1,0:T(8,128)(2,1)} %refs_0_.2, bf16[1024,1792]{1,0:T(8,128)(2,1)} %refs_1_), custom_call_target="tpu_custom_call" | custom-call | flops 2000000000 | tf_op jit(solution)/shard_map/cut_tails/pallas_call | solution.py:62
  18.5 3.8 %collective-permute-start.1 = (bf16[512,1280]{1,0:T(8,128)(2,1)S(1)}, bf16[512,1280]{1,0:T(8,128)(2,1)S(1)}, u32[]{:S(2)}, u32[]{:S(2)}) collective-permute-start(bf16[512,1280]{1,0:T(8,128)(2,1)S(1)} %cut_tails.1), channel_id=1, source_target_pairs={{0,4},{4,8},{8,12},{12,16},{16,20},{20,24},{24,28},{28,32},{32,36}... | collective-permute-start | bytes 3932168 | tf_op jit(solution)/shard_map/ppermute | solution.py:451
  22.3 2.0 %copy-done.2 = bf16[1024,1792]{1,0:T(8,128)(2,1)S(1)} copy-done((bf16[1024,1792]{1,0:T(8,128)(2,1)S(1)}, bf16[1024,1792]{1,0:T(8,128)(2,1)}, u32[]{:S(2)}) %copy-start.2) | copy-done | bytes 3670040
  24.4 14.7 %own_attention.1 = (f32[512,1792]{1,0:T(8,128)S(1)}, f32[512,128]{1,0:T(8,128)S(1)}, bf16[1024,1792]{1,0:T(8,128)(2,1)S(1)}) custom-call(bf16[1024,1792]{1,0:T(8,128)(2,1)S(1)} %copy-done.2, bf16[1024,1792]{1,0:T(8,128)(2,1)S(1)} %copy-done, bf16[1024,1792]{1,0:T(8,128)(2,1)S(1)} %copy-done.1), custom_call_target="tpu_custom_call" | custom-call | flops 20000000000 | tf_op jit(solution)/shard_map/own_attention/pallas_call | solution.py:249
  39.0 1.9 %copy-done.5 = bf16[1024,1792]{1,0:T(8,128)(2,1)} copy-done((bf16[1024,1792]{1,0:T(8,128)(2,1)}, bf16[1024,1792]{1,0:T(8,128)(2,1)S(1)}, u32[]{:S(2)}) %copy-start.5) | copy-done | bytes 3670040
  41.0 1.9 %copy-done.6 = f32[512,1792]{1,0:T(8,128)} copy-done((f32[512,1792]{1,0:T(8,128)}, f32[512,1792]{1,0:T(8,128)S(1)}, u32[]{:S(2)}) %copy-start.6) | copy-done | bytes 3670040
  42.9 4.7 %far_attention.1 = bf16[512,1280]{1,0:T(8,128)(2,1)S(1)} custom-call(bf16[512,1152]{1,0:T(8,128)(2,1)} %collective-permute-done.q_ref, bf16[1024,1792]{1,0:T(8,128)(2,1)S(1)} %copy-done, bf16[1024,1792]{1,0:T(8,128)(2,1)S(1)} %copy-done.1), custom_call_target="tpu_custom_call" | custom-call | flops 60000002048 | tf_op jit(solution)/shard_map/far_attention/pallas_call | solution.py:308
  47.6 1.1 copy-done.4
  48.7 18.3 %all-to-all-done.store_ref = bf16[32,57,8,128]{3,2,1,0:T(8,128)(2,1)} async-done(((bf16[32,57,8,128]{3,2,1,0:T(8,128)(2,1)}), bf16[32,57,8,128]{3,2,1,0:T(8,128)(2,1)}, u32[]{:S(2)}, u32[]{:S(2)}) %all-to-all-start) | async-done | bytes 3735584 | tf_op jit(solution)/shard_map/all_to_all | solution.py:452
  67.0 1.9 %collective-permute-start.2 = (bf16[512,1280]{1,0:T(8,128)(2,1)}, bf16[512,1280]{1,0:T(8,128)(2,1)}, u32[]{:S(2)}, u32[]{:S(2)}) collective-permute-start(bf16[512,1280]{1,0:T(8,128)(2,1)} %copy-done.4), channel_id=1, source_target_pairs={{0,4},{4,8},{8,12},{12,16},{16,20},{20,24},{24,28},{28,32},{32,36}... | collective-permute-start | bytes 3932168 | tf_op jit(solution)/shard_map/ppermute | solution.py:464
  69.0 5.6 %gather_pieces.1 = bf16[32,56,8,128]{3,2,1,0:T(8,128)(2,1)} custom-call(bf16[32,57,8,128]{3,2,1,0:T(8,128)(2,1)} %all-to-all-done.store_ref), custom_call_target="tpu_custom_call" | custom-call | flops 6000000000 | tf_op jit(solution)/shard_map/gather_pieces/pallas_call | solution.py:170
  74.6 8.0 %all-to-all-start.1 = ((bf16[32,56,8,128]{3,2,1,0:T(8,128)(2,1)}), bf16[32,56,8,128]{3,2,1,0:T(8,128)(2,1)}, u32[]{:S(2)}, u32[]{:S(2)}) async-start(bf16[32,56,8,128]{3,2,1,0:T(8,128)(2,1)} %gather_pieces.1), calls=%async_computation.1 | async-start | bytes 7340032 | tf_op jit(solution)/shard_map/all_to_all | solution.py:467
  82.6 2.0 %copy-done.3 = bf16[1024,1792]{1,0:T(8,128)(2,1)S(1)} copy-done((bf16[1024,1792]{1,0:T(8,128)(2,1)S(1)}, bf16[1024,1792]{1,0:T(8,128)(2,1)}, u32[]{:S(2)}) %copy-start.3) | copy-done | bytes 3670040
  84.7 2.1 %near_attention.1.near_ref = bf16[512,768]{1,0:T(8,128)(2,1)S(1)} custom-call(bf16[1024,1792]{1,0:T(8,128)(2,1)S(1)} %copy-done.3, bf16[512,1280]{1,0:T(8,128)(2,1)S(1)} %collective-permute-done.1.kv_ref), custom_call_target="tpu_custom_call" | custom-call | flops 5000000000 | tf_op jit(solution)/shard_map/near_attention/pallas_call | solution.py:308
  86.7 27.8 %collective-permute-done.2.far_ref = bf16[512,1280]{1,0:T(8,128)(2,1)} collective-permute-done((bf16[512,1280]{1,0:T(8,128)(2,1)}, bf16[512,1280]{1,0:T(8,128)(2,1)}, u32[]{:S(2)}, u32[]{:S(2)}) %collective-permute-start.2) | collective-permute-done | bytes 1310752 | tf_op jit(solution)/shard_map/ppermute | solution.py:464
  114.5 4.5 %merge_local.1.local_hbm = bf16[1024,1792]{1,0:T(8,128)(2,1)} custom-call(s32[1]{0:T(128)} %bitcast.5.first_ref, f32[512,1792]{1,0:T(8,128)S(1)} %copy-done.7, f32[512,128]{1,0:T(8,128)S(1)} %get-tuple-element.41.lse_ref, bf16[512,768]{1,0:T(8,128)(2,1)S(1)} %near_attention.1.near_ref, ...), custom_call_target="tpu_custom_call", output_to_operand_aliasing={{}: (5, {})} | custom-call | flops 60000002048 | tf_op jit(solution)/shard_map/merge_local/pallas_call | solution.py:348
  119.0 12.0 %all-to-all-done.1.kv_hbm = bf16[32,56,8,128]{3,2,1,0:T(8,128)(2,1)} async-done(((bf16[32,56,8,128]{3,2,1,0:T(8,128)(2,1)}), bf16[32,56,8,128]{3,2,1,0:T(8,128)(2,1)}, u32[]{:S(2)}, u32[]{:S(2)}) %all-to-all-start.1) | async-done | bytes 3670048 | tf_op jit(solution)/shard_map/all_to_all | solution.py:467
  131.0 8.7 %final_attention.1 = bf16[1024,1792]{1,0:T(8,128)(2,1)} custom-call(f32[14]{0:T(128)S(1)} %add_divide_fusion.gate_ref, bf16[1024,1792]{1,0:T(8,128)(2,1)} %q_hbm.1, bf16[32,56,8,128]{3,2,1,0:T(8,128)(2,1)} %all-to-all-done.1.kv_hbm, bf16[1024,1792]{1,0:T(8,128)(2,1)} %merge_local.1.local_hbm), custom_call_target="tpu_custom_call" | custom-call | flops 7000000000 | tf_op jit(solution)/shard_map/final_attention/pallas_call | solution.py:412
  (21 shorter events, 0.1 us)
Async XLA Ops:
  0.0 5.7 %copy-start.8 = (s32[2,14,2]{1,2,0:T(2,128)S(1)}, s32[2,14,2]{1,2,0:T(2,128)}, u32[]{:S(2)}) copy-start(s32[2,14,2]{1,2,0:T(2,128)} %param.14) | copy-start | bytes 676
  2.3 40.6 %collective-permute-start = (bf16[512,1152]{1,0:T(8,128)(2,1)}, bf16[512,1152]{1,0:T(8,128)(2,1)}, u32[]{:S(2)}, u32[]{:S(2)}) collective-permute-start(bf16[512,1152]{1,0:T(8,128)(2,1)} %cut_queries.1), channel_id=1, source_target_pairs={{4,0},{8,4},{12,8},{16,12},{20,16},{24,20},{28,24},{32,28},{36,32}... | collective-permute-start | bytes 3538952 | tf_op jit(solution)/shard_map/ppermute | solution.py:443
  9.1 58.0 %all-to-all-start = ((bf16[32,57,8,128]{3,2,1,0:T(8,128)(2,1)}), bf16[32,57,8,128]{3,2,1,0:T(8,128)(2,1)}, u32[]{:S(2)}, u32[]{:S(2)}) async-start(bf16[32,57,8,128]{3,2,1,0:T(8,128)(2,1)} %pack_pieces.1), calls=%async_computation | async-start | bytes 7471104 | tf_op jit(solution)/shard_map/all_to_all | solution.py:452
  17.0 5.3 %copy-start = (bf16[1024,1792]{1,0:T(8,128)(2,1)S(1)}, bf16[1024,1792]{1,0:T(8,128)(2,1)}, u32[]{:S(2)}) copy-start(bf16[1024,1792]{1,0:T(8,128)(2,1)} %refs_0_.2) | copy-start | bytes 11010052
  17.0 5.3 %copy-start.1 = (bf16[1024,1792]{1,0:T(8,128)(2,1)S(1)}, bf16[1024,1792]{1,0:T(8,128)(2,1)}, u32[]{:S(2)}) copy-start(bf16[1024,1792]{1,0:T(8,128)(2,1)} %refs_1_) | copy-start | bytes 11010052
  18.5 64.1 %collective-permute-start.1 = (bf16[512,1280]{1,0:T(8,128)(2,1)S(1)}, bf16[512,1280]{1,0:T(8,128)(2,1)S(1)}, u32[]{:S(2)}, u32[]{:S(2)}) collective-permute-start(bf16[512,1280]{1,0:T(8,128)(2,1)S(1)} %cut_tails.1), channel_id=1, source_target_pairs={{0,4},{4,8},{8,12},{12,16},{16,20},{20,24},{24,28},{28,32},{32,36}... | collective-permute-start | bytes 3932168 | tf_op jit(solution)/shard_map/ppermute | solution.py:451
  22.3 2.0 %copy-start.2 = (bf16[1024,1792]{1,0:T(8,128)(2,1)S(1)}, bf16[1024,1792]{1,0:T(8,128)(2,1)}, u32[]{:S(2)}) copy-start(bf16[1024,1792]{1,0:T(8,128)(2,1)} %q_hbm.1) | copy-start | bytes 11010052
  39.0 1.9 %copy-start.5 = (bf16[1024,1792]{1,0:T(8,128)(2,1)}, bf16[1024,1792]{1,0:T(8,128)(2,1)S(1)}, u32[]{:S(2)}) copy-start(bf16[1024,1792]{1,0:T(8,128)(2,1)S(1)} %get-tuple-element.46.into_ref) | copy-start | bytes 11010052
  41.0 1.9 %copy-start.6 = (f32[512,1792]{1,0:T(8,128)}, f32[512,1792]{1,0:T(8,128)S(1)}, u32[]{:S(2)}) copy-start(f32[512,1792]{1,0:T(8,128)S(1)} %get-tuple-element.40.low_ref) | copy-start | bytes 11010052
  42.9 26.1 %copy-start.9 = (f32[14]{0:T(128)S(1)}, f32[14]{0:T(128)}, u32[]{:S(2)}) copy-start(f32[14]{0:T(128)} %param.15) | copy-start | bytes 172
  47.6 1.1 copy-start.4
  67.0 47.5 %collective-permute-start.2 = (bf16[512,1280]{1,0:T(8,128)(2,1)}, bf16[512,1280]{1,0:T(8,128)(2,1)}, u32[]{:S(2)}, u32[]{:S(2)}) collective-permute-start(bf16[512,1280]{1,0:T(8,128)(2,1)} %copy-done.4), channel_id=1, source_target_pairs={{0,4},{4,8},{8,12},{12,16},{16,20},{20,24},{24,28},{28,32},{32,36}... | collective-permute-start | bytes 3932168 | tf_op jit(solution)/shard_map/ppermute | solution.py:464
  74.6 56.4 %all-to-all-start.1 = ((bf16[32,56,8,128]{3,2,1,0:T(8,128)(2,1)}), bf16[32,56,8,128]{3,2,1,0:T(8,128)(2,1)}, u32[]{:S(2)}, u32[]{:S(2)}) async-start(bf16[32,56,8,128]{3,2,1,0:T(8,128)(2,1)} %gather_pieces.1), calls=%async_computation.1 | async-start | bytes 7340032 | tf_op jit(solution)/shard_map/all_to_all | solution.py:467
  82.6 2.0 %copy-start.3 = (bf16[1024,1792]{1,0:T(8,128)(2,1)S(1)}, bf16[1024,1792]{1,0:T(8,128)(2,1)}, u32[]{:S(2)}) copy-start(bf16[1024,1792]{1,0:T(8,128)(2,1)} %q_hbm.1) | copy-start | bytes 11010052
  84.7 29.9 %copy-start.7 = (f32[512,1792]{1,0:T(8,128)S(1)}, f32[512,1792]{1,0:T(8,128)}, u32[]{:S(2)}) copy-start(f32[512,1792]{1,0:T(8,128)} %copy-done.6) | copy-start | bytes 11010052

commit v7 on v6

--- a/solution.py
+++ b/solution.py
@@ -453,15 +453,16 @@
     gate_share = 1.0 / (1.0 + jnp.exp(-gate_bias))
     first = lax.axis_index("seq").reshape(1).astype(jnp.int32)
     low, lse, local = own_attention(queries, token_keys, token_values, heads, scale)
+    low, far_keys, far_values = lax.optimization_barrier((low, token_keys, token_values))
     far_part = edge_attention(
         functools.partial(far_kernel, scale, heads),
-        (far_q, token_keys, token_values),
+        (far_q, far_keys, far_values),
         heads - FORWARD,
         60,
         "far_attention",
     )
-    store, low, lse, local, far_part = lax.optimization_barrier((store, low, lse, local, far_part))
     far = lax.ppermute(far_part, "seq", upward)
+    store, low, lse, local, _ = lax.optimization_barrier((store, low, lse, local, far_part))
     pieces = gather(store, blocks, heads, wanted)
     pieces, late_q = lax.optimization_barrier((pieces, queries))
     kv = lax.all_to_all(pieces, "seq", split_axis=0, concat_axis=0, tiled=True)

time: 141 us -> 142 us (level)
  local copies, waits for them, and re-layouts: 9.23 us -> 4.34 us
  waiting for transfers between devices: 58.1 us -> 62.7 us
  Pallas kernels: 47.1 us -> 49.1 us
  starting transfers between devices: 25 us -> 23.4 us
    ppermute x1, waiting for transfers between devices: 27.8 us -> 39.8 us  [body(): far = lax.ppermute(far_part, 'seq', upward)]
    all_to_all x1, waiting for transfers between devices: 12 us -> 3.78 us  [body(): kv = lax.all_to_all(pieces, 'seq', split_axis=0, concat_axis=0, tiled=True)]
    unnamed x20 -> x18, local copies, waits for them, and re-layouts: 8.99 us -> 4.1 us
    pallas_call x2, Pallas kernels: 6.79 us -> 8.79 us  [edge_attention(): pl.pallas_call(kernel, out_shape=jax.ShapeDtypeStruct((WIN, (count + 1) *...]
    all_to_all x1, starting transfers between devices: 8.04 us -> 6.34 us  [body(): kv = lax.all_to_all(pieces, 'seq', split_axis=0, concat_axis=0, tiled=True)]
  transfers between devices with their start and end apart: 5 -> 5, of which waited for: 3 -> 3; matrix products, arithmetic and copies ran while one was open for 0% -> 0% of each run, Pallas kernels for 26% -> 27%
where the time goes in v7:
time: 142 us; the launch traced here: 140 us
  waiting for transfers between devices  62.7 us (44%)
  Pallas kernels  49.1 us (35%)
  starting transfers between devices  23.4 us (16%)
  local copies, waits for them, and re-layouts  4.34 us (3%)
    ppermute x1, waiting for transfers between devices, body(): far = lax.ppermute(far_part, 'seq', upward)  39.8 us
    all_to_all x1, waiting for transfers between devices, body(): store = lax.all_to_all(sent, 'seq', split_axis=0, concat_axis=0, tiled=True)  19.1 us
    pallas_call x1, Pallas kernels, own_attention(): pl.pallas_call(functools.partial(own_kernel, scale, heads), out_shape=(ja...  14.7 us
    pallas_call x2, Pallas kernels, edge_attention(): pl.pallas_call(kernel, out_shape=jax.ShapeDtypeStruct((WIN, (count + 1) *...  8.79 us
    pallas_call x1, Pallas kernels, final_attention(): pl.pallas_call(functools.partial(final_kernel, scale, heads), out_shape=p...  8.66 us
    all_to_all x1, starting transfers between devices, body(): store = lax.all_to_all(sent, 'seq', split_axis=0, concat_axis=0, tiled=True)  7.93 us
    all_to_all x1, starting transfers between devices, body(): kv = lax.all_to_all(pieces, 'seq', split_axis=0, concat_axis=0, tiled=True)  6.34 us
    pallas_call x1, Pallas kernels, gather(): pl.pallas_call(functools.partial(gather_kernel, blocks, heads, wanted), o...  5.57 us
  transfers between devices with their start and end apart: 5, of which 3 were waited for; matrix products, arithmetic and copies ran while one was open for 0% of the time, Pallas kernels for 27%

profile of v7, /device:TPU:1, one launch (start us, length us, event | category | flops | bytes accessed | tf_op | source)
XLA Modules:
  0.0 139.9 jit_solution(5097755011855094793)
XLA Ops:
  0.0 2.3 %cut_queries.1 = bf16[512,1152]{1,0:T(8,128)(2,1)} custom-call(bf16[1024,1792]{1,0:T(8,128)(2,1)} %q_hbm.1), custom_call_target="tpu_custom_call" | custom-call | flops 2000000000 | tf_op jit(solution)/shard_map/cut_queries/pallas_call | solution.py:62
  2.3 3.3 %collective-permute-start = (bf16[512,1152]{1,0:T(8,128)(2,1)}, bf16[512,1152]{1,0:T(8,128)(2,1)}, u32[]{:S(2)}, u32[]{:S(2)}) collective-permute-start(bf16[512,1152]{1,0:T(8,128)(2,1)} %cut_queries.1), channel_id=1, source_target_pairs={{4,0},{8,4},{12,8},{16,12},{20,16},{24,20},{28,24},{32,28},{36,32}... | collective-permute-start | bytes 3538952 | tf_op jit(solution)/shard_map/ppermute | solution.py:443
  5.7 0.1 copy.10
  5.8 0.1 convert_element_type.7
  5.9 3.1 %pack_pieces.1 = bf16[32,57,8,128]{3,2,1,0:T(8,128)(2,1)} custom-call(bf16[64,14,8,128]{3,2,1,0:T(8,128)(2,1)} %bitcast.9, bf16[64,14,8,128]{3,2,1,0:T(8,128)(2,1)} %bitcast.10, bf16[32,1,8,128]{3,2,1,0:T(8,128)(2,1)S(1)} %broadcast_in_dim.4.ids_ref), custom_call_target="tpu_custom_call" | custom-call | flops 2000000000 | tf_op jit(solution)/shard_map/pack_pieces/pallas_call | solution.py:106
  9.1 7.9 %all-to-all-start = ((bf16[32,57,8,128]{3,2,1,0:T(8,128)(2,1)}), bf16[32,57,8,128]{3,2,1,0:T(8,128)(2,1)}, u32[]{:S(2)}, u32[]{:S(2)}) async-start(bf16[32,57,8,128]{3,2,1,0:T(8,128)(2,1)} %pack_pieces.1), calls=%async_computation | async-start | bytes 7471104 | tf_op jit(solution)/shard_map/all_to_all | solution.py:452
  17.0 0.0 copy-start
  17.0 0.0 copy-start.1
  17.0 1.5 %cut_tails.1 = bf16[512,1280]{1,0:T(8,128)(2,1)S(1)} custom-call(bf16[1024,1792]{1,0:T(8,128)(2,1)} %refs_0_.2, bf16[1024,1792]{1,0:T(8,128)(2,1)} %refs_1_), custom_call_target="tpu_custom_call" | custom-call | flops 2000000000 | tf_op jit(solution)/shard_map/cut_tails/pallas_call | solution.py:62
  18.5 3.8 %collective-permute-start.1 = (bf16[512,1280]{1,0:T(8,128)(2,1)S(1)}, bf16[512,1280]{1,0:T(8,128)(2,1)S(1)}, u32[]{:S(2)}, u32[]{:S(2)}) collective-permute-start(bf16[512,1280]{1,0:T(8,128)(2,1)S(1)} %cut_tails.1), channel_id=1, source_target_pairs={{0,4},{4,8},{8,12},{12,16},{16,20},{20,24},{24,28},{28,32},{32,36}... | collective-permute-start | bytes 3932168 | tf_op jit(solution)/shard_map/ppermute | solution.py:451
  22.3 0.0 copy-start.2
  22.3 2.0 %copy-done.2 = bf16[1024,1792]{1,0:T(8,128)(2,1)S(1)} copy-done((bf16[1024,1792]{1,0:T(8,128)(2,1)S(1)}, bf16[1024,1792]{1,0:T(8,128)(2,1)}, u32[]{:S(2)}) %copy-start.2) | copy-done | bytes 3670040
  24.4 14.7 %own_attention.1 = (f32[512,1792]{1,0:T(8,128)S(1)}, f32[512,128]{1,0:T(8,128)S(1)}, bf16[1024,1792]{1,0:T(8,128)(2,1)S(1)}) custom-call(bf16[1024,1792]{1,0:T(8,128)(2,1)S(1)} %copy-done.2, bf16[1024,1792]{1,0:T(8,128)(2,1)S(1)} %copy-done, bf16[1024,1792]{1,0:T(8,128)(2,1)S(1)} %copy-done.1), custom_call_target="tpu_custom_call" | custom-call | flops 20000000000 | tf_op jit(solution)/shard_map/own_attention/pallas_call | solution.py:249
  39.1 6.7 %far_attention.1 = bf16[512,1280]{1,0:T(8,128)(2,1)} custom-call(bf16[512,1152]{1,0:T(8,128)(2,1)} %collective-permute-done.q_ref, bf16[1024,1792]{1,0:T(8,128)(2,1)S(1)} %copy-done, bf16[1024,1792]{1,0:T(8,128)(2,1)S(1)} %copy-done.1), custom_call_target="tpu_custom_call" | custom-call | flops 60000002048 | tf_op jit(solution)/shard_map/far_attention/pallas_call | solution.py:308
  45.8 2.0 %collective-permute-start.2 = (bf16[512,1280]{1,0:T(8,128)(2,1)}, bf16[512,1280]{1,0:T(8,128)(2,1)}, u32[]{:S(2)}, u32[]{:S(2)}) collective-permute-start(bf16[512,1280]{1,0:T(8,128)(2,1)} %far_attention.1), channel_id=1, source_target_pairs={{0,4},{4,8},{8,12},{12,16},{16,20},{20,24},{24,28},{28,32},{32,36}... | collective-permute-start | bytes 3932168 | tf_op jit(solution)/shard_map/ppermute | solution.py:464
  47.9 19.1 %all-to-all-done.store_ref = bf16[32,57,8,128]{3,2,1,0:T(8,128)(2,1)} async-done(((bf16[32,57,8,128]{3,2,1,0:T(8,128)(2,1)}), bf16[32,57,8,128]{3,2,1,0:T(8,128)(2,1)}, u32[]{:S(2)}, u32[]{:S(2)}) %all-to-all-start) | async-done | bytes 3735584 | tf_op jit(solution)/shard_map/all_to_all | solution.py:452
  67.0 5.6 %gather_pieces.1 = bf16[32,56,8,128]{3,2,1,0:T(8,128)(2,1)} custom-call(bf16[32,57,8,128]{3,2,1,0:T(8,128)(2,1)} %all-to-all-done.store_ref), custom_call_target="tpu_custom_call" | custom-call | flops 6000000000 | tf_op jit(solution)/shard_map/gather_pieces/pallas_call | solution.py:170
  72.6 6.3 %all-to-all-start.1 = ((bf16[32,56,8,128]{3,2,1,0:T(8,128)(2,1)}), bf16[32,56,8,128]{3,2,1,0:T(8,128)(2,1)}, u32[]{:S(2)}, u32[]{:S(2)}) async-start(bf16[32,56,8,128]{3,2,1,0:T(8,128)(2,1)} %gather_pieces.1), calls=%async_computation.1 | async-start | bytes 7340032 | tf_op jit(solution)/shard_map/all_to_all | solution.py:468
  79.0 2.0 %copy-done.3 = bf16[1024,1792]{1,0:T(8,128)(2,1)S(1)} copy-done((bf16[1024,1792]{1,0:T(8,128)(2,1)S(1)}, bf16[1024,1792]{1,0:T(8,128)(2,1)}, u32[]{:S(2)}) %copy-start.3) | copy-done | bytes 3670040
  81.0 2.1 %near_attention.1.near_ref = bf16[512,768]{1,0:T(8,128)(2,1)S(1)} custom-call(bf16[1024,1792]{1,0:T(8,128)(2,1)S(1)} %copy-done.3, bf16[512,1280]{1,0:T(8,128)(2,1)S(1)} %collective-permute-done.1.kv_ref), custom_call_target="tpu_custom_call" | custom-call | flops 5000000000 | tf_op jit(solution)/shard_map/near_attention/pallas_call | solution.py:308
  83.1 39.8 %collective-permute-done.2.far_ref = bf16[512,1280]{1,0:T(8,128)(2,1)} collective-permute-done((bf16[512,1280]{1,0:T(8,128)(2,1)}, bf16[512,1280]{1,0:T(8,128)(2,1)}, u32[]{:S(2)}, u32[]{:S(2)}) %collective-permute-start.2) | collective-permute-done | bytes 1310752 | tf_op jit(solution)/shard_map/ppermute | solution.py:464
  122.8 4.5 %merge_local.1.local_hbm = bf16[1024,1792]{1,0:T(8,128)(2,1)} custom-call(s32[1]{0:T(128)} %bitcast.5.first_ref, f32[512,1792]{1,0:T(8,128)S(1)} %copy-done.6, f32[512,128]{1,0:T(8,128)S(1)} %get-tuple-element.46.lse_ref, bf16[512,768]{1,0:T(8,128)(2,1)S(1)} %near_attention.1.near_ref, ...), custom_call_target="tpu_custom_call", output_to_operand_aliasing={{}: (5, {})} | custom-call | flops 60000002048 | tf_op jit(solution)/shard_map/merge_local/pallas_call | solution.py:348
  127.3 3.8 %all-to-all-done.1.kv_hbm = bf16[32,56,8,128]{3,2,1,0:T(8,128)(2,1)} async-done(((bf16[32,56,8,128]{3,2,1,0:T(8,128)(2,1)}), bf16[32,56,8,128]{3,2,1,0:T(8,128)(2,1)}, u32[]{:S(2)}, u32[]{:S(2)}) %all-to-all-start.1) | async-done | bytes 3670048 | tf_op jit(solution)/shard_map/all_to_all | solution.py:468
  131.1 8.7 %final_attention.1 = bf16[1024,1792]{1,0:T(8,128)(2,1)} custom-call(f32[14]{0:T(128)S(1)} %add_divide_fusion.gate_ref, bf16[1024,1792]{1,0:T(8,128)(2,1)} %q_hbm.1, bf16[32,56,8,128]{3,2,1,0:T(8,128)(2,1)} %all-to-all-done.1.kv_hbm, bf16[1024,1792]{1,0:T(8,128)(2,1)} %merge_local.1.local_hbm), custom_call_target="tpu_custom_call" | custom-call | flops 7000000000 | tf_op jit(solution)/shard_map/final_attention/pallas_call | solution.py:412
  (19 shorter events, 0.1 us)
Async XLA Ops:
  0.0 5.7 %copy-start.7 = (s32[2,14,2]{1,2,0:T(2,128)S(1)}, s32[2,14,2]{1,2,0:T(2,128)}, u32[]{:S(2)}) copy-start(s32[2,14,2]{1,2,0:T(2,128)} %param.14) | copy-start | bytes 676
  2.3 36.8 %collective-permute-start = (bf16[512,1152]{1,0:T(8,128)(2,1)}, bf16[512,1152]{1,0:T(8,128)(2,1)}, u32[]{:S(2)}, u32[]{:S(2)}) collective-permute-start(bf16[512,1152]{1,0:T(8,128)(2,1)} %cut_queries.1), channel_id=1, source_target_pairs={{4,0},{8,4},{12,8},{16,12},{20,16},{24,20},{28,24},{32,28},{36,32}... | collective-permute-start | bytes 3538952 | tf_op jit(solution)/shard_map/ppermute | solution.py:443
  9.1 58.0 %all-to-all-start = ((bf16[32,57,8,128]{3,2,1,0:T(8,128)(2,1)}), bf16[32,57,8,128]{3,2,1,0:T(8,128)(2,1)}, u32[]{:S(2)}, u32[]{:S(2)}) async-start(bf16[32,57,8,128]{3,2,1,0:T(8,128)(2,1)} %pack_pieces.1), calls=%async_computation | async-start | bytes 7471104 | tf_op jit(solution)/shard_map/all_to_all | solution.py:452
  17.0 5.3 %copy-start = (bf16[1024,1792]{1,0:T(8,128)(2,1)S(1)}, bf16[1024,1792]{1,0:T(8,128)(2,1)}, u32[]{:S(2)}) copy-start(bf16[1024,1792]{1,0:T(8,128)(2,1)} %refs_0_.2) | copy-start | bytes 11010052
  17.0 5.3 %copy-start.1 = (bf16[1024,1792]{1,0:T(8,128)(2,1)S(1)}, bf16[1024,1792]{1,0:T(8,128)(2,1)}, u32[]{:S(2)}) copy-start(bf16[1024,1792]{1,0:T(8,128)(2,1)} %refs_1_) | copy-start | bytes 11010052
  18.5 60.5 %collective-permute-start.1 = (bf16[512,1280]{1,0:T(8,128)(2,1)S(1)}, bf16[512,1280]{1,0:T(8,128)(2,1)S(1)}, u32[]{:S(2)}, u32[]{:S(2)}) collective-permute-start(bf16[512,1280]{1,0:T(8,128)(2,1)S(1)} %cut_tails.1), channel_id=1, source_target_pairs={{0,4},{4,8},{8,12},{12,16},{16,20},{20,24},{24,28},{28,32},{32,36}... | collective-permute-start | bytes 3932168 | tf_op jit(solution)/shard_map/ppermute | solution.py:451
  22.3 2.0 %copy-start.2 = (bf16[1024,1792]{1,0:T(8,128)(2,1)S(1)}, bf16[1024,1792]{1,0:T(8,128)(2,1)}, u32[]{:S(2)}) copy-start(bf16[1024,1792]{1,0:T(8,128)(2,1)} %q_hbm.1) | copy-start | bytes 11010052
  39.1 6.8 %copy-start.4 = (bf16[1024,1792]{1,0:T(8,128)(2,1)}, bf16[1024,1792]{1,0:T(8,128)(2,1)S(1)}, u32[]{:S(2)}) copy-start(bf16[1024,1792]{1,0:T(8,128)(2,1)S(1)} %get-tuple-element.50.into_ref) | copy-start | bytes 11010052
  39.1 6.8 %copy-start.5 = (f32[512,1792]{1,0:T(8,128)}, f32[512,1792]{1,0:T(8,128)S(1)}, u32[]{:S(2)}) copy-start(f32[512,1792]{1,0:T(8,128)S(1)} %get-tuple-element.45.low_ref) | copy-start | bytes 11010052
  39.1 8.8 %copy-start.8 = (f32[14]{0:T(128)S(1)}, f32[14]{0:T(128)}, u32[]{:S(2)}) copy-start(f32[14]{0:T(128)} %param.15) | copy-start | bytes 172
  45.8 77.0 %collective-permute-start.2 = (bf16[512,1280]{1,0:T(8,128)(2,1)}, bf16[512,1280]{1,0:T(8,128)(2,1)}, u32[]{:S(2)}, u32[]{:S(2)}) collective-permute-start(bf16[512,1280]{1,0:T(8,128)(2,1)} %far_attention.1), channel_id=1, source_target_pairs={{0,4},{4,8},{8,12},{12,16},{16,20},{20,24},{24,28},{28,32},{32,36}... | collective-permute-start | bytes 3932168 | tf_op jit(solution)/shard_map/ppermute | solution.py:464
  72.6 58.5 %all-to-all-start.1 = ((bf16[32,56,8,128]{3,2,1,0:T(8,128)(2,1)}), bf16[32,56,8,128]{3,2,1,0:T(8,128)(2,1)}, u32[]{:S(2)}, u32[]{:S(2)}) async-start(bf16[32,56,8,128]{3,2,1,0:T(8,128)(2,1)} %gather_pieces.1), calls=%async_computation.1 | async-start | bytes 7340032 | tf_op jit(solution)/shard_map/all_to_all | solution.py:468
  79.0 2.0 %copy-start.3 = (bf16[1024,1792]{1,0:T(8,128)(2,1)S(1)}, bf16[1024,1792]{1,0:T(8,128)(2,1)}, u32[]{:S(2)}) copy-start(bf16[1024,1792]{1,0:T(8,128)(2,1)} %q_hbm.1) | copy-start | bytes 11010052
  81.0 41.8 %copy-start.6 = (f32[512,1792]{1,0:T(8,128)S(1)}, f32[512,1792]{1,0:T(8,128)}, u32[]{:S(2)}) copy-start(f32[512,1792]{1,0:T(8,128)} %copy-done.5) | copy-start | bytes 11010052

commit v8 on v7

--- a/solution.py
+++ b/solution.py
@@ -14,7 +14,7 @@
 DH = 128
 PIECE = 8
 EDGE = 256
-FORWARD = 5
+FORWARD = 3
 HALVES = 2
 LOG2E = 1.4426950408889634
 NEG = -1e30

time: 142 us -> 148 us (1.042); the launches traced: 140 us -> 148 us
  waiting for transfers between devices: 62.7 us -> 72.5 us
  local copies, waits for them, and re-layouts: 4.34 us -> 9.08 us
  Pallas kernels: 49.1 us -> 44.4 us
  starting transfers between devices: 23.4 us -> 21.3 us
    ppermute x1, waiting for transfers between devices: 0.01 us -> 46.3 us  [body(): near_kv = lax.ppermute(ahead_kv, 'seq', upward)]
    ppermute x1, waiting for transfers between devices: 39.8 us -> 0.01 us  [body(): far = lax.ppermute(far_part, 'seq', upward)]
    ppermute x1, waiting for transfers between devices: 0.01 us -> 26.2 us  [body(): far_q = lax.ppermute(back_q, 'seq', downward)]
    all_to_all x1, waiting for transfers between devices: 19.1 us -> 0.01 us  [body(): store = lax.all_to_all(sent, 'seq', split_axis=0, concat_axis=0, tiled=True)]
    unnamed x18 -> x20, local copies, waits for them, and re-layouts: 4.1 us -> 8.84 us
    all_to_all x1, waiting for transfers between devices: 3.78 us -> 0.01 us  [body(): kv = lax.all_to_all(pieces, 'seq', split_axis=0, concat_axis=0, tiled=True)]
    pallas_call x2, Pallas kernels: 8.79 us -> 6.68 us  [edge_attention(): pl.pallas_call(kernel, out_shape=jax.ShapeDtypeStruct((WIN, (count + 1) *...]
    ppermute x1, starting transfers between devices: 3.8 us -> 1.92 us  [body(): near_kv = lax.ppermute(ahead_kv, 'seq', upward)]
  transfers between devices with their start and end apart: 5 -> 5, of which waited for: 3 -> 2; matrix products, arithmetic and copies ran while one was open for 0% -> 0% of each run, Pallas kernels for 27% -> 23%
where the time goes in v8:
time: 148 us
  waiting for transfers between devices  72.5 us (49%)
  Pallas kernels  44.4 us (30%)
  starting transfers between devices  21.3 us (14%)
  local copies, waits for them, and re-layouts  9.08 us (6%)
    ppermute x1, waiting for transfers between devices, body(): near_kv = lax.ppermute(ahead_kv, 'seq', upward)  46.3 us
    ppermute x1, waiting for transfers between devices, body(): far_q = lax.ppermute(back_q, 'seq', downward)  26.2 us
    pallas_call x1, Pallas kernels, own_attention(): pl.pallas_call(functools.partial(own_kernel, scale, heads), out_shape=(ja...  14.6 us
    unnamed x20, local copies, waits for them, and re-layouts  8.84 us
    pallas_call x1, Pallas kernels, final_attention(): pl.pallas_call(functools.partial(final_kernel, scale, heads), out_shape=p...  8.66 us
    all_to_all x1, starting transfers between devices, body(): store = lax.all_to_all(sent, 'seq', split_axis=0, concat_axis=0, tiled=True)  7.34 us
    pallas_call x2, Pallas kernels, edge_attention(): pl.pallas_call(kernel, out_shape=jax.ShapeDtypeStruct((WIN, (count + 1) *...  6.68 us
    all_to_all x1, starting transfers between devices, body(): kv = lax.all_to_all(pieces, 'seq', split_axis=0, concat_axis=0, tiled=True)  6.68 us
  transfers between devices with their start and end apart: 5, of which 2 were waited for; matrix products, arithmetic and copies ran while one was open for 0% of the time, Pallas kernels for 23%

profile of v8, /device:TPU:1, one launch (start us, length us, event | category | flops | bytes accessed | tf_op | source)
XLA Modules:
  0.0 147.7 jit_solution(1619454562719781949)
XLA Ops:
  0.0 1.4 cut_queries.1
  1.4 3.3 %collective-permute-start = (bf16[512,1408]{1,0:T(8,128)(2,1)S(1)}, bf16[512,1408]{1,0:T(8,128)(2,1)S(1)}, u32[]{:S(2)}, u32[]{:S(2)}) collective-permute-start(bf16[512,1408]{1,0:T(8,128)(2,1)S(1)} %cut_queries.1), channel_id=1, source_target_pairs={{4,0},{8,4},{12,8},{16,12},{20,16},{24,20},{28,24},{32,28},{36,32}... | collective-permute-start | bytes 4325384 | tf_op jit(solution)/shard_map/ppermute | solution.py:443
  4.8 0.1 copy.10
  4.9 0.1 convert_element_type.7
  5.0 3.1 %pack_pieces.1 = bf16[32,57,8,128]{3,2,1,0:T(8,128)(2,1)} custom-call(bf16[64,14,8,128]{3,2,1,0:T(8,128)(2,1)} %bitcast.9, bf16[64,14,8,128]{3,2,1,0:T(8,128)(2,1)} %bitcast.10, bf16[32,1,8,128]{3,2,1,0:T(8,128)(2,1)S(1)} %broadcast_in_dim.4.ids_ref), custom_call_target="tpu_custom_call" | custom-call | flops 2000000000 | tf_op jit(solution)/shard_map/pack_pieces/pallas_call | solution.py:106
  8.1 7.3 %all-to-all-start = ((bf16[32,57,8,128]{3,2,1,0:T(8,128)(2,1)}), bf16[32,57,8,128]{3,2,1,0:T(8,128)(2,1)}, u32[]{:S(2)}, u32[]{:S(2)}) async-start(bf16[32,57,8,128]{3,2,1,0:T(8,128)(2,1)} %pack_pieces.1), calls=%async_computation | async-start | bytes 7471104 | tf_op jit(solution)/shard_map/all_to_all | solution.py:452
  15.5 0.0 copy-start
  15.5 2.0 %copy-done = bf16[1024,1792]{1,0:T(8,128)(2,1)S(1)} copy-done((bf16[1024,1792]{1,0:T(8,128)(2,1)S(1)}, bf16[1024,1792]{1,0:T(8,128)(2,1)}, u32[]{:S(2)}) %copy-start) | copy-done | bytes 3670040
  17.5 2.0 %copy-done.2 = bf16[1024,1792]{1,0:T(8,128)(2,1)S(1)} copy-done((bf16[1024,1792]{1,0:T(8,128)(2,1)S(1)}, bf16[1024,1792]{1,0:T(8,128)(2,1)}, u32[]{:S(2)}) %copy-start.2) | copy-done | bytes 3670040
  19.6 2.0 %copy-done.3 = bf16[1024,1792]{1,0:T(8,128)(2,1)S(1)} copy-done((bf16[1024,1792]{1,0:T(8,128)(2,1)S(1)}, bf16[1024,1792]{1,0:T(8,128)(2,1)}, u32[]{:S(2)}) %copy-start.3) | copy-done | bytes 3670040
  21.6 14.6 %own_attention.1 = (f32[512,1792]{1,0:T(8,128)S(1)}, f32[512,128]{1,0:T(8,128)S(1)}, bf16[1024,1792]{1,0:T(8,128)(2,1)S(1)}) custom-call(bf16[1024,1792]{1,0:T(8,128)(2,1)S(1)} %copy-done.3, bf16[1024,1792]{1,0:T(8,128)(2,1)S(1)} %copy-done, bf16[1024,1792]{1,0:T(8,128)(2,1)S(1)} %copy-done.2), custom_call_target="tpu_custom_call" | custom-call | flops 20000000000 | tf_op jit(solution)/shard_map/own_attention/pallas_call | solution.py:249
  36.3 26.2 %collective-permute-done.q_ref = bf16[512,1408]{1,0:T(8,128)(2,1)S(1)} collective-permute-done((bf16[512,1408]{1,0:T(8,128)(2,1)S(1)}, bf16[512,1408]{1,0:T(8,128)(2,1)S(1)}, u32[]{:S(2)}, u32[]{:S(2)}) %collective-permute-start) | collective-permute-done | bytes 1441824 | tf_op jit(solution)/shard_map/ppermute | solution.py:443
  62.5 5.3 %far_attention.1 = bf16[512,1536]{1,0:T(8,128)(2,1)} custom-call(bf16[512,1408]{1,0:T(8,128)(2,1)S(1)} %collective-permute-done.q_ref, bf16[1024,1792]{1,0:T(8,128)(2,1)S(1)} %copy-done.1, bf16[1024,1792]{1,0:T(8,128)(2,1)S(1)} %copy-done.2), custom_call_target="tpu_custom_call" | custom-call | flops 60000002048 | tf_op jit(solution)/shard_map/far_attention/pallas_call | solution.py:308
  67.9 2.0 %collective-permute-start.2 = (bf16[512,1536]{1,0:T(8,128)(2,1)}, bf16[512,1536]{1,0:T(8,128)(2,1)S(1)}, u32[]{:S(2)}, u32[]{:S(2)}) collective-permute-start(bf16[512,1536]{1,0:T(8,128)(2,1)} %far_attention.1), channel_id=1, source_target_pairs={{0,4},{4,8},{8,12},{12,16},{16,20},{20,24},{24,28},{28,32},{32,36}... | collective-permute-start | bytes 4718600 | tf_op jit(solution)/shard_map/ppermute | solution.py:464
  69.9 1.1 cut_tails.1
  71.1 1.9 %collective-permute-start.1 = (bf16[512,768]{1,0:T(8,128)(2,1)S(1)}, bf16[512,768]{1,0:T(8,128)(2,1)S(1)}, u32[]{:S(2)}, u32[]{:S(2)}) collective-permute-start(bf16[512,768]{1,0:T(8,128)(2,1)S(1)} %cut_tails.1), channel_id=1, source_target_pairs={{0,4},{4,8},{8,12},{12,16},{16,20},{20,24},{24,28},{28,32},{32,36}... | collective-permute-start | bytes 2359304 | tf_op jit(solution)/shard_map/ppermute | solution.py:451
  73.0 5.6 %gather_pieces.1 = bf16[32,56,8,128]{3,2,1,0:T(8,128)(2,1)} custom-call(bf16[32,57,8,128]{3,2,1,0:T(8,128)(2,1)} %all-to-all-done.store_ref), custom_call_target="tpu_custom_call" | custom-call | flops 6000000000 | tf_op jit(solution)/shard_map/gather_pieces/pallas_call | solution.py:170
  78.6 6.7 %all-to-all-start.1 = ((bf16[32,56,8,128]{3,2,1,0:T(8,128)(2,1)}), bf16[32,56,8,128]{3,2,1,0:T(8,128)(2,1)}, u32[]{:S(2)}, u32[]{:S(2)}) async-start(bf16[32,56,8,128]{3,2,1,0:T(8,128)(2,1)} %gather_pieces.1), calls=%async_computation.1 | async-start | bytes 7340032 | tf_op jit(solution)/shard_map/all_to_all | solution.py:468
  85.3 46.3 %collective-permute-done.1.kv_ref = bf16[512,768]{1,0:T(8,128)(2,1)S(1)} collective-permute-done((bf16[512,768]{1,0:T(8,128)(2,1)S(1)}, bf16[512,768]{1,0:T(8,128)(2,1)S(1)}, u32[]{:S(2)}, u32[]{:S(2)}) %collective-permute-start.1) | collective-permute-done | bytes 786464 | tf_op jit(solution)/shard_map/ppermute | solution.py:451
  131.6 2.0 %copy-done.4 = bf16[1024,1792]{1,0:T(8,128)(2,1)S(1)} copy-done((bf16[1024,1792]{1,0:T(8,128)(2,1)S(1)}, bf16[1024,1792]{1,0:T(8,128)(2,1)}, u32[]{:S(2)}) %copy-start.4) | copy-done | bytes 3670040
  133.6 1.4 near_attention.1.near_ref
  135.0 0.7 copy-done.7
  135.7 3.2 %merge_local.1.local_hbm = bf16[1024,1792]{1,0:T(8,128)(2,1)} custom-call(s32[1]{0:T(128)} %bitcast.5.first_ref, f32[512,1792]{1,0:T(8,128)S(1)} %copy-done.7, f32[512,128]{1,0:T(8,128)S(1)} %get-tuple-element.46.lse_ref, bf16[512,512]{1,0:T(8,128)(2,1)S(1)} %near_attention.1.near_ref, ...), custom_call_target="tpu_custom_call", output_to_operand_aliasing={{}: (5, {})} | custom-call | flops 60000002048 | tf_op jit(solution)/shard_map/merge_local/pallas_call | solution.py:348
  138.9 8.7 %final_attention.1 = bf16[1024,1792]{1,0:T(8,128)(2,1)} custom-call(f32[14]{0:T(128)S(1)} %add_divide_fusion.gate_ref, bf16[1024,1792]{1,0:T(8,128)(2,1)} %q_hbm.1, bf16[32,56,8,128]{3,2,1,0:T(8,128)(2,1)} %all-to-all-done.1.kv_hbm, bf16[1024,1792]{1,0:T(8,128)(2,1)} %merge_local.1.local_hbm), custom_call_target="tpu_custom_call" | custom-call | flops 7000000000 | tf_op jit(solution)/shard_map/final_attention/pallas_call | solution.py:412
  (21 shorter events, 0.1 us)
Async XLA Ops:
  0.0 4.7 %copy-start.8 = (s32[2,14,2]{1,2,0:T(2,128)S(1)}, s32[2,14,2]{1,2,0:T(2,128)}, u32[]{:S(2)}) copy-start(s32[2,14,2]{1,2,0:T(2,128)} %param.14) | copy-start | bytes 676
  1.4 61.1 %collective-permute-start = (bf16[512,1408]{1,0:T(8,128)(2,1)S(1)}, bf16[512,1408]{1,0:T(8,128)(2,1)S(1)}, u32[]{:S(2)}, u32[]{:S(2)}) collective-permute-start(bf16[512,1408]{1,0:T(8,128)(2,1)S(1)} %cut_queries.1), channel_id=1, source_target_pairs={{4,0},{8,4},{12,8},{16,12},{20,16},{24,20},{28,24},{32,28},{36,32}... | collective-permute-start | bytes 4325384 | tf_op jit(solution)/shard_map/ppermute | solution.py:443
  8.1 64.9 %all-to-all-start = ((bf16[32,57,8,128]{3,2,1,0:T(8,128)(2,1)}), bf16[32,57,8,128]{3,2,1,0:T(8,128)(2,1)}, u32[]{:S(2)}, u32[]{:S(2)}) async-start(bf16[32,57,8,128]{3,2,1,0:T(8,128)(2,1)} %pack_pieces.1), calls=%async_computation | async-start | bytes 7471104 | tf_op jit(solution)/shard_map/all_to_all | solution.py:452
  15.5 2.0 %copy-start = (bf16[1024,1792]{1,0:T(8,128)(2,1)S(1)}, bf16[1024,1792]{1,0:T(8,128)(2,1)}, u32[]{:S(2)}) copy-start(bf16[1024,1792]{1,0:T(8,128)(2,1)} %refs_0_.2) | copy-start | bytes 11010052
  17.5 2.0 %copy-start.2 = (bf16[1024,1792]{1,0:T(8,128)(2,1)S(1)}, bf16[1024,1792]{1,0:T(8,128)(2,1)}, u32[]{:S(2)}) copy-start(bf16[1024,1792]{1,0:T(8,128)(2,1)} %refs_1_) | copy-start | bytes 11010052
  19.6 2.0 %copy-start.3 = (bf16[1024,1792]{1,0:T(8,128)(2,1)S(1)}, bf16[1024,1792]{1,0:T(8,128)(2,1)}, u32[]{:S(2)}) copy-start(bf16[1024,1792]{1,0:T(8,128)(2,1)} %q_hbm.1) | copy-start | bytes 11010052
  21.6 40.9 %copy-start.1 = (bf16[1024,1792]{1,0:T(8,128)(2,1)S(1)}, bf16[1024,1792]{1,0:T(8,128)(2,1)}, u32[]{:S(2)}) copy-start(bf16[1024,1792]{1,0:T(8,128)(2,1)} %refs_0_.2) | copy-start | bytes 11010052
  36.3 31.6 %copy-start.5 = (bf16[1024,1792]{1,0:T(8,128)(2,1)}, bf16[1024,1792]{1,0:T(8,128)(2,1)S(1)}, u32[]{:S(2)}) copy-start(bf16[1024,1792]{1,0:T(8,128)(2,1)S(1)} %get-tuple-element.50.into_ref) | copy-start | bytes 11010052
  36.3 31.6 %copy-start.6 = (f32[512,1792]{1,0:T(8,128)}, f32[512,1792]{1,0:T(8,128)S(1)}, u32[]{:S(2)}) copy-start(f32[512,1792]{1,0:T(8,128)S(1)} %get-tuple-element.45.low_ref) | copy-start | bytes 11010052
  67.9 5.1 %copy-start.9 = (f32[14]{0:T(128)S(1)}, f32[14]{0:T(128)}, u32[]{:S(2)}) copy-start(f32[14]{0:T(128)} %param.15) | copy-start | bytes 172
  67.9 67.1 %collective-permute-start.2 = (bf16[512,1536]{1,0:T(8,128)(2,1)}, bf16[512,1536]{1,0:T(8,128)(2,1)S(1)}, u32[]{:S(2)}, u32[]{:S(2)}) collective-permute-start(bf16[512,1536]{1,0:T(8,128)(2,1)} %far_attention.1), channel_id=1, source_target_pairs={{0,4},{4,8},{8,12},{12,16},{16,20},{20,24},{24,28},{28,32},{32,36}... | collective-permute-start | bytes 4718600 | tf_op jit(solution)/shard_map/ppermute | solution.py:464
  71.1 60.5 %collective-permute-start.1 = (bf16[512,768]{1,0:T(8,128)(2,1)S(1)}, bf16[512,768]{1,0:T(8,128)(2,1)S(1)}, u32[]{:S(2)}, u32[]{:S(2)}) collective-permute-start(bf16[512,768]{1,0:T(8,128)(2,1)S(1)} %cut_tails.1), channel_id=1, source_target_pairs={{0,4},{4,8},{8,12},{12,16},{16,20},{20,24},{24,28},{28,32},{32,36}... | collective-permute-start | bytes 2359304 | tf_op jit(solution)/shard_map/ppermute | solution.py:451
  78.6 60.2 %all-to-all-start.1 = ((bf16[32,56,8,128]{3,2,1,0:T(8,128)(2,1)}), bf16[32,56,8,128]{3,2,1,0:T(8,128)(2,1)}, u32[]{:S(2)}, u32[]{:S(2)}) async-start(bf16[32,56,8,128]{3,2,1,0:T(8,128)(2,1)} %gather_pieces.1), calls=%async_computation.1 | async-start | bytes 7340032 | tf_op jit(solution)/shard_map/all_to_all | solution.py:468
  131.6 2.0 %copy-start.4 = (bf16[1024,1792]{1,0:T(8,128)(2,1)S(1)}, bf16[1024,1792]{1,0:T(8,128)(2,1)}, u32[]{:S(2)}) copy-start(bf16[1024,1792]{1,0:T(8,128)(2,1)} %q_hbm.1) | copy-start | bytes 11010052
  133.6 2.0 %copy-start.7 = (f32[512,1792]{1,0:T(8,128)S(1)}, f32[512,1792]{1,0:T(8,128)}, u32[]{:S(2)}) copy-start(f32[512,1792]{1,0:T(8,128)} %copy-done.6) | copy-start | bytes 11010052

commit v9 on v4

--- a/solution.py
+++ b/solution.py
@@ -16,9 +16,9 @@
 EDGE = 256
 FORWARD = 5
 HALVES = 2
+DEPTH = 2
 LOG2E = 1.4426950408889634
 NEG = -1e30
-VMEM_LIMIT = 40 << 20
 BF = jnp.bfloat16
 F32 = jnp.float32
 ANY = pl.BlockSpec(memory_space=pl.ANY)
@@ -26,8 +26,8 @@
 SMALL = pl.BlockSpec(memory_space=pltpu.SMEM)
 
 
-def params():
-    return pltpu.CompilerParams(vmem_limit_bytes=VMEM_LIMIT)
+def params(mebibytes):
+    return pltpu.CompilerParams(vmem_limit_bytes=mebibytes << 20)
 
 
 def cost(micros):
@@ -75,7 +75,7 @@
         in_specs=[ANY] * 3,
         out_specs=(WHOLE, WHOLE),
         scratch_shapes=[pltpu.SemaphoreType.DMA((3,))],
-        compiler_params=params(),
+        compiler_params=params(8),
         cost_estimate=cost(2),
         name="cut_edges",
     )(in_hbm(queries), in_hbm(keys), in_hbm(values))
@@ -123,7 +123,7 @@
             pltpu.SemaphoreType.DMA((2 * blocks,)),
             pltpu.SemaphoreType.DMA((2 * blocks + 1,)),
         ],
-        compiler_params=params(),
+        compiler_params=params(8),
         cost_estimate=cost(2),
         name="pack_pieces",
     )(
@@ -192,7 +192,7 @@
             pltpu.SemaphoreType.DMA((4,)),
             pltpu.SemaphoreType.DMA((8,)),
         ],
-        compiler_params=params(),
+        compiler_params=params(16),
         cost_estimate=cost(6),
         name="gather_pieces",
     )(in_hbm(store))
@@ -265,7 +265,7 @@
         ),
         in_specs=[WHOLE] * 3,
         out_specs=(WHOLE,) * 3,
-        compiler_params=params(),
+        compiler_params=params(30),
         cost_estimate=cost(1),
         name="own_attention",
     )(queries, keys, values)
@@ -324,7 +324,7 @@
         in_specs=[WHOLE] * 5,
         out_specs=(WHOLE,) * 2,
         scratch_shapes=[pltpu.VMEM((WIN, DH), F32)],
-        compiler_params=params(),
+        compiler_params=params(24),
         cost_estimate=cost(60),
         name="edge_attention",
     )(far_q, near_kv, queries, keys, values)
@@ -365,7 +365,7 @@
         in_specs=[SMALL, whole(low), whole(lse), whole(near), whole(far), ANY],
         out_specs=pl.BlockSpec((WIN, width), lambda i: (0, 0)),
         input_output_aliases={5: 0},
-        compiler_params=params(),
+        compiler_params=params(16),
         cost_estimate=cost(60),
         name="merge_local",
     )(first, low, lse, near, far, in_hbm(local))
@@ -392,14 +392,14 @@
             ]
         )
         stores.append(pltpu.make_async_copy(out_ref.at[area], out_hbm.at[area], out_sems.at[index]))
-    for index in range(2):
+    for index in range(DEPTH):
         for load in loads[index]:
             load.start()
     for index, (block, half) in enumerate(chunks):
         for load in loads[index]:
             load.wait()
-        if index + 2 < len(chunks):
-            for load in loads[index + 2]:
+        if index + DEPTH < len(chunks):
+            for load in loads[index + DEPTH]:
                 load.start()
         rows = pl.ds(block * QB, QB)
         for head in range(half * step, (half + 1) * step):
@@ -435,7 +435,7 @@
             pltpu.SemaphoreType.DMA((chunks, 3)),
             pltpu.SemaphoreType.DMA((chunks,)),
         ],
-        compiler_params=params(),
+        compiler_params=params(24),
         cost_estimate=cost(7),
         name="final_attention",
     )(gate, in_hbm(queries), in_hbm(kv), in_hbm(local))
@@ -462,13 +462,14 @@
     gate_share = 1.0 / (1.0 + jnp.exp(-gate_bias))
     first = lax.axis_index("seq").reshape(1).astype(jnp.int32)
     low, lse, local = own_attention(queries, token_keys, token_values, heads, scale)
-    far_part, near = edge_attention(
-        far_q, near_kv, queries, token_keys, token_values, heads, scale
-    )
-    store, low, lse, local, far_part, near = lax.optimization_barrier(
-        (store, low, lse, local, far_part, near)
-    )
+    low, edge_q, edge_k, edge_v = lax.optimization_barrier(
+        (low, queries, token_keys, token_values)
+    )
+    far_part, near = edge_attention(far_q, near_kv, edge_q, edge_k, edge_v, heads, scale)
     far = lax.ppermute(far_part, "seq", upward)
+    store, low, lse, local, near, _ = lax.optimization_barrier(
+        (store, low, lse, local, near, far_part)
+    )
     pieces = gather(store, blocks, heads, wanted)
     kv = lax.all_to_all(pieces, "seq", split_axis=0, concat_axis=0, tiled=True)
     local = merge(first, low, lse, near, far, local, heads)

time: 141 us -> 138 us (0.979)
  Pallas kernels: 48.8 us -> 44.4 us
  waiting for transfers between devices: 57.4 us -> 59.4 us
  starting transfers between devices: 24.1 us -> 22.5 us
    pallas_call x1, Pallas kernels: 17.9 us -> 14.6 us  [own_attention(): pl.pallas_call(functools.partial(own_kernel, scale, heads), out_shape=(ja...]
    ppermute x1, waiting for transfers between devices: 2.37 us -> 5.4 us  [body(): far_q = lax.ppermute(back_q, 'seq', downward)]
    all_to_all x1, starting transfers between devices: 7.98 us -> 6.37 us  [body(): kv = lax.all_to_all(pieces, 'seq', split_axis=0, concat_axis=0, tiled=True)]
    unnamed x18 -> x24, local copies, waits for them, and re-layouts: 9.93 us -> 10.2 us
  transfers between devices with their start and end apart: 5 -> 5, of which waited for: 4 -> 3; matrix products, arithmetic and copies ran while one was open for 0% -> 0% of each run, Pallas kernels for 27% -> 24%
where the time goes in v9:
time: 138 us; the launch traced here: 137 us
  waiting for transfers between devices  59.4 us (43%)
  Pallas kernels  44.4 us (32%)
  starting transfers between devices  22.5 us (16%)
  local copies, waits for them, and re-layouts  10.4 us (8%)
    all_to_all x1, waiting for transfers between devices, body(): kv = lax.all_to_all(pieces, 'seq', split_axis=0, concat_axis=0, tiled=True)  39.6 us
    pallas_call x1, Pallas kernels, own_attention(): pl.pallas_call(functools.partial(own_kernel, scale, heads), out_shape=(ja...  14.6 us
    all_to_all x1, waiting for transfers between devices, body(): store = lax.all_to_all(sent, 'seq', split_axis=0, concat_axis=0, tiled=True)  14.4 us
    unnamed x24, local copies, waits for them, and re-layouts  10.2 us
    pallas_call x1, Pallas kernels, final_attention(): pl.pallas_call(functools.partial(final_kernel, scale, heads), out_shape=p...  8.66 us
    all_to_all x1, starting transfers between devices, body(): store = lax.all_to_all(sent, 'seq', split_axis=0, concat_axis=0, tiled=True)  7.7 us
    pallas_call x1, Pallas kernels, edge_attention(): pl.pallas_call(functools.partial(edge_kernel, scale, heads), out_shape=(j...  6.5 us
    all_to_all x1, starting transfers between devices, body(): kv = lax.all_to_all(pieces, 'seq', split_axis=0, concat_axis=0, tiled=True)  6.37 us
  transfers between devices with their start and end apart: 5, of which 3 were waited for; matrix products, arithmetic and copies ran while one was open for 0% of the time, Pallas kernels for 24%

profile of v9, /device:TPU:1, one launch (start us, length us, event | category | flops | bytes accessed | tf_op | source)
XLA Modules:
  0.0 137.1 jit_solution(15462835793401404624)
XLA Ops:
  0.0 2.7 %cut_edges.1 = (bf16[512,1152]{1,0:T(8,128)(2,1)}, bf16[512,1280]{1,0:T(8,128)(2,1)S(1)}) custom-call(bf16[1024,1792]{1,0:T(8,128)(2,1)} %q_hbm.1, bf16[1024,1792]{1,0:T(8,128)(2,1)} %k_ref.4, bf16[1024,1792]{1,0:T(8,128)(2,1)} %v_ref.4), custom_call_target="tpu_custom_call" | custom-call | flops 2000000000 | tf_op jit(solution)/shard_map/cut_edges/pallas_call | solution.py:69
  2.7 4.6 %collective-permute-start.1 = (bf16[512,1280]{1,0:T(8,128)(2,1)S(1)}, bf16[512,1280]{1,0:T(8,128)(2,1)S(1)}, u32[]{:S(2)}, u32[]{:S(2)}) collective-permute-start(bf16[512,1280]{1,0:T(8,128)(2,1)S(1)} %get-tuple-element.42), channel_id=1, source_target_pairs={{0,4},{4,8},{8,12},{12,16},{16,20},{20,24},{24,28},{28,32},{32,36}... | collective-permute-start | bytes 3932168 | tf_op jit(solution)/shard_map/ppermute | solution.py:456
  7.3 1.9 %collective-permute-start = (bf16[512,1152]{1,0:T(8,128)(2,1)}, bf16[512,1152]{1,0:T(8,128)(2,1)}, u32[]{:S(2)}, u32[]{:S(2)}) collective-permute-start(bf16[512,1152]{1,0:T(8,128)(2,1)} %get-tuple-element.36), channel_id=1, source_target_pairs={{4,0},{8,4},{12,8},{16,12},{20,16},{24,20},{28,24},{32,28},{36,32}... | collective-permute-start | bytes 3538952 | tf_op jit(solution)/shard_map/ppermute | solution.py:455
  9.3 0.1 copy.10
  9.4 0.1 convert_element_type.7
  9.5 3.1 %pack_pieces.1 = bf16[32,57,8,128]{3,2,1,0:T(8,128)(2,1)} custom-call(bf16[64,14,8,128]{3,2,1,0:T(8,128)(2,1)} %bitcast.9, bf16[64,14,8,128]{3,2,1,0:T(8,128)(2,1)} %bitcast.10, bf16[32,1,8,128]{3,2,1,0:T(8,128)(2,1)S(1)} %broadcast_in_dim.4.ids_ref), custom_call_target="tpu_custom_call" | custom-call | flops 2000000000 | tf_op jit(solution)/shard_map/pack_pieces/pallas_call | solution.py:116
  12.6 7.7 %all-to-all-start = ((bf16[32,57,8,128]{3,2,1,0:T(8,128)(2,1)}), bf16[32,57,8,128]{3,2,1,0:T(8,128)(2,1)}, u32[]{:S(2)}, u32[]{:S(2)}) async-start(bf16[32,57,8,128]{3,2,1,0:T(8,128)(2,1)} %pack_pieces.1), calls=%async_computation | async-start | bytes 7471104 | tf_op jit(solution)/shard_map/all_to_all | solution.py:461
  20.3 0.0 copy-start
  20.3 2.0 %copy-done = bf16[1024,1792]{1,0:T(8,128)(2,1)S(1)} copy-done((bf16[1024,1792]{1,0:T(8,128)(2,1)S(1)}, bf16[1024,1792]{1,0:T(8,128)(2,1)}, u32[]{:S(2)}) %copy-start) | copy-done | bytes 3670040
  22.4 2.0 %copy-done.2 = bf16[1024,1792]{1,0:T(8,128)(2,1)S(1)} copy-done((bf16[1024,1792]{1,0:T(8,128)(2,1)S(1)}, bf16[1024,1792]{1,0:T(8,128)(2,1)}, u32[]{:S(2)}) %copy-start.2) | copy-done | bytes 3670040
  24.4 2.0 %copy-done.4 = bf16[1024,1792]{1,0:T(8,128)(2,1)S(1)} copy-done((bf16[1024,1792]{1,0:T(8,128)(2,1)S(1)}, bf16[1024,1792]{1,0:T(8,128)(2,1)}, u32[]{:S(2)}) %copy-start.4) | copy-done | bytes 3670040
  26.5 14.6 %own_attention.1 = (f32[512,1792]{1,0:T(8,128)S(1)}, f32[512,128]{1,0:T(8,128)S(1)}, bf16[1024,1792]{1,0:T(8,128)(2,1)S(1)}) custom-call(bf16[1024,1792]{1,0:T(8,128)(2,1)S(1)} %copy-done.4, bf16[1024,1792]{1,0:T(8,128)(2,1)S(1)} %copy-done, bf16[1024,1792]{1,0:T(8,128)(2,1)S(1)} %copy-done.2), custom_call_target="tpu_custom_call" | custom-call | flops 1000000000 | tf_op jit(solution)/shard_map/own_attention/pallas_call | solution.py:259
  41.1 5.4 %collective-permute-done.far_q_ref = bf16[512,1152]{1,0:T(8,128)(2,1)} collective-permute-done((bf16[512,1152]{1,0:T(8,128)(2,1)}, bf16[512,1152]{1,0:T(8,128)(2,1)}, u32[]{:S(2)}, u32[]{:S(2)}) %collective-permute-start) | collective-permute-done | bytes 1179680 | tf_op jit(solution)/shard_map/ppermute | solution.py:455
  46.6 6.5 %edge_attention.1 = (bf16[512,1280]{1,0:T(8,128)(2,1)S(1)}, bf16[512,768]{1,0:T(8,128)(2,1)S(1)}) custom-call(bf16[512,1152]{1,0:T(8,128)(2,1)} %collective-permute-done.far_q_ref, bf16[512,1280]{1,0:T(8,128)(2,1)S(1)} %collective-permute-done.1.near_kv_ref, bf16[1024,1792]{1,0:T(8,128)(2,1)S(1)} %copy-done.4, bf16[1024,1792]{1,0:T(8,128)(2,1)S(1)} %copy-done.1, ...), custom_call_target="tpu_custom_call" | custom-call | flops 60000002048 | tf_op jit(solution)/shard_map/edge_attention/pallas_call | solution.py:318
  53.1 0.9 copy-done.8
  54.0 1.9 %collective-permute-start.2 = (bf16[512,1280]{1,0:T(8,128)(2,1)S(1)}, bf16[512,1280]{1,0:T(8,128)(2,1)S(1)}, u32[]{:S(2)}, u32[]{:S(2)}) collective-permute-start(bf16[512,1280]{1,0:T(8,128)(2,1)S(1)} %get-tuple-element.47), channel_id=1, source_target_pairs={{0,4},{4,8},{8,12},{12,16},{16,20},{20,24},{24,28},{28,32},{32,36}... | collective-permute-start | bytes 3932168 | tf_op jit(solution)/shard_map/ppermute | solution.py:469
  55.9 14.4 %all-to-all-done.store_ref = bf16[32,57,8,128]{3,2,1,0:T(8,128)(2,1)} async-done(((bf16[32,57,8,128]{3,2,1,0:T(8,128)(2,1)}), bf16[32,57,8,128]{3,2,1,0:T(8,128)(2,1)}, u32[]{:S(2)}, u32[]{:S(2)}) %all-to-all-start) | async-done | bytes 3735584 | tf_op jit(solution)/shard_map/all_to_all | solution.py:461
  70.3 5.6 %gather_pieces.1 = bf16[32,56,8,128]{3,2,1,0:T(8,128)(2,1)} custom-call(bf16[32,57,8,128]{3,2,1,0:T(8,128)(2,1)} %all-to-all-done.store_ref), custom_call_target="tpu_custom_call" | custom-call | flops 6000000000 | tf_op jit(solution)/shard_map/gather_pieces/pallas_call | solution.py:180
  75.9 6.4 %all-to-all-start.1 = ((bf16[32,56,8,128]{3,2,1,0:T(8,128)(2,1)}), bf16[32,56,8,128]{3,2,1,0:T(8,128)(2,1)}, u32[]{:S(2)}, u32[]{:S(2)}) async-start(bf16[32,56,8,128]{3,2,1,0:T(8,128)(2,1)} %gather_pieces.1), calls=%async_computation.1 | async-start | bytes 7340032 | tf_op jit(solution)/shard_map/all_to_all | solution.py:474
  82.3 2.0 %copy-done.6 = f32[512,1792]{1,0:T(8,128)S(1)} copy-done((f32[512,1792]{1,0:T(8,128)S(1)}, f32[512,1792]{1,0:T(8,128)}, u32[]{:S(2)}) %copy-start.6) | copy-done | bytes 3670040
  84.3 1.1 copy-done.9
  85.4 3.2 %merge_local.1.local_hbm = bf16[1024,1792]{1,0:T(8,128)(2,1)} custom-call(s32[1]{0:T(128)} %bitcast.5.first_ref, f32[512,1792]{1,0:T(8,128)S(1)} %copy-done.6, f32[512,128]{1,0:T(8,128)S(1)} %get-tuple-element.50.lse_ref, bf16[512,768]{1,0:T(8,128)(2,1)S(1)} %copy-done.9, ...), custom_call_target="tpu_custom_call", output_to_operand_aliasing={{}: (5, {})} | custom-call | flops 60000002048 | tf_op jit(solution)/shard_map/merge_local/pallas_call | solution.py:361
  88.6 39.6 %all-to-all-done.1.kv_hbm = bf16[32,56,8,128]{3,2,1,0:T(8,128)(2,1)} async-done(((bf16[32,56,8,128]{3,2,1,0:T(8,128)(2,1)}), bf16[32,56,8,128]{3,2,1,0:T(8,128)(2,1)}, u32[]{:S(2)}, u32[]{:S(2)}) %all-to-all-start.1) | async-done | bytes 3670048 | tf_op jit(solution)/shard_map/all_to_all | solution.py:474
  128.2 8.7 %final_attention.1 = bf16[1024,1792]{1,0:T(8,128)(2,1)} custom-call(f32[14]{0:T(128)S(1)} %add_divide_fusion.gate_ref, bf16[1024,1792]{1,0:T(8,128)(2,1)} %q_hbm.1, bf16[32,56,8,128]{3,2,1,0:T(8,128)(2,1)} %all-to-all-done.1.kv_hbm, bf16[1024,1792]{1,0:T(8,128)(2,1)} %merge_local.1.local_hbm), custom_call_target="tpu_custom_call" | custom-call | flops 7000000000 | tf_op jit(solution)/shard_map/final_attention/pallas_call | solution.py:425
  (23 shorter events, 0.1 us)
Async XLA Ops:
  0.0 9.2 %copy-start.10 = (s32[2,14,2]{1,2,0:T(2,128)S(1)}, s32[2,14,2]{1,2,0:T(2,128)}, u32[]{:S(2)}) copy-start(s32[2,14,2]{1,2,0:T(2,128)} %param.14) | copy-start | bytes 676
  2.7 43.8 %collective-permute-start.1 = (bf16[512,1280]{1,0:T(8,128)(2,1)S(1)}, bf16[512,1280]{1,0:T(8,128)(2,1)S(1)}, u32[]{:S(2)}, u32[]{:S(2)}) collective-permute-start(bf16[512,1280]{1,0:T(8,128)(2,1)S(1)} %get-tuple-element.42), channel_id=1, source_target_pairs={{0,4},{4,8},{8,12},{12,16},{16,20},{20,24},{24,28},{28,32},{32,36}... | collective-permute-start | bytes 3932168 | tf_op jit(solution)/shard_map/ppermute | solution.py:456
  7.3 39.2 %collective-permute-start = (bf16[512,1152]{1,0:T(8,128)(2,1)}, bf16[512,1152]{1,0:T(8,128)(2,1)}, u32[]{:S(2)}, u32[]{:S(2)}) collective-permute-start(bf16[512,1152]{1,0:T(8,128)(2,1)} %get-tuple-element.36), channel_id=1, source_target_pairs={{4,0},{8,4},{12,8},{16,12},{20,16},{24,20},{28,24},{32,28},{36,32}... | collective-permute-start | bytes 3538952 | tf_op jit(solution)/shard_map/ppermute | solution.py:455
  12.6 57.7 %all-to-all-start = ((bf16[32,57,8,128]{3,2,1,0:T(8,128)(2,1)}), bf16[32,57,8,128]{3,2,1,0:T(8,128)(2,1)}, u32[]{:S(2)}, u32[]{:S(2)}) async-start(bf16[32,57,8,128]{3,2,1,0:T(8,128)(2,1)} %pack_pieces.1), calls=%async_computation | async-start | bytes 7471104 | tf_op jit(solution)/shard_map/all_to_all | solution.py:461
  20.3 2.0 %copy-start = (bf16[1024,1792]{1,0:T(8,128)(2,1)S(1)}, bf16[1024,1792]{1,0:T(8,128)(2,1)}, u32[]{:S(2)}) copy-start(bf16[1024,1792]{1,0:T(8,128)(2,1)} %k_ref.4) | copy-start | bytes 11010052
  22.4 2.0 %copy-start.2 = (bf16[1024,1792]{1,0:T(8,128)(2,1)S(1)}, bf16[1024,1792]{1,0:T(8,128)(2,1)}, u32[]{:S(2)}) copy-start(bf16[1024,1792]{1,0:T(8,128)(2,1)} %v_ref.4) | copy-start | bytes 11010052
  24.4 2.0 %copy-start.4 = (bf16[1024,1792]{1,0:T(8,128)(2,1)S(1)}, bf16[1024,1792]{1,0:T(8,128)(2,1)}, u32[]{:S(2)}) copy-start(bf16[1024,1792]{1,0:T(8,128)(2,1)} %q_hbm.1) | copy-start | bytes 11010052
  26.5 20.1 %copy-start.1 = (bf16[1024,1792]{1,0:T(8,128)(2,1)S(1)}, bf16[1024,1792]{1,0:T(8,128)(2,1)}, u32[]{:S(2)}) copy-start(bf16[1024,1792]{1,0:T(8,128)(2,1)} %k_ref.4) | copy-start | bytes 11010052
  26.5 20.1 %copy-start.3 = (bf16[1024,1792]{1,0:T(8,128)(2,1)S(1)}, bf16[1024,1792]{1,0:T(8,128)(2,1)}, u32[]{:S(2)}) copy-start(bf16[1024,1792]{1,0:T(8,128)(2,1)} %v_ref.4) | copy-start | bytes 11010052
  41.1 12.0 %copy-start.5 = (f32[512,1792]{1,0:T(8,128)}, f32[512,1792]{1,0:T(8,128)S(1)}, u32[]{:S(2)}) copy-start(f32[512,1792]{1,0:T(8,128)S(1)} %get-tuple-element.49.low_ref) | copy-start | bytes 11010052
  41.1 12.0 %copy-start.7 = (bf16[1024,1792]{1,0:T(8,128)(2,1)}, bf16[1024,1792]{1,0:T(8,128)(2,1)S(1)}, u32[]{:S(2)}) copy-start(bf16[1024,1792]{1,0:T(8,128)(2,1)S(1)} %get-tuple-element.52.into_ref) | copy-start | bytes 11010052
  41.1 14.8 %copy-start.11 = (f32[14]{0:T(128)S(1)}, f32[14]{0:T(128)}, u32[]{:S(2)}) copy-start(f32[14]{0:T(128)} %param.15) | copy-start | bytes 172
  53.1 0.9 copy-start.8
  54.0 28.3 %collective-permute-start.2 = (bf16[512,1280]{1,0:T(8,128)(2,1)S(1)}, bf16[512,1280]{1,0:T(8,128)(2,1)S(1)}, u32[]{:S(2)}, u32[]{:S(2)}) collective-permute-start(bf16[512,1280]{1,0:T(8,128)(2,1)S(1)} %get-tuple-element.47), channel_id=1, source_target_pairs={{0,4},{4,8},{8,12},{12,16},{16,20},{20,24},{24,28},{28,32},{32,36}... | collective-permute-start | bytes 3932168 | tf_op jit(solution)/shard_map/ppermute | solution.py:469
  75.9 52.4 %all-to-all-start.1 = ((bf16[32,56,8,128]{3,2,1,0:T(8,128)(2,1)}), bf16[32,56,8,128]{3,2,1,0:T(8,128)(2,1)}, u32[]{:S(2)}, u32[]{:S(2)}) async-start(bf16[32,56,8,128]{3,2,1,0:T(8,128)(2,1)} %gather_pieces.1), calls=%async_computation.1 | async-start | bytes 7340032 | tf_op jit(solution)/shard_map/all_to_all | solution.py:474
  82.3 2.0 %copy-start.6 = (f32[512,1792]{1,0:T(8,128)S(1)}, f32[512,1792]{1,0:T(8,128)}, u32[]{:S(2)}) copy-start(f32[512,1792]{1,0:T(8,128)} %copy-done.5) | copy-start | bytes 11010052
  84.3 1.1 copy-start.9

commit v10 on v9

--- a/solution.py
+++ b/solution.py
@@ -14,7 +14,7 @@
 DH = 128
 PIECE = 8
 EDGE = 256
-FORWARD = 5
+FORWARD = 4
 HALVES = 2
 DEPTH = 2
 LOG2E = 1.4426950408889634
@@ -45,40 +45,31 @@
         copy.wait()
 
 
-def edges_kernel(q_ref, k_ref, v_ref, back_ref, ahead_ref, sems):
-    split = FORWARD * DH
-    tail = pl.ds(k_ref.shape[0] - WIN, WIN)
-    width = q_ref.shape[1] - split
-    copy_all(
-        [
-            pltpu.make_async_copy(
-                q_ref.at[pl.ds(0, WIN), pl.ds(split, width)], back_ref, sems.at[0]
-            ),
-            pltpu.make_async_copy(
-                k_ref.at[tail, pl.ds(0, split)], ahead_ref.at[:, pl.ds(0, split)], sems.at[1]
-            ),
-            pltpu.make_async_copy(
-                v_ref.at[tail, pl.ds(0, split)], ahead_ref.at[:, pl.ds(split, split)], sems.at[2]
-            ),
-        ]
-    )
-
-
-def edges(queries, keys, values):
-    split = FORWARD * DH
-    return pl.pallas_call(
-        edges_kernel,
-        out_shape=(
-            jax.ShapeDtypeStruct((WIN, queries.shape[1] - split), BF),
-            jax.ShapeDtypeStruct((WIN, 2 * split), BF),
-        ),
-        in_specs=[ANY] * 3,
-        out_specs=(WHOLE, WHOLE),
-        scratch_shapes=[pltpu.SemaphoreType.DMA((3,))],
-        compiler_params=params(8),
+def cut_kernel(areas, *refs):
+    out_ref, sems = refs[-2:]
+    width = out_ref.shape[1] // len(areas)
+    copies = [
+        pltpu.make_async_copy(
+            ref.at[pl.ds(row, WIN), pl.ds(col, width)],
+            out_ref.at[:, pl.ds(index * width, width)],
+            sems.at[index],
+        )
+        for index, (ref, (row, col)) in enumerate(zip(refs, areas))
+    ]
+    copy_all(copies)
+
+
+def cut(arrays, areas, width, name):
+    return pl.pallas_call(
+        functools.partial(cut_kernel, areas),
+        out_shape=jax.ShapeDtypeStruct((WIN, width), BF),
+        in_specs=[ANY] * len(arrays),
+        out_specs=WHOLE,
+        scratch_shapes=[pltpu.SemaphoreType.DMA((len(arrays),))],
+        compiler_params=params(4),
         cost_estimate=cost(2),
-        name="cut_edges",
-    )(in_hbm(queries), in_hbm(keys), in_hbm(values))
+        name=name,
+    )(*map(in_hbm, arrays))
 
 
 def pack_kernel(blocks, heads, keys_ref, values_ref, ids_ref, out_ref, stage, in_sems, out_sems):
@@ -451,12 +442,15 @@
     wanted = q_blocks * heads * TOPK
     upward = [(i, i + 1) for i in range(devices - 1)]
     downward = [(i, i - 1) for i in range(1, devices)]
-    back_q, ahead_kv = edges(queries, token_keys, token_values)
+    split = FORWARD * DH
+    tail = tokens - WIN
+    back_q = cut([queries], [(0, split)], heads * DH - split, "cut_queries")
     far_q = lax.ppermute(back_q, "seq", downward)
+    ahead_kv = cut([token_keys, token_values], [(tail, 0)] * 2, 2 * split, "cut_tails")
     near_kv = lax.ppermute(ahead_kv, "seq", upward)
     ids = retrieved.reshape(-1)
     ids_tile = jnp.zeros((PIECE * DH,), BF).at[:wanted].set(ids.astype(BF)).reshape(PIECE, DH)
-    ids_tile, _ = lax.optimization_barrier((ids_tile, back_q))
+    ids_tile, _, _ = lax.optimization_barrier((ids_tile, back_q, ahead_kv))
     sent = pack(mem_keys, mem_values, ids_tile, blocks, heads)
     store = lax.all_to_all(sent, "seq", split_axis=0, concat_axis=0, tiled=True)
     gate_share = 1.0 / (1.0 + jnp.exp(-gate_bias))

time: 138 us -> 138 us (level)
  waiting for transfers between devices: 59.4 us -> 49.8 us
  local copies, waits for them, and re-layouts: 10.4 us -> 16.6 us
  starting transfers between devices: 22.5 us -> 26.1 us
    unnamed x24 -> x36, local copies, waits for them, and re-layouts: 10.2 us -> 16.3 us
    ppermute x1, waiting for transfers between devices: 5.4 us -> 0.01 us  [body(): far_q = lax.ppermute(back_q, 'seq', downward)]
    all_to_all x1, waiting for transfers between devices: 14.4 us -> 10.1 us  [body(): store = lax.all_to_all(sent, 'seq', split_axis=0, concat_axis=0, tiled=True)]
    ppermute x1, starting transfers between devices: 1.91 us -> 3.53 us  [body(): far = lax.ppermute(far_part, 'seq', upward)]
    ppermute x1, starting transfers between devices: 4.59 us -> 3.19 us  [body(): near_kv = lax.ppermute(ahead_kv, 'seq', upward)]
    ppermute x1, starting transfers between devices: 1.92 us -> 3.33 us  [body(): far_q = lax.ppermute(back_q, 'seq', downward)]
    pallas_call x1 -> x2, Pallas kernels: 2.69 us -> 3.6 us  [cut(): pl.pallas_call(functools.partial(cut_kernel, areas), out_shape=jax.ShapeD...]
  transfers between devices with their start and end apart: 5 -> 5, of which waited for: 3 -> 2; matrix products, arithmetic and copies ran while one was open for 0% -> 0% of each run, Pallas kernels for 24% -> 24%
where the time goes in v10:
time: 138 us; the launch traced here: 137 us
  waiting for transfers between devices  49.8 us (36%)
  Pallas kernels  44 us (32%)
  starting transfers between devices  26.1 us (19%)
  local copies, waits for them, and re-layouts  16.6 us (12%)
    all_to_all x1, waiting for transfers between devices, body(): kv = lax.all_to_all(pieces, 'seq', split_axis=0, concat_axis=0, tiled=True)  39.6 us
    unnamed x36, local copies, waits for them, and re-layouts  16.3 us
    pallas_call x1, Pallas kernels, own_attention(): pl.pallas_call(functools.partial(own_kernel, scale, heads), out_shape=(ja...  14.6 us
    all_to_all x1, waiting for transfers between devices, body(): store = lax.all_to_all(sent, 'seq', split_axis=0, concat_axis=0, tiled=True)  10.1 us
    all_to_all x1, starting transfers between devices, body(): store = lax.all_to_all(sent, 'seq', split_axis=0, concat_axis=0, tiled=True)  9.07 us
    pallas_call x1, Pallas kernels, final_attention(): pl.pallas_call(functools.partial(final_kernel, scale, heads), out_shape=p...  8.66 us
    all_to_all x1, starting transfers between devices, body(): kv = lax.all_to_all(pieces, 'seq', split_axis=0, concat_axis=0, tiled=True)  7.02 us
    pallas_call x1, Pallas kernels, gather(): pl.pallas_call(functools.partial(gather_kernel, blocks, heads, wanted), o...  5.57 us
  transfers between devices with their start and end apart: 5, of which 2 were waited for; matrix products, arithmetic and copies ran while one was open for 0% of the time, Pallas kernels for 24%

profile of v10, /device:TPU:1, one launch (start us, length us, event | category | flops | bytes accessed | tf_op | source)
XLA Modules:
  0.0 136.9 jit_solution(4978460710337912274)
XLA Ops:
  0.0 2.4 %cut_queries.1 = bf16[512,1280]{1,0:T(8,128)(2,1)} custom-call(bf16[1024,1792]{1,0:T(8,128)(2,1)} %q_hbm.1), custom_call_target="tpu_custom_call" | custom-call | flops 2000000000 | tf_op jit(solution)/shard_map/cut_queries/pallas_call | solution.py:63
  2.4 3.3 %collective-permute-start = (bf16[512,1280]{1,0:T(8,128)(2,1)}, bf16[512,1280]{1,0:T(8,128)(2,1)S(1)}, u32[]{:S(2)}, u32[]{:S(2)}) collective-permute-start(bf16[512,1280]{1,0:T(8,128)(2,1)} %cut_queries.1), channel_id=1, source_target_pairs={{4,0},{8,4},{12,8},{16,12},{20,16},{24,20},{28,24},{32,28},{36,32}... | collective-permute-start | bytes 3932168 | tf_op jit(solution)/shard_map/ppermute | solution.py:448
  5.7 1.2 cut_tails.1
  7.0 3.2 %collective-permute-start.1 = (bf16[512,1024]{1,0:T(8,128)(2,1)S(1)}, bf16[512,1024]{1,0:T(8,128)(2,1)S(1)}, u32[]{:S(2)}, u32[]{:S(2)}) collective-permute-start(bf16[512,1024]{1,0:T(8,128)(2,1)S(1)} %cut_tails.1), channel_id=1, source_target_pairs={{0,4},{4,8},{8,12},{12,16},{16,20},{20,24},{24,28},{28,32},{32,36}... | collective-permute-start | bytes 3145736 | tf_op jit(solution)/shard_map/ppermute | solution.py:450
  10.4 3.1 %pack_pieces.1 = bf16[32,57,8,128]{3,2,1,0:T(8,128)(2,1)} custom-call(bf16[64,14,8,128]{3,2,1,0:T(8,128)(2,1)} %bitcast.9, bf16[64,14,8,128]{3,2,1,0:T(8,128)(2,1)} %bitcast.10, bf16[32,1,8,128]{3,2,1,0:T(8,128)(2,1)S(1)} %broadcast_in_dim.4.ids_ref), custom_call_target="tpu_custom_call" | custom-call | flops 2000000000 | tf_op jit(solution)/shard_map/pack_pieces/pallas_call | solution.py:107
  13.6 9.1 %all-to-all-start = ((bf16[32,57,8,128]{3,2,1,0:T(8,128)(2,1)}), bf16[32,57,8,128]{3,2,1,0:T(8,128)(2,1)}, u32[]{:S(2)}, u32[]{:S(2)}) async-start(bf16[32,57,8,128]{3,2,1,0:T(8,128)(2,1)} %pack_pieces.1), calls=%async_computation | async-start | bytes 7471104 | tf_op jit(solution)/shard_map/all_to_all | solution.py:455
  22.6 2.0 %copy-done = bf16[1024,1792]{1,0:T(8,128)(2,1)S(1)} copy-done((bf16[1024,1792]{1,0:T(8,128)(2,1)S(1)}, bf16[1024,1792]{1,0:T(8,128)(2,1)}, u32[]{:S(2)}) %copy-start) | copy-done | bytes 3670040
  24.7 2.0 %copy-done.2 = bf16[1024,1792]{1,0:T(8,128)(2,1)S(1)} copy-done((bf16[1024,1792]{1,0:T(8,128)(2,1)S(1)}, bf16[1024,1792]{1,0:T(8,128)(2,1)}, u32[]{:S(2)}) %copy-start.2) | copy-done | bytes 3670040
  26.7 2.0 %copy-done.4 = bf16[1024,1792]{1,0:T(8,128)(2,1)S(1)} copy-done((bf16[1024,1792]{1,0:T(8,128)(2,1)S(1)}, bf16[1024,1792]{1,0:T(8,128)(2,1)}, u32[]{:S(2)}) %copy-start.4) | copy-done | bytes 3670040
  28.8 14.6 %own_attention.1 = (f32[512,1792]{1,0:T(8,128)S(1)}, f32[512,128]{1,0:T(8,128)S(1)}, bf16[1024,1792]{1,0:T(8,128)(2,1)S(1)}) custom-call(bf16[1024,1792]{1,0:T(8,128)(2,1)S(1)} %copy-done.4, bf16[1024,1792]{1,0:T(8,128)(2,1)S(1)} %copy-done, bf16[1024,1792]{1,0:T(8,128)(2,1)S(1)} %copy-done.2), custom_call_target="tpu_custom_call" | custom-call | flops 1000000000 | tf_op jit(solution)/shard_map/own_attention/pallas_call | solution.py:250
  44.1 1.0 copy-done.10
  45.1 1.1 copy-done.8
  46.2 2.3 %copy-done.9 = bf16[512,1280]{1,0:T(8,128)(2,1)S(1)} copy-done((bf16[512,1280]{1,0:T(8,128)(2,1)S(1)}, bf16[512,1280]{1,0:T(8,128)(2,1)}, u32[]{:S(2)}) %copy-start.9) | copy-done | bytes 1310744
  48.5 1.2 copy-done.11
  49.7 5.2 %edge_attention.1 = (bf16[512,1408]{1,0:T(8,128)(2,1)S(1)}, bf16[512,640]{1,0:T(8,128)(2,1)S(1)}) custom-call(bf16[512,1280]{1,0:T(8,128)(2,1)S(1)} %copy-done.9, bf16[512,1024]{1,0:T(8,128)(2,1)S(1)} %copy-done.11, bf16[1024,1792]{1,0:T(8,128)(2,1)S(1)} %copy-done.4, bf16[1024,1792]{1,0:T(8,128)(2,1)S(1)} %copy-done.1, bf16[1024,1792]{1,0:T(8,128)(2,1)S(1)} %copy-done.3), custom_call_target="tpu_custom_call" | custom-call | flops 60000002048 | tf_op jit(solution)/shard_map/edge_attention/pallas_call | solution.py:309
  55.8 3.5 %collective-permute-start.2 = (bf16[512,1408]{1,0:T(8,128)(2,1)S(1)}, bf16[512,1408]{1,0:T(8,128)(2,1)S(1)}, u32[]{:S(2)}, u32[]{:S(2)}) collective-permute-start(bf16[512,1408]{1,0:T(8,128)(2,1)S(1)} %get-tuple-element.43), channel_id=1, source_target_pairs={{0,4},{4,8},{8,12},{12,16},{16,20},{20,24},{24,28},{28,32},{32,36}... | collective-permute-start | bytes 4325384 | tf_op jit(solution)/shard_map/ppermute | solution.py:463
  59.4 10.1 %all-to-all-done.store_ref = bf16[32,57,8,128]{3,2,1,0:T(8,128)(2,1)} async-done(((bf16[32,57,8,128]{3,2,1,0:T(8,128)(2,1)}), bf16[32,57,8,128]{3,2,1,0:T(8,128)(2,1)}, u32[]{:S(2)}, u32[]{:S(2)}) %all-to-all-start) | async-done | bytes 3735584 | tf_op jit(solution)/shard_map/all_to_all | solution.py:455
  69.5 5.6 %gather_pieces.1 = bf16[32,56,8,128]{3,2,1,0:T(8,128)(2,1)} custom-call(bf16[32,57,8,128]{3,2,1,0:T(8,128)(2,1)} %all-to-all-done.store_ref), custom_call_target="tpu_custom_call" | custom-call | flops 6000000000 | tf_op jit(solution)/shard_map/gather_pieces/pallas_call | solution.py:171
  75.1 7.0 %all-to-all-start.1 = ((bf16[32,56,8,128]{3,2,1,0:T(8,128)(2,1)}), bf16[32,56,8,128]{3,2,1,0:T(8,128)(2,1)}, u32[]{:S(2)}, u32[]{:S(2)}) async-start(bf16[32,56,8,128]{3,2,1,0:T(8,128)(2,1)} %gather_pieces.1), calls=%async_computation.1 | async-start | bytes 7340032 | tf_op jit(solution)/shard_map/all_to_all | solution.py:468
  82.1 2.0 %copy-done.6 = f32[512,1792]{1,0:T(8,128)S(1)} copy-done((f32[512,1792]{1,0:T(8,128)S(1)}, f32[512,1792]{1,0:T(8,128)}, u32[]{:S(2)}) %copy-start.6) | copy-done | bytes 3670040
  84.2 1.1 copy-done.15
  85.3 3.2 %merge_local.1.local_hbm = bf16[1024,1792]{1,0:T(8,128)(2,1)} custom-call(s32[1]{0:T(128)} %bitcast.5.first_ref, f32[512,1792]{1,0:T(8,128)S(1)} %copy-done.6, f32[512,128]{1,0:T(8,128)S(1)} %copy-done.13, bf16[512,640]{1,0:T(8,128)(2,1)S(1)} %copy-done.15, bf16[512,1408]{1,0:T(8,128)(2,1)S(1)} %collective-permute-done.2.far_ref, ...), custom_call_target="tpu_custom_call", output_to_operand_aliasing={{}: (5, {})} | custom-call | flops 60000002048 | tf_op jit(solution)/shard_map/merge_local/pallas_call | solution.py:352
  88.4 39.6 %all-to-all-done.1.kv_hbm = bf16[32,56,8,128]{3,2,1,0:T(8,128)(2,1)} async-done(((bf16[32,56,8,128]{3,2,1,0:T(8,128)(2,1)}), bf16[32,56,8,128]{3,2,1,0:T(8,128)(2,1)}, u32[]{:S(2)}, u32[]{:S(2)}) %all-to-all-start.1) | async-done | bytes 3670048 | tf_op jit(solution)/shard_map/all_to_all | solution.py:468
  128.1 8.7 %final_attention.1 = bf16[1024,1792]{1,0:T(8,128)(2,1)} custom-call(f32[14]{0:T(128)S(1)} %add_divide_fusion.gate_ref, bf16[1024,1792]{1,0:T(8,128)(2,1)} %q_hbm.1, bf16[32,56,8,128]{3,2,1,0:T(8,128)(2,1)} %all-to-all-done.1.kv_hbm, bf16[1024,1792]{1,0:T(8,128)(2,1)} %merge_local.1.local_hbm), custom_call_target="tpu_custom_call" | custom-call | flops 7000000000 | tf_op jit(solution)/shard_map/final_attention/pallas_call | solution.py:416
  (36 shorter events, 1.8 us)
Async XLA Ops:
  2.4 7.8 %copy-start.16 = (s32[2,14,2]{1,2,0:T(2,128)S(1)}, s32[2,14,2]{1,2,0:T(2,128)}, u32[]{:S(2)}) copy-start(s32[2,14,2]{1,2,0:T(2,128)} %param.14) | copy-start | bytes 676
  2.4 42.7 %collective-permute-start = (bf16[512,1280]{1,0:T(8,128)(2,1)}, bf16[512,1280]{1,0:T(8,128)(2,1)S(1)}, u32[]{:S(2)}, u32[]{:S(2)}) collective-permute-start(bf16[512,1280]{1,0:T(8,128)(2,1)} %cut_queries.1), channel_id=1, source_target_pairs={{4,0},{8,4},{12,8},{16,12},{20,16},{24,20},{28,24},{32,28},{36,32}... | collective-permute-start | bytes 3932168 | tf_op jit(solution)/shard_map/ppermute | solution.py:448
  7.0 37.1 %collective-permute-start.1 = (bf16[512,1024]{1,0:T(8,128)(2,1)S(1)}, bf16[512,1024]{1,0:T(8,128)(2,1)S(1)}, u32[]{:S(2)}, u32[]{:S(2)}) collective-permute-start(bf16[512,1024]{1,0:T(8,128)(2,1)S(1)} %cut_tails.1), channel_id=1, source_target_pairs={{0,4},{4,8},{8,12},{12,16},{16,20},{20,24},{24,28},{28,32},{32,36}... | collective-permute-start | bytes 3145736 | tf_op jit(solution)/shard_map/ppermute | solution.py:450
  13.6 55.9 %all-to-all-start = ((bf16[32,57,8,128]{3,2,1,0:T(8,128)(2,1)}), bf16[32,57,8,128]{3,2,1,0:T(8,128)(2,1)}, u32[]{:S(2)}, u32[]{:S(2)}) async-start(bf16[32,57,8,128]{3,2,1,0:T(8,128)(2,1)} %pack_pieces.1), calls=%async_computation | async-start | bytes 7471104 | tf_op jit(solution)/shard_map/all_to_all | solution.py:455
  22.6 2.0 %copy-start = (bf16[1024,1792]{1,0:T(8,128)(2,1)S(1)}, bf16[1024,1792]{1,0:T(8,128)(2,1)}, u32[]{:S(2)}) copy-start(bf16[1024,1792]{1,0:T(8,128)(2,1)} %k_ref.2) | copy-start | bytes 11010052
  24.7 2.0 %copy-start.2 = (bf16[1024,1792]{1,0:T(8,128)(2,1)S(1)}, bf16[1024,1792]{1,0:T(8,128)(2,1)}, u32[]{:S(2)}) copy-start(bf16[1024,1792]{1,0:T(8,128)(2,1)} %v_ref.2) | copy-start | bytes 11010052
  26.7 2.0 %copy-start.4 = (bf16[1024,1792]{1,0:T(8,128)(2,1)S(1)}, bf16[1024,1792]{1,0:T(8,128)(2,1)}, u32[]{:S(2)}) copy-start(bf16[1024,1792]{1,0:T(8,128)(2,1)} %q_hbm.1) | copy-start | bytes 11010052
  28.8 17.4 %copy-start.1 = (bf16[1024,1792]{1,0:T(8,128)(2,1)S(1)}, bf16[1024,1792]{1,0:T(8,128)(2,1)}, u32[]{:S(2)}) copy-start(bf16[1024,1792]{1,0:T(8,128)(2,1)} %k_ref.2) | copy-start | bytes 11010052
  28.8 17.4 %copy-start.3 = (bf16[1024,1792]{1,0:T(8,128)(2,1)S(1)}, bf16[1024,1792]{1,0:T(8,128)(2,1)}, u32[]{:S(2)}) copy-start(bf16[1024,1792]{1,0:T(8,128)(2,1)} %v_ref.2) | copy-start | bytes 11010052
  43.4 0.7 copy-start.12
  44.1 10.8 %copy-start.5 = (f32[512,1792]{1,0:T(8,128)}, f32[512,1792]{1,0:T(8,128)S(1)}, u32[]{:S(2)}) copy-start(f32[512,1792]{1,0:T(8,128)S(1)} %get-tuple-element.45.low_ref) | copy-start | bytes 11010052
  44.1 10.8 %copy-start.7 = (bf16[1024,1792]{1,0:T(8,128)(2,1)}, bf16[1024,1792]{1,0:T(8,128)(2,1)S(1)}, u32[]{:S(2)}) copy-start(bf16[1024,1792]{1,0:T(8,128)(2,1)S(1)} %get-tuple-element.48.into_ref) | copy-start | bytes 11010052
  44.1 15.2 %copy-start.17 = (f32[14]{0:T(128)S(1)}, f32[14]{0:T(128)}, u32[]{:S(2)}) copy-start(f32[14]{0:T(128)} %param.15) | copy-start | bytes 172
  44.1 1.0 copy-start.10
  45.1 1.1 copy-start.8
  46.2 2.3 %copy-start.9 = (bf16[512,1280]{1,0:T(8,128)(2,1)S(1)}, bf16[512,1280]{1,0:T(8,128)(2,1)}, u32[]{:S(2)}) copy-start(bf16[512,1280]{1,0:T(8,128)(2,1)} %copy-done.8) | copy-start | bytes 3932164
  48.5 1.2 copy-start.11
  55.0 0.8 copy-start.14
  55.8 26.3 %collective-permute-start.2 = (bf16[512,1408]{1,0:T(8,128)(2,1)S(1)}, bf16[512,1408]{1,0:T(8,128)(2,1)S(1)}, u32[]{:S(2)}, u32[]{:S(2)}) collective-permute-start(bf16[512,1408]{1,0:T(8,128)(2,1)S(1)} %get-tuple-element.43), channel_id=1, source_target_pairs={{0,4},{4,8},{8,12},{12,16},{16,20},{20,24},{24,28},{28,32},{32,36}... | collective-permute-start | bytes 4325384 | tf_op jit(solution)/shard_map/ppermute | solution.py:463
  75.1 7.1 %copy-start.13 = (f32[512,128]{1,0:T(8,128)S(1)}, f32[512,128]{1,0:T(8,128)}, u32[]{:S(2)}) copy-start(f32[512,128]{1,0:T(8,128)} %copy-done.12) | copy-start | bytes 786436
  75.1 53.0 %all-to-all-start.1 = ((bf16[32,56,8,128]{3,2,1,0:T(8,128)(2,1)}), bf16[32,56,8,128]{3,2,1,0:T(8,128)(2,1)}, u32[]{:S(2)}, u32[]{:S(2)}) async-start(bf16[32,56,8,128]{3,2,1,0:T(8,128)(2,1)} %gather_pieces.1), calls=%async_computation.1 | async-start | bytes 7340032 | tf_op jit(solution)/shard_map/all_to_all | solution.py:468
  82.1 2.0 %copy-start.6 = (f32[512,1792]{1,0:T(8,128)S(1)}, f32[512,1792]{1,0:T(8,128)}, u32[]{:S(2)}) copy-start(f32[512,1792]{1,0:T(8,128)} %copy-done.5) | copy-start | bytes 11010052
  84.2 1.1 copy-start.15

commit v11 on v10

--- a/solution.py
+++ b/solution.py
@@ -459,7 +459,7 @@
     low, edge_q, edge_k, edge_v = lax.optimization_barrier(
         (low, queries, token_keys, token_values)
     )
-    far_part, near = edge_attention(far_q, near_kv, edge_q, edge_k, edge_v, heads, scale)
+    far_part, near = edge_attention(in_hbm(far_q), in_hbm(near_kv), edge_q, edge_k, edge_v, heads, scale)
     far = lax.ppermute(far_part, "seq", upward)
     store, low, lse, local, near, _ = lax.optimization_barrier(
         (store, low, lse, local, near, far_part)

time: 138 us -> 136 us (0.986)
  local copies, waits for them, and re-layouts: 16.6 us -> 10.4 us
  waiting for transfers between devices: 49.8 us -> 52.6 us
  Pallas kernels: 44 us -> 46.4 us
    unnamed x36 -> x22, local copies, waits for them, and re-layouts: 16.3 us -> 10.1 us
    pallas_call x1, Pallas kernels: 5.24 us -> 8.65 us  [edge_attention(): pl.pallas_call(functools.partial(edge_kernel, scale, heads), out_shape=(j...]
    all_to_all x1, waiting for transfers between devices: 10.1 us -> 13 us  [body(): store = lax.all_to_all(sent, 'seq', split_axis=0, concat_axis=0, tiled=True)]
  transfers between devices with their start and end apart: 5 -> 5, of which waited for: 2 -> 2; matrix products, arithmetic and copies ran while one was open for 0% -> 0% of each run, Pallas kernels for 24% -> 27%
where the time goes in v11:
time: 136 us
  waiting for transfers between devices  52.6 us (39%)
  Pallas kernels  46.4 us (34%)
  starting transfers between devices  26 us (19%)
  local copies, waits for them, and re-layouts  10.4 us (8%)
    all_to_all x1, waiting for transfers between devices, body(): kv = lax.all_to_all(pieces, 'seq', split_axis=0, concat_axis=0, tiled=True)  39.6 us
    pallas_call x1, Pallas kernels, own_attention(): pl.pallas_call(functools.partial(own_kernel, scale, heads), out_shape=(ja...  14.7 us
    all_to_all x1, waiting for transfers between devices, body(): store = lax.all_to_all(sent, 'seq', split_axis=0, concat_axis=0, tiled=True)  13 us
    unnamed x22, local copies, waits for them, and re-layouts  10.1 us
    all_to_all x1, starting transfers between devices, body(): store = lax.all_to_all(sent, 'seq', split_axis=0, concat_axis=0, tiled=True)  9.07 us
    pallas_call x1, Pallas kernels, final_attention(): pl.pallas_call(functools.partial(final_kernel, scale, heads), out_shape=p...  8.66 us
    pallas_call x1, Pallas kernels, edge_attention(): pl.pallas_call(functools.partial(edge_kernel, scale, heads), out_shape=(j...  8.65 us
    all_to_all x1, starting transfers between devices, body(): kv = lax.all_to_all(pieces, 'seq', split_axis=0, concat_axis=0, tiled=True)  6.89 us
  transfers between devices with their start and end apart: 5, of which 2 were waited for; matrix products, arithmetic and copies ran while one was open for 0% of the time, Pallas kernels for 27%

profile of v11, /device:TPU:1, one launch (start us, length us, event | category | flops | bytes accessed | tf_op | source)
XLA Modules:
  0.0 135.8 jit_solution(3331987680324627124)
XLA Ops:
  0.0 1.3 cut_queries.1
  1.3 0.0 copy-start.9
  1.3 3.3 %collective-permute-start = (bf16[512,1280]{1,0:T(8,128)(2,1)S(1)}, bf16[512,1280]{1,0:T(8,128)(2,1)}, u32[]{:S(2)}, u32[]{:S(2)}) collective-permute-start(bf16[512,1280]{1,0:T(8,128)(2,1)S(1)} %cut_queries.1), channel_id=1, source_target_pairs={{4,0},{8,4},{12,8},{16,12},{20,16},{24,20},{28,24},{32,28},{36,32}... | collective-permute-start | bytes 3932168 | tf_op jit(solution)/shard_map/ppermute | solution.py:448
  4.7 1.2 cut_tails.1
  5.9 3.2 %collective-permute-start.1 = (bf16[512,1024]{1,0:T(8,128)(2,1)S(1)}, bf16[512,1024]{1,0:T(8,128)(2,1)}, u32[]{:S(2)}, u32[]{:S(2)}) collective-permute-start(bf16[512,1024]{1,0:T(8,128)(2,1)S(1)} %cut_tails.1), channel_id=1, source_target_pairs={{0,4},{4,8},{8,12},{12,16},{16,20},{20,24},{24,28},{28,32},{32,36}... | collective-permute-start | bytes 3145736 | tf_op jit(solution)/shard_map/ppermute | solution.py:450
  9.1 0.1 copy.10
  9.2 0.1 convert_element_type.7
  9.4 3.1 %pack_pieces.1 = bf16[32,57,8,128]{3,2,1,0:T(8,128)(2,1)} custom-call(bf16[64,14,8,128]{3,2,1,0:T(8,128)(2,1)} %bitcast.9, bf16[64,14,8,128]{3,2,1,0:T(8,128)(2,1)} %bitcast.10, bf16[32,1,8,128]{3,2,1,0:T(8,128)(2,1)S(1)} %broadcast_in_dim.4.ids_ref), custom_call_target="tpu_custom_call" | custom-call | flops 2000000000 | tf_op jit(solution)/shard_map/pack_pieces/pallas_call | solution.py:107
  12.5 9.1 %all-to-all-start = ((bf16[32,57,8,128]{3,2,1,0:T(8,128)(2,1)}), bf16[32,57,8,128]{3,2,1,0:T(8,128)(2,1)}, u32[]{:S(2)}, u32[]{:S(2)}) async-start(bf16[32,57,8,128]{3,2,1,0:T(8,128)(2,1)} %pack_pieces.1), calls=%async_computation | async-start | bytes 7471104 | tf_op jit(solution)/shard_map/all_to_all | solution.py:455
  21.6 2.0 %copy-done = bf16[1024,1792]{1,0:T(8,128)(2,1)S(1)} copy-done((bf16[1024,1792]{1,0:T(8,128)(2,1)S(1)}, bf16[1024,1792]{1,0:T(8,128)(2,1)}, u32[]{:S(2)}) %copy-start) | copy-done | bytes 3670040
  23.6 2.0 %copy-done.2 = bf16[1024,1792]{1,0:T(8,128)(2,1)S(1)} copy-done((bf16[1024,1792]{1,0:T(8,128)(2,1)S(1)}, bf16[1024,1792]{1,0:T(8,128)(2,1)}, u32[]{:S(2)}) %copy-start.2) | copy-done | bytes 3670040
  25.7 2.0 %copy-done.3 = bf16[1024,1792]{1,0:T(8,128)(2,1)S(1)} copy-done((bf16[1024,1792]{1,0:T(8,128)(2,1)S(1)}, bf16[1024,1792]{1,0:T(8,128)(2,1)}, u32[]{:S(2)}) %copy-start.3) | copy-done | bytes 3670040
  27.7 14.7 %own_attention.1 = (f32[512,1792]{1,0:T(8,128)S(1)}, f32[512,128]{1,0:T(8,128)S(1)}, bf16[1024,1792]{1,0:T(8,128)(2,1)S(1)}) custom-call(bf16[1024,1792]{1,0:T(8,128)(2,1)S(1)} %copy-done.3, bf16[1024,1792]{1,0:T(8,128)(2,1)S(1)} %copy-done, bf16[1024,1792]{1,0:T(8,128)(2,1)S(1)} %copy-done.2), custom_call_target="tpu_custom_call" | custom-call | flops 1000000000 | tf_op jit(solution)/shard_map/own_attention/pallas_call | solution.py:250
  42.4 8.7 %edge_attention.1 = (bf16[512,1408]{1,0:T(8,128)(2,1)S(1)}, bf16[512,640]{1,0:T(8,128)(2,1)S(1)}) custom-call(bf16[512,1280]{1,0:T(8,128)(2,1)} %collective-permute-done.far_q_ref, bf16[512,1024]{1,0:T(8,128)(2,1)} %collective-permute-done.1.near_kv_ref, bf16[1024,1792]{1,0:T(8,128)(2,1)S(1)} %copy-done.3, bf16[1024,1792]{1,0:T(8,128)(2,1)S(1)} %copy-done.1, ...), custom_call_target="tpu_custom_call" | custom-call | flops 60000002048 | tf_op jit(solution)/shard_map/edge_attention/pallas_call | solution.py:309
  51.1 0.9 copy-done.7
  52.0 3.5 %collective-permute-start.2 = (bf16[512,1408]{1,0:T(8,128)(2,1)S(1)}, bf16[512,1408]{1,0:T(8,128)(2,1)S(1)}, u32[]{:S(2)}, u32[]{:S(2)}) collective-permute-start(bf16[512,1408]{1,0:T(8,128)(2,1)S(1)} %get-tuple-element.43), channel_id=1, source_target_pairs={{0,4},{4,8},{8,12},{12,16},{16,20},{20,24},{24,28},{28,32},{32,36}... | collective-permute-start | bytes 4325384 | tf_op jit(solution)/shard_map/ppermute | solution.py:463
  55.5 13.0 %all-to-all-done.store_ref = bf16[32,57,8,128]{3,2,1,0:T(8,128)(2,1)} async-done(((bf16[32,57,8,128]{3,2,1,0:T(8,128)(2,1)}), bf16[32,57,8,128]{3,2,1,0:T(8,128)(2,1)}, u32[]{:S(2)}, u32[]{:S(2)}) %all-to-all-start) | async-done | bytes 3735584 | tf_op jit(solution)/shard_map/all_to_all | solution.py:455
  68.5 5.6 %gather_pieces.1 = bf16[32,56,8,128]{3,2,1,0:T(8,128)(2,1)} custom-call(bf16[32,57,8,128]{3,2,1,0:T(8,128)(2,1)} %all-to-all-done.store_ref), custom_call_target="tpu_custom_call" | custom-call | flops 6000000000 | tf_op jit(solution)/shard_map/gather_pieces/pallas_call | solution.py:171
  74.1 6.9 %all-to-all-start.1 = ((bf16[32,56,8,128]{3,2,1,0:T(8,128)(2,1)}), bf16[32,56,8,128]{3,2,1,0:T(8,128)(2,1)}, u32[]{:S(2)}, u32[]{:S(2)}) async-start(bf16[32,56,8,128]{3,2,1,0:T(8,128)(2,1)} %gather_pieces.1), calls=%async_computation.1 | async-start | bytes 7340032 | tf_op jit(solution)/shard_map/all_to_all | solution.py:468
  81.0 2.0 %copy-done.5 = f32[512,1792]{1,0:T(8,128)S(1)} copy-done((f32[512,1792]{1,0:T(8,128)S(1)}, f32[512,1792]{1,0:T(8,128)}, u32[]{:S(2)}) %copy-start.5) | copy-done | bytes 3670040
  83.1 1.1 copy-done.8
  84.1 3.2 %merge_local.1.local_hbm = bf16[1024,1792]{1,0:T(8,128)(2,1)} custom-call(s32[1]{0:T(128)} %bitcast.5.first_ref, f32[512,1792]{1,0:T(8,128)S(1)} %copy-done.5, f32[512,128]{1,0:T(8,128)S(1)} %get-tuple-element.46.lse_ref, bf16[512,640]{1,0:T(8,128)(2,1)S(1)} %copy-done.8, ...), custom_call_target="tpu_custom_call", output_to_operand_aliasing={{}: (5, {})} | custom-call | flops 60000002048 | tf_op jit(solution)/shard_map/merge_local/pallas_call | solution.py:352
  87.3 39.6 %all-to-all-done.1.kv_hbm = bf16[32,56,8,128]{3,2,1,0:T(8,128)(2,1)} async-done(((bf16[32,56,8,128]{3,2,1,0:T(8,128)(2,1)}), bf16[32,56,8,128]{3,2,1,0:T(8,128)(2,1)}, u32[]{:S(2)}, u32[]{:S(2)}) %all-to-all-start.1) | async-done | bytes 3670048 | tf_op jit(solution)/shard_map/all_to_all | solution.py:468
  127.0 8.7 %final_attention.1 = bf16[1024,1792]{1,0:T(8,128)(2,1)} custom-call(f32[14]{0:T(128)S(1)} %add_divide_fusion.gate_ref, bf16[1024,1792]{1,0:T(8,128)(2,1)} %q_hbm.1, bf16[32,56,8,128]{3,2,1,0:T(8,128)(2,1)} %all-to-all-done.1.kv_hbm, bf16[1024,1792]{1,0:T(8,128)(2,1)} %merge_local.1.local_hbm), custom_call_target="tpu_custom_call" | custom-call | flops 7000000000 | tf_op jit(solution)/shard_map/final_attention/pallas_call | solution.py:416
  (22 shorter events, 0.1 us)
Async XLA Ops:
  1.3 7.8 %copy-start.9 = (s32[2,14,2]{1,2,0:T(2,128)S(1)}, s32[2,14,2]{1,2,0:T(2,128)}, u32[]{:S(2)}) copy-start(s32[2,14,2]{1,2,0:T(2,128)} %param.14) | copy-start | bytes 676
  1.3 41.1 %collective-permute-start = (bf16[512,1280]{1,0:T(8,128)(2,1)S(1)}, bf16[512,1280]{1,0:T(8,128)(2,1)}, u32[]{:S(2)}, u32[]{:S(2)}) collective-permute-start(bf16[512,1280]{1,0:T(8,128)(2,1)S(1)} %cut_queries.1), channel_id=1, source_target_pairs={{4,0},{8,4},{12,8},{16,12},{20,16},{24,20},{28,24},{32,28},{36,32}... | collective-permute-start | bytes 3932168 | tf_op jit(solution)/shard_map/ppermute | solution.py:448
  5.9 36.5 %collective-permute-start.1 = (bf16[512,1024]{1,0:T(8,128)(2,1)S(1)}, bf16[512,1024]{1,0:T(8,128)(2,1)}, u32[]{:S(2)}, u32[]{:S(2)}) collective-permute-start(bf16[512,1024]{1,0:T(8,128)(2,1)S(1)} %cut_tails.1), channel_id=1, source_target_pairs={{0,4},{4,8},{8,12},{12,16},{16,20},{20,24},{24,28},{28,32},{32,36}... | collective-permute-start | bytes 3145736 | tf_op jit(solution)/shard_map/ppermute | solution.py:450
  12.5 56.0 %all-to-all-start = ((bf16[32,57,8,128]{3,2,1,0:T(8,128)(2,1)}), bf16[32,57,8,128]{3,2,1,0:T(8,128)(2,1)}, u32[]{:S(2)}, u32[]{:S(2)}) async-start(bf16[32,57,8,128]{3,2,1,0:T(8,128)(2,1)} %pack_pieces.1), calls=%async_computation | async-start | bytes 7471104 | tf_op jit(solution)/shard_map/all_to_all | solution.py:455
  21.6 2.0 %copy-start = (bf16[1024,1792]{1,0:T(8,128)(2,1)S(1)}, bf16[1024,1792]{1,0:T(8,128)(2,1)}, u32[]{:S(2)}) copy-start(bf16[1024,1792]{1,0:T(8,128)(2,1)} %k_ref.2) | copy-start | bytes 11010052
  23.6 2.0 %copy-start.2 = (bf16[1024,1792]{1,0:T(8,128)(2,1)S(1)}, bf16[1024,1792]{1,0:T(8,128)(2,1)}, u32[]{:S(2)}) copy-start(bf16[1024,1792]{1,0:T(8,128)(2,1)} %v_ref.2) | copy-start | bytes 11010052
  25.7 2.0 %copy-start.3 = (bf16[1024,1792]{1,0:T(8,128)(2,1)S(1)}, bf16[1024,1792]{1,0:T(8,128)(2,1)}, u32[]{:S(2)}) copy-start(bf16[1024,1792]{1,0:T(8,128)(2,1)} %q_hbm.1) | copy-start | bytes 11010052
  27.7 14.7 %copy-start.1 = (bf16[1024,1792]{1,0:T(8,128)(2,1)S(1)}, bf16[1024,1792]{1,0:T(8,128)(2,1)}, u32[]{:S(2)}) copy-start(bf16[1024,1792]{1,0:T(8,128)(2,1)} %k_ref.2) | copy-start | bytes 11010052
  42.4 8.7 %copy-start.4 = (f32[512,1792]{1,0:T(8,128)}, f32[512,1792]{1,0:T(8,128)S(1)}, u32[]{:S(2)}) copy-start(f32[512,1792]{1,0:T(8,128)S(1)} %get-tuple-element.45.low_ref) | copy-start | bytes 11010052
  42.4 8.7 %copy-start.6 = (bf16[1024,1792]{1,0:T(8,128)(2,1)}, bf16[1024,1792]{1,0:T(8,128)(2,1)S(1)}, u32[]{:S(2)}) copy-start(bf16[1024,1792]{1,0:T(8,128)(2,1)S(1)} %get-tuple-element.48.into_ref) | copy-start | bytes 11010052
  42.4 13.1 %copy-start.10 = (f32[14]{0:T(128)S(1)}, f32[14]{0:T(128)}, u32[]{:S(2)}) copy-start(f32[14]{0:T(128)} %param.15) | copy-start | bytes 172
  51.1 0.9 copy-start.7
  52.0 29.0 %collective-permute-start.2 = (bf16[512,1408]{1,0:T(8,128)(2,1)S(1)}, bf16[512,1408]{1,0:T(8,128)(2,1)S(1)}, u32[]{:S(2)}, u32[]{:S(2)}) collective-permute-start(bf16[512,1408]{1,0:T(8,128)(2,1)S(1)} %get-tuple-element.43), channel_id=1, source_target_pairs={{0,4},{4,8},{8,12},{12,16},{16,20},{20,24},{24,28},{28,32},{32,36}... | collective-permute-start | bytes 4325384 | tf_op jit(solution)/shard_map/ppermute | solution.py:463
  74.1 52.9 %all-to-all-start.1 = ((bf16[32,56,8,128]{3,2,1,0:T(8,128)(2,1)}), bf16[32,56,8,128]{3,2,1,0:T(8,128)(2,1)}, u32[]{:S(2)}, u32[]{:S(2)}) async-start(bf16[32,56,8,128]{3,2,1,0:T(8,128)(2,1)} %gather_pieces.1), calls=%async_computation.1 | async-start | bytes 7340032 | tf_op jit(solution)/shard_map/all_to_all | solution.py:468
  81.0 2.0 %copy-start.5 = (f32[512,1792]{1,0:T(8,128)S(1)}, f32[512,1792]{1,0:T(8,128)}, u32[]{:S(2)}) copy-start(f32[512,1792]{1,0:T(8,128)} %copy-done.4) | copy-start | bytes 11010052
  83.0 1.1 copy-start.8
